TPU v7x, 32 devices: a whole 2x2x4 slice. The times are simulated.
32 devices in a mesh: seq: 8 (over y, x, core), wshard: 4 (over z).
Axes of the slice: x: 2, y: 2, z: 4, core: 2. Of those that a mesh axis runs over, the one named last changes fastest.
Arguments:
- block_in: bfloat16 [4, 1024, 2560], P('wshard', 'seq'), may hold values from -6 to 6
- cotangent: bfloat16 [4, 1024, 2560], P('wshard', 'seq'), may hold values from -6 to 6
- w_x: bfloat16 [2560, 2560], P('wshard'), may hold values from -0.125 to 0.125
- w_y: bfloat16 [2560, 2560], P('wshard'), may hold values from -0.125 to 0.125
- w_out: bfloat16 [2560, 2560], P('wshard'), may hold values from -0.125 to 0.125
- w_gate: bfloat16 [7680, 2560], P('wshard'), may hold values from -0.125 to 0.125
- w_up: bfloat16 [7680, 2560], P('wshard'), may hold values from -0.125 to 0.125
- w_down: bfloat16 [7680, 2560], P('wshard'), may hold values from -0.0625 to 0.0625
- norm1_gain: bfloat16 [2560], P('wshard'), may hold values from 0.099609375 to 1.8984375
- norm2_gain: bfloat16 [2560], P('wshard'), may hold values from 0.099609375 to 1.8984375
- conv_weight: bfloat16 [4, 2560], P(None, 'wshard'), may hold values from -3 to 3
- conv_bias: bfloat16 [2560], P('wshard'), may hold values from -3 to 3
- gate_weight: bfloat16 [2, 10, 256, 256], P(None, None, 'wshard'), may hold values from -0.375 to 0.375
- gate_bias: bfloat16 [2, 2560], P(None, 'wshard'), may hold values from -4 to 4
- decay_param: bfloat16 [2560], P('wshard'), may hold values from 5 to 11
Outputs:
- block_out: bfloat16 [4, 1024, 2560], P('wshard', 'seq')
- grad_input: float32 [4, 1024, 2560], P('wshard', 'seq')
- grad_w_x: float32 [2560, 2560], P('wshard', 'seq')
- grad_w_y: float32 [2560, 2560], P('wshard', 'seq')
- grad_w_out: float32 [2560, 2560], P('wshard', 'seq')
- grad_w_gate: float32 [7680, 2560], P('wshard', 'seq')
- grad_w_up: float32 [7680, 2560], P('wshard', 'seq')
- grad_w_down: float32 [7680, 2560], P('wshard', 'seq')
- grad_norm1: float32 [2560], P('wshard')
- grad_norm2: float32 [2560], P('wshard')
- grad_conv_weight: float32 [4, 2560], P(None, 'wshard')
- grad_conv_bias: float32 [2560], P('wshard')
- grad_gate_weight: float32 [2, 10, 256, 256], P(None, None, 'wshard')
- grad_gate_bias: float32 [2, 2560], P(None, 'wshard')
- grad_decay: float32 [2560], P('wshard')
All inputs are finite; a program needn't handle non-finite values.
Results may differ from a plain program's by a relative error of at most 0.019.
Values may be sent and summed in bfloat16 or wider, within the bound.
No kernel may reach another device: no remote copies, remote signals or barrier semaphores. Data moves between devices by JAX's collectives and lax.ppermute only.
A program may use at most 768 MiB of HBM per device.

v0:
```python
import jax
import jax.numpy as jnp
from jax import lax
from jax.sharding import PartitionSpec as P

SCAN_BLOCK = 32


EPS = 1e-06
DECAY_SCALE = 8.0
HIGH = lax.Precision.HIGHEST


def shortened(shard):

    def short(part):
        return part.astype(jnp.bfloat16) if part.dtype == jnp.float32 else part

    return jax.tree.map(short, shard)


def shifted(value, axis, steps):
    count = lax.axis_size(axis)
    leading, last = (max(0, -steps), min(count, count - steps))
    return lax.ppermute(value, axis, [(source, source + steps) for source in range(leading, last)])


def rms_norm(values, gain):
    return values * lax.rsqrt(jnp.mean(values * values, axis=-1, keepdims=True) + EPS) * gain


def gelu_tanh(values):
    return jax.nn.gelu(values, approximate=True)


def mixing(gate, up):
    return gelu_tanh(gate) * up


def scan_terms(log_decay, inputs):
    return (jnp.exp(log_decay), jnp.sqrt(-jnp.expm1(2.0 * log_decay)) * inputs)


def gate_terms(conv, logit_rec, logit_in, decay):
    log_decay = -DECAY_SCALE * jax.nn.softplus(-decay) * jax.nn.sigmoid(logit_rec)
    return (log_decay, conv * jax.nn.sigmoid(logit_in))


def head_forward(inputs, weights):
    rows = inputs.shape[0]
    split = inputs.reshape(rows, weights.shape[0], weights.shape[1])
    return jnp.einsum("shi,hio->sho", split, weights, preferred_element_type=jnp.float32).reshape(
        rows, -1
    )


def head_backward(grads, weights):
    rows = grads.shape[0]
    split = grads.reshape(rows, weights.shape[0], weights.shape[2])
    return jnp.einsum("sho,hio->shi", split, weights, preferred_element_type=jnp.float32).reshape(
        rows, -1
    )


def head_weight_grad(inputs, grads, heads):
    rows = inputs.shape[0]
    left = inputs.reshape(rows, heads, -1)
    right = grads.reshape(rows, heads, -1)
    return jnp.einsum("shi,sho->hio", left, right, preferred_element_type=jnp.float32)


def linear_scan(log_decay, inputs):
    length, width = inputs.shape
    count = length // SCAN_BLOCK
    places = jnp.arange(SCAN_BLOCK)
    mask = places[:, None] >= places[None, :]

    def step(carry, pair):
        decay_block, value_block = pair
        cumul = jnp.cumsum(decay_block, axis=0)
        spread = cumul[:, None, :] - cumul[None, :, :]
        weights = jnp.exp(jnp.where(mask[:, :, None], spread, -1e30))
        result = (
            jnp.einsum("tsw,sw->tw", weights, value_block, precision=HIGH)
            + jnp.exp(cumul) * carry[None, :]
        )
        return (result[-1], result)

    _, outs = lax.scan(
        step,
        jnp.zeros((width,), jnp.float32),
        (log_decay.reshape(count, SCAN_BLOCK, width), inputs.reshape(count, SCAN_BLOCK, width)),
    )
    return outs.reshape(length, width)


def on_device(
    block_in,
    cotangent,
    w_x,
    w_y,
    w_out,
    w_gate,
    w_up,
    w_down,
    norm1_gain,
    norm2_gain,
    conv_weight,
    conv_bias,
    gate_weight,
    gate_bias,
    decay_param,
):
    gathered = (
        lax.all_gather(norm1_gain, "wshard", axis=0, tiled=True),
        lax.all_gather(norm2_gain, "wshard", axis=0, tiled=True),
        lax.all_gather(conv_weight, "wshard", axis=1, tiled=True),
        lax.all_gather(conv_bias, "wshard", axis=0, tiled=True),
        lax.all_gather(gate_weight, "wshard", axis=2, tiled=True),
        lax.all_gather(gate_bias, "wshard", axis=1, tiled=True),
        lax.all_gather(decay_param, "wshard", axis=0, tiled=True),
    )
    gain_one = gathered[0].astype(jnp.float32)
    gain_two = gathered[1].astype(jnp.float32)
    conv_full = gathered[2].astype(jnp.float32)
    conv_shift = gathered[3].astype(jnp.float32)
    gates_full = gathered[4]
    gates_shift = gathered[5].astype(jnp.float32)
    decay_full = gathered[6].astype(jnp.float32)
    heads = gates_full.shape[1]
    inputs = block_in[0].astype(jnp.float32)
    grad_out = cotangent[0]
    tokens = inputs.shape[0]
    model = inputs.shape[1]
    shards = lax.axis_size("wshard")
    width = w_x.shape[0] * shards
    hidden = w_gate.shape[0] * shards
    taps = conv_full.shape[0]
    empty_branch = jnp.zeros((tokens, width), jnp.float32)
    empty_hidden = jnp.zeros((tokens, hidden), jnp.float32)

    def to_channels(parts):
        return lax.all_to_all(parts, "seq", split_axis=1, concat_axis=0, tiled=True)

    def to_tokens(parts):
        return jax.tree.map(
            lambda part, own: part.astype(own.dtype),
            lax.all_to_all(shortened(parts), "seq", split_axis=0, concat_axis=1, tiled=True),
            parts,
        )

    normed_one = rms_norm(inputs, gain_one).astype(jnp.bfloat16)

    def fetch_branch(fn, init):
        return fn(
            init,
            (
                lax.all_gather(w_x, "wshard", axis=0, tiled=True),
                lax.all_gather(w_y, "wshard", axis=0, tiled=True),
            ),
            jnp.int32(0),
        )

    def fetch_out(fn, init):
        return fn(init, lax.all_gather(w_out, "wshard", axis=0, tiled=True), jnp.int32(0))

    def fetch_mlp(fn, init):
        return fn(
            init,
            (
                lax.all_gather(w_gate, "wshard", axis=0, tiled=True),
                lax.all_gather(w_up, "wshard", axis=0, tiled=True),
            ),
            jnp.int32(0),
        )

    def fetch_down(fn, init):
        return fn(init, lax.all_gather(w_down, "wshard", axis=0, tiled=True), jnp.int32(0))

    def weight_term(fn, rows):
        return lax.psum_scatter(
            fn(jnp.int32(0), rows * lax.axis_size("wshard")).astype(jnp.bfloat16),
            "wshard",
            scatter_dimension=0,
            tiled=True,
        ).astype(jnp.float32)

    def branch_forward(carry, pieces, start):
        part_x = jnp.einsum("sd,cd->sc", normed_one, pieces[0], preferred_element_type=jnp.float32)
        part_y = jnp.einsum("sd,cd->sc", normed_one, pieces[1], preferred_element_type=jnp.float32)
        return (part_x, part_y)

    branch_x, branch_y = fetch_branch(branch_forward, (empty_branch, empty_branch))
    conv_in = branch_x.astype(jnp.bfloat16)
    previous = shifted(conv_in[tokens - taps + 1 :], "seq", 1)
    extended = jnp.concatenate([previous, conv_in], axis=0).astype(jnp.float32)
    conv_out = conv_shift + jnp.zeros((tokens, width), jnp.float32)
    for tap in range(taps):
        conv_out = conv_out + conv_full[tap] * extended[taps - 1 - tap : taps - 1 - tap + tokens]
    conv_low = conv_out.astype(jnp.bfloat16)
    logit_rec = head_forward(conv_low, gates_full[0]) + gates_shift[0]
    logit_in = head_forward(conv_low, gates_full[1]) + gates_shift[1]
    log_decay, scan_in = gate_terms(conv_out, logit_rec, logit_in, decay_full)
    scan_in_chan, log_decay_chan = to_channels((scan_in, log_decay))
    state = linear_scan(log_decay_chan, scan_terms(log_decay_chan, scan_in_chan)[1])
    (state_tok,) = to_tokens((state.astype(jnp.bfloat16),))
    state_val = state_tok.astype(jnp.float32)
    gelu_y = gelu_tanh(branch_y)
    mixed = (gelu_y * state_val).astype(jnp.bfloat16)

    def out_forward(total, piece, start):
        return jnp.dot(mixed, piece, preferred_element_type=jnp.float32)

    out_sum = fetch_out(out_forward, jnp.zeros((tokens, model), jnp.float32))
    residual = inputs + out_sum
    normed_two = rms_norm(residual, gain_two).astype(jnp.bfloat16)

    def mlp_forward(carry, pieces, start):
        part_gate = jnp.einsum(
            "sd,fd->sf", normed_two, pieces[0], preferred_element_type=jnp.float32
        )
        part_up = jnp.einsum("sd,fd->sf", normed_two, pieces[1], preferred_element_type=jnp.float32)
        return (part_gate, part_up)

    gate, up = fetch_mlp(mlp_forward, (empty_hidden, empty_hidden))
    activ = mixing(gate, up).astype(jnp.bfloat16)

    def down_forward(total, piece, start):
        return jnp.dot(activ, piece, preferred_element_type=jnp.float32)

    mlp_out = fetch_down(down_forward, jnp.zeros((tokens, model), jnp.float32))

    def down_backward(carry, piece, start):
        part = jnp.einsum("sd,fd->sf", grad_out, piece, preferred_element_type=jnp.float32)
        return part

    grad_activ = fetch_down(down_backward, empty_hidden)
    grad_down = weight_term(
        lambda start, count: jnp.einsum(
            "sf,sd->fd", activ, grad_out, preferred_element_type=jnp.float32
        ),
        w_down.shape[0],
    )
    _, pull_mix = jax.vjp(mixing, gate, up)
    grad_gate_f, grad_up_f = pull_mix(grad_activ)
    grad_gate = grad_gate_f.astype(jnp.bfloat16)
    grad_up = grad_up_f.astype(jnp.bfloat16)

    def mlp_backward(total, pieces, start):
        total = jnp.dot(grad_gate, pieces[0], preferred_element_type=jnp.float32)
        return total + jnp.dot(grad_up, pieces[1], preferred_element_type=jnp.float32)

    grad_normed_two = fetch_mlp(mlp_backward, jnp.zeros((tokens, model), jnp.float32))
    grad_gate_w = weight_term(
        lambda start, count: jnp.einsum(
            "sf,sd->fd", grad_gate, normed_two, preferred_element_type=jnp.float32
        ),
        w_gate.shape[0],
    )
    grad_up_w = weight_term(
        lambda start, count: jnp.einsum(
            "sf,sd->fd", grad_up, normed_two, preferred_element_type=jnp.float32
        ),
        w_up.shape[0],
    )
    block_out = (residual + mlp_out).astype(jnp.bfloat16)
    _, pull_two = jax.vjp(rms_norm, residual, gain_two)
    grad_res_norm, grad_gain_two = pull_two(grad_normed_two)
    grad_residual = grad_out.astype(jnp.float32) + grad_res_norm
    grad_proj = grad_residual.astype(jnp.bfloat16)

    def out_backward(carry, piece, start):
        part = jnp.einsum("sd,cd->sc", grad_proj, piece, preferred_element_type=jnp.float32)
        return part

    grad_mixed = fetch_out(out_backward, empty_branch)
    grad_out_w = weight_term(
        lambda start, count: jnp.einsum(
            "sc,sd->cd", mixed, grad_proj, preferred_element_type=jnp.float32
        ),
        w_out.shape[0],
    )
    _, pull_gelu = jax.vjp(gelu_tanh, branch_y)
    grad_branch_y = pull_gelu(grad_mixed * state_val)[0].astype(jnp.bfloat16)
    grad_state = (grad_mixed * gelu_y).astype(jnp.bfloat16)
    (grad_state_chan,) = to_channels((grad_state.astype(jnp.float32),))
    zero_row = jnp.zeros((1, state.shape[1]), jnp.float32)
    flipped_decay = jnp.concatenate([zero_row, jnp.flip(log_decay_chan, 0)[:-1]], axis=0)
    carried = jnp.flip(linear_scan(flipped_decay, jnp.flip(grad_state_chan, 0)), 0)
    state_before = jnp.concatenate([zero_row, state[:-1]], axis=0)
    _, pull_scan = jax.vjp(scan_terms, log_decay_chan, scan_in_chan)
    grad_log_chan, grad_in_chan = pull_scan((carried * state_before, carried))
    grad_in_tok, grad_log_tok = to_tokens(
        (grad_in_chan.astype(jnp.bfloat16), grad_log_chan.astype(jnp.bfloat16))
    )
    _, pull_gates = jax.vjp(gate_terms, conv_out, logit_rec, logit_in, decay_full)
    grad_conv_scan, grad_rec, grad_inp, grad_decay = pull_gates(
        (grad_log_tok.astype(jnp.float32), grad_in_tok.astype(jnp.float32))
    )
    rec_low = grad_rec.astype(jnp.bfloat16)
    inp_low = grad_inp.astype(jnp.bfloat16)
    grad_conv = (
        grad_conv_scan
        + head_backward(rec_low, gates_full[0])
        + head_backward(inp_low, gates_full[1])
    )
    grad_gates = jnp.stack(
        [head_weight_grad(conv_low, rec_low, heads), head_weight_grad(conv_low, inp_low, heads)]
    )
    grad_gate_shift = jnp.stack(
        [jnp.sum(rec_low.astype(jnp.float32), axis=0), jnp.sum(inp_low.astype(jnp.float32), axis=0)]
    )
    following = shifted(grad_conv[: taps - 1], "seq", -1)
    grad_extended = jnp.concatenate([grad_conv, following], axis=0)
    grad_conv_in = jnp.zeros((tokens, width), jnp.float32)
    tap_grads = []
    for tap in range(taps):
        grad_conv_in = grad_conv_in + conv_full[tap] * grad_extended[tap : tap + tokens]
        tap_grads.append(
            jnp.sum(grad_conv * extended[taps - 1 - tap : taps - 1 - tap + tokens], axis=0)
        )
    grad_conv_w = jnp.stack(tap_grads)
    grad_conv_b = jnp.sum(grad_conv, axis=0)
    grad_x_low = grad_conv_in.astype(jnp.bfloat16)

    def branch_backward(total, pieces, start):
        total = jnp.dot(grad_x_low, pieces[0], preferred_element_type=jnp.float32)
        return total + jnp.dot(grad_branch_y, pieces[1], preferred_element_type=jnp.float32)

    grad_normed_one = fetch_branch(branch_backward, jnp.zeros((tokens, model), jnp.float32))
    grad_x_w = weight_term(
        lambda start, count: jnp.einsum(
            "sc,sd->cd", grad_x_low, normed_one, preferred_element_type=jnp.float32
        ),
        w_x.shape[0],
    )
    grad_y_w = weight_term(
        lambda start, count: jnp.einsum(
            "sc,sd->cd", grad_branch_y, normed_one, preferred_element_type=jnp.float32
        ),
        w_y.shape[0],
    )
    _, pull_one = jax.vjp(rms_norm, inputs, gain_one)
    grad_in_norm, grad_gain_one = pull_one(grad_normed_one)
    grad_input = grad_residual + grad_in_norm
    seq_parts = (
        lax.psum_scatter(
            grad_x_w.astype(jnp.bfloat16), "seq", scatter_dimension=1, tiled=True
        ).astype(jnp.float32),
        lax.psum_scatter(
            grad_y_w.astype(jnp.bfloat16), "seq", scatter_dimension=1, tiled=True
        ).astype(jnp.float32),
        lax.psum_scatter(
            grad_out_w.astype(jnp.bfloat16), "seq", scatter_dimension=1, tiled=True
        ).astype(jnp.float32),
        lax.psum_scatter(
            grad_gate_w.astype(jnp.bfloat16), "seq", scatter_dimension=1, tiled=True
        ).astype(jnp.float32),
        lax.psum_scatter(
            grad_up_w.astype(jnp.bfloat16), "seq", scatter_dimension=1, tiled=True
        ).astype(jnp.float32),
        lax.psum_scatter(
            grad_down.astype(jnp.bfloat16), "seq", scatter_dimension=1, tiled=True
        ).astype(jnp.float32),
    )
    summed = lax.psum(
        (
            grad_gain_one,
            grad_gain_two,
            grad_conv_w,
            grad_conv_b,
            grad_gates,
            grad_gate_shift,
            grad_decay,
        ),
        ("seq", "wshard"),
    )
    position = lax.axis_index("wshard")

    def own_part(values, dim):
        length = values.shape[dim] // shards
        return lax.dynamic_slice_in_dim(values, position * length, length, dim)

    return (
        block_out[None],
        grad_input[None],
        seq_parts[0],
        seq_parts[1],
        seq_parts[2],
        seq_parts[3],
        seq_parts[4],
        seq_parts[5],
        own_part(summed[0], 0),
        own_part(summed[1], 0),
        own_part(summed[2], 1),
        own_part(summed[3], 0),
        own_part(summed[4], 2),
        own_part(summed[5], 1),
        own_part(summed[6], 0),
    )


def solution(mesh):
    return jax.shard_map(
        on_device,
        mesh=mesh,
        in_specs=(
            P("wshard", "seq", None),
            P("wshard", "seq", None),
            P("wshard", None),
            P("wshard", None),
            P("wshard", None),
            P("wshard", None),
            P("wshard", None),
            P("wshard", None),
            P("wshard"),
            P("wshard"),
            P(None, "wshard"),
            P("wshard"),
            P(None, None, "wshard", None),
            P(None, "wshard"),
            P("wshard"),
        ),
        out_specs=(
            P("wshard", "seq", None),
            P("wshard", "seq", None),
            P("wshard", "seq"),
            P("wshard", "seq"),
            P("wshard", "seq"),
            P("wshard", "seq"),
            P("wshard", "seq"),
            P("wshard", "seq"),
            P("wshard"),
            P("wshard"),
            P(None, "wshard"),
            P("wshard"),
            P(None, None, "wshard", None),
            P(None, "wshard"),
            P("wshard"),
        ),
        check_vma=False,
    )
```

profile of v0, /device:TPU:0, one launch (start us, length us, event | category | flops | bytes accessed | tf_op | source)
XLA Modules:
  0.0 6098.9 jit_solution(3443877817069143643)
XLA Ops:
  12.0 14.6 all-gather
  26.7 20.1 all_gather.49
  46.8 18.4 all_gather.52
  65.2 17.7 all-gather.2
  83.4 156.3 %all-gather.14.cloned.1.call-done = bf16[2560,2560]{1,0:T(8,128)(2,1)} async-done(((bf16[640,2560]{1,0:T(8,128)(2,1)}), bf16[2560,2560]{1,0:T(8,128)(2,1)}) %all-gather.14.cloned.1.call-update) | async-done | bytes 13107216 | tf_op jit(solution)/shard_map/all_gather | solution.py:158
  239.7 9.1 convolution_convert_fusion.6
  253.8 40.5 all-gather.16.cloned.1.call-done
  309.4 19.6 all-gather.1
  342.6 15.3 all-to-all-done
  364.8 69.3 %while.26 = (s32[]{:T(128)}, f32[320]{0:T(512)S(1)}, f32[32,32,320]{2,1,0:T(8,128)}, f32[32,32,320]{2,1,0:T(8,128)}, f32[32,32,320]{2,1,0:T(8,128)}, /*index=5*/s32[]{:T(128)}, f32[]{:T(128)}) while((s32[]{:T(128)}, f32[320]{0:T(512)S(1)}, f32[32,32,320]{2,1,0:T(8,128)}, f32[32,32,320]{2,1,0:T(8,128)}, f32[32,32,320]{2,1,0:T(8,128)}, ...), condition=%wide.region_3.4_spmd.clone, body=%wide.region_1.3_spmd.clone.sunk | while | flops 1639426 | bytes 547157 | solution.py:89
  440.4 14.9 all-gather.3
  458.2 63.6 %all-gather.12.cloned.1.call-done = bf16[2560,2560]{1,0:T(8,128)(2,1)} async-done(((bf16[640,2560]{1,0:T(8,128)(2,1)}), bf16[2560,2560]{1,0:T(8,128)(2,1)}) %all-gather.12.cloned.1.call-update) | async-done | bytes 13107216 | tf_op jit(solution)/shard_map/all_gather | solution.py:159
  521.8 10.4 multiply_convert_fusion.5
  532.2 216.0 %all-gather.18.cloned.1.call-done = bf16[2560,2560]{1,0:T(8,128)(2,1)} async-done(((bf16[640,2560]{1,0:T(8,128)(2,1)}), bf16[2560,2560]{1,0:T(8,128)(2,1)}) %all-gather.18.cloned.1.call-update) | async-done | bytes 13107216 | tf_op jit(solution)/shard_map/all_gather | solution.py:165
  756.3 648.7 %all-gather.20.cloned.1.call-done = bf16[7680,2560]{1,0:T(8,128)(2,1)} async-done(((bf16[1920,2560]{1,0:T(8,128)(2,1)}), bf16[7680,2560]{1,0:T(8,128)(2,1)}) %all-gather.20.cloned.1.call-update) | async-done | bytes 39321616 | tf_op jit(solution)/shard_map/all_gather | solution.py:171
  1405.0 24.4 fusion.75
  1429.4 632.6 %all-gather.22.cloned.1.call-done = bf16[7680,2560]{1,0:T(8,128)(2,1)} async-done(((bf16[1920,2560]{1,0:T(8,128)(2,1)}), bf16[7680,2560]{1,0:T(8,128)(2,1)}) %all-gather.22.cloned.1.call-update) | async-done | bytes 39321616 | tf_op jit(solution)/shard_map/all_gather | solution.py:172
  2062.0 24.4 fusion.76
  2086.4 632.8 %all-gather.24.cloned.1.call-done = bf16[7680,2560]{1,0:T(8,128)(2,1)} async-done(((bf16[1920,2560]{1,0:T(8,128)(2,1)}), bf16[7680,2560]{1,0:T(8,128)(2,1)}) %all-gather.24.cloned.1.call-update) | async-done | bytes 39321616 | tf_op jit(solution)/shard_map/all_gather | solution.py:178
  2719.2 21.0 multiply_convert_fusion
  2740.2 15.6 fusion.77
  2755.8 26.6 multiply_reduce_fusion.6
  2793.4 12.6 fusion.31
  2815.0 13.3 reverse.1
  2849.0 13.2 rev.8
  2866.5 69.4 %while.27 = (s32[]{:T(128)}, f32[320]{0:T(512)S(1)}, f32[32,32,320]{2,1,0:T(8,128)}, f32[32,32,320]{2,1,0:T(8,128)}, f32[32,32,320]{2,1,0:T(8,128)}, /*index=5*/s32[]{:T(128)}, f32[]{:T(128)}) while((s32[]{:T(128)}, f32[320]{0:T(512)S(1)}, f32[32,32,320]{2,1,0:T(8,128)}, f32[32,32,320]{2,1,0:T(8,128)}, f32[32,32,320]{2,1,0:T(8,128)}, ...), condition=%wide.region_8.9_spmd.clone, body=%wide.region_6.8_spmd.clone.sunk | while | flops 1639426 | bytes 547157 | solution.py:89
  2938.8 13.2 rev.9
  2962.2 10.2 all-to-all-done.4
  3026.0 17.9 convolution_convert_fusion.2
  3044.4 18.0 convolution_convert_fusion.1
  3063.4 18.1 convolution_convert_fusion
  3114.4 120.3 %reduce-scatter.27.cloned.1.call-done = bf16[640,2560]{1,0:T(8,128)(2,1)} async-done(((bf16[2560,2560]{1,0:T(8,128)(2,1)}), bf16[640,2560]{1,0:T(8,128)(2,1)}) %reduce-scatter.27.cloned.1.call-update) | async-done | bytes 3276816 | tf_op jit(solution)/shard_map/reduce_scatter | solution.py:181
  3240.6 217.7 %reduce-scatter.25.cloned.1.call-done = bf16[640,2560]{1,0:T(8,128)(2,1)} async-done(((bf16[2560,2560]{1,0:T(8,128)(2,1)}), bf16[640,2560]{1,0:T(8,128)(2,1)}) %reduce-scatter.25.cloned.1.call-update) | async-done | bytes 3276816 | tf_op jit(solution)/shard_map/reduce_scatter | solution.py:181
  3464.0 642.1 %reduce-scatter.31.cloned.1.call-done = bf16[1920,2560]{1,0:T(8,128)(2,1)} async-done(((bf16[7680,2560]{1,0:T(8,128)(2,1)}), bf16[1920,2560]{1,0:T(8,128)(2,1)}) %reduce-scatter.31.cloned.1.call-update) | async-done | bytes 9830416 | tf_op jit(solution)/shard_map/reduce_scatter | solution.py:181
  4106.2 14.4 copy.183
  4120.7 633.5 %reduce-scatter.33.cloned.1.call-done = bf16[1920,2560]{1,0:T(8,128)(2,1)} async-done(((bf16[7680,2560]{1,0:T(8,128)(2,1)}), bf16[1920,2560]{1,0:T(8,128)(2,1)}) %reduce-scatter.33.cloned.1.call-update) | async-done | bytes 9830416 | tf_op jit(solution)/shard_map/reduce_scatter | solution.py:181
  4754.1 14.4 copy.185
  4768.6 633.5 %reduce-scatter.35.cloned.1.call-done = bf16[1920,2560]{1,0:T(8,128)(2,1)} async-done(((bf16[7680,2560]{1,0:T(8,128)(2,1)}), bf16[1920,2560]{1,0:T(8,128)(2,1)}) %reduce-scatter.35.cloned.1.call-update) | async-done | bytes 9830416 | tf_op jit(solution)/shard_map/reduce_scatter | solution.py:181
  5402.1 14.4 copy.187
  5417.9 16.6 fusion.12
  5436.0 99.3 %all-reduce.8.cloned.1.call-done = (f32[2560]{0:T(1024)}, f32[2560]{0:T(1024)}, f32[4,2560]{1,0:T(4,128)}, f32[2560]{0:T(1024)}, f32[2,2560]{1,0:T(2,128)}, /*index=5*/f32[2560]{0:T(1024)}) async-done(((f32[2560]{0:T(1024)}, f32[2560]{0:T(1024)}, f32[4,2560]{1,0:T(4,128)}, f32[2560]{0:T(1024)}, f32[2,2560]{1,0:T(2,128)}, /*index=5*/f32[2560]{0:T(1024)}), (f32[2560]{0:T(1024)}, f32[2560]{0:T(1024)}, ...) | async-done | bytes 102416 | tf_op jit(solution)/shard_map/psum | solution.py:366
  5543.3 146.9 %all-reduce.6.cloned.1.call-done = f32[2,10,256,256]{3,2,1,0:T(8,128)} async-done(((f32[2,10,256,256]{3,2,1,0:T(8,128)}), f32[2,10,256,256]{3,2,1,0:T(8,128)}) %all-reduce.6.cloned.1.call-update) | async-done | bytes 5242896 | tf_op jit(solution)/shard_map/psum | solution.py:366
  5692.7 46.6 reduce-scatter.41.cloned.1.call-done
  5741.6 48.2 reduce-scatter.39.cloned.1.call-done
  5792.2 48.2 reduce-scatter.37.cloned.1.call-done
  5842.7 79.9 %reduce-scatter.43.cloned.1.call-done = bf16[320,1920]{1,0:T(8,128)(2,1)} async-done(((bf16[2560,1920]{1,0:T(8,128)(2,1)}), bf16[320,1920]{1,0:T(8,128)(2,1)}) %reduce-scatter.43.cloned.1.call-update) | async-done | bytes 1228816
  5927.4 77.4 %reduce-scatter.45.cloned.1.call-done = bf16[320,1920]{1,0:T(8,128)(2,1)} async-done(((bf16[2560,1920]{1,0:T(8,128)(2,1)}), bf16[320,1920]{1,0:T(8,128)(2,1)}) %reduce-scatter.45.cloned.1.call-update) | async-done | bytes 1228816
  6009.5 77.6 %reduce-scatter.47.cloned.1.call-done = bf16[320,1920]{1,0:T(8,128)(2,1)} async-done(((bf16[2560,1920]{1,0:T(8,128)(2,1)}), bf16[320,1920]{1,0:T(8,128)(2,1)}) %reduce-scatter.47.cloned.1.call-update) | async-done | bytes 1228816
  (679 shorter events, 392.2 us)
Async XLA Ops:
  7.2 232.5 %all-gather.14.cloned.1.call-start = ((), (), s32[]{:S(2)}) async-start(), calls=%async_computation.19 | async-start | bytes 16384000 | tf_op jit(solution)/shard_map/all_gather | solution.py:158
  7.9 286.4 %all-gather.16.cloned.1.call-start = ((), (), s32[]{:S(2)}) async-start(), calls=%async_computation.20 | async-start | bytes 3276800 | tf_op jit(solution)/shard_map/all_gather | solution.py:119
  8.7 513.1 %all-gather.12.cloned.1.call-start = ((), (), s32[]{:S(2)}) async-start(), calls=%async_computation.18 | async-start | bytes 16384000 | tf_op jit(solution)/shard_map/all_gather | solution.py:159
  9.4 738.8 %all-gather.18.cloned.1.call-start = ((), (), s32[]{:S(2)}) async-start(), calls=%async_computation.21 | async-start | bytes 16384000 | tf_op jit(solution)/shard_map/all_gather | solution.py:165
  10.0 1395.1 %all-gather.20.cloned.1.call-start = ((), (), s32[]{:S(2)}) async-start(), calls=%async_computation.22 | async-start | bytes 49152000 | tf_op jit(solution)/shard_map/all_gather | solution.py:171
  10.6 2051.5 %all-gather.22.cloned.1.call-start = ((), (), s32[]{:S(2)}) async-start(), calls=%async_computation.23 | async-start | bytes 49152000 | tf_op jit(solution)/shard_map/all_gather | solution.py:172
  11.1 15.5 copy-start.43
  11.2 35.7 copy-start.46
  11.2 35.7 copy-start.44
  11.2 71.9 %copy-start.2 = (bf16[1,128,2560]{2,1,0:T(8,128)(2,1)S(1)}, bf16[1,128,2560]{2,1,0:T(8,128)(2,1)}, u32[]{:S(2)}) copy-start(bf16[1,128,2560]{2,1,0:T(8,128)(2,1)} %param.19) | copy-start | bytes 1966084
  11.2 2708.0 %all-gather.24.cloned.1.call-start = ((), (), s32[]{:S(2)}) async-start(), calls=%async_computation.24 | async-start | bytes 49152000 | tf_op jit(solution)/shard_map/all_gather | solution.py:178
  83.1 168.7 %copy-start.35 = (f32[2560]{0:T(1024)}, f32[2560]{0:T(1024)S(1)}, u32[]{:S(2)}) copy-start(f32[2560]{0:T(1024)S(1)} %get-tuple-element.180) | copy-start | bytes 30724
  83.1 168.7 %copy-start.37 = (f32[2560]{0:T(1024)}, f32[2560]{0:T(1024)S(1)}, u32[]{:S(2)}) copy-start(f32[2560]{0:T(1024)S(1)} %get-tuple-element.181) | copy-start | bytes 30724
  83.2 168.7 %copy-start.39 = (f32[2560]{0:T(1024)}, f32[2560]{0:T(1024)S(1)}, u32[]{:S(2)}) copy-start(f32[2560]{0:T(1024)S(1)} %get-tuple-element.182) | copy-start | bytes 30724
  83.2 168.7 %copy-start.41 = (f32[2560]{0:T(1024)}, f32[2560]{0:T(1024)S(1)}, u32[]{:S(2)}) copy-start(f32[2560]{0:T(1024)S(1)} %get-tuple-element.183) | copy-start | bytes 30724
  83.4 165.4 %copy-start.49 = (f32[128]{0:T(128)}, f32[128]{0:T(128)S(1)}, u32[]{:S(2)}) copy-start(f32[128]{0:T(128)S(1)} %fusion.41) | copy-start | bytes 1540
  248.8 2.8 collective-permute-start
  253.8 76.0 %copy-start.8 = (bf16[128,2560]{0,1:T(8,128)(2,1)}, bf16[128,2560]{0,1:T(8,128)(2,1)S(1)}, u32[]{:S(2)}) copy-start(bf16[128,2560]{0,1:T(8,128)(2,1)S(1)} %copy.122) | copy-start | bytes 1966084
  304.9 31.1 all-to-all-start.1
  309.4 24.9 copy-start.29
  336.0 21.9 all-to-all-start
  436.8 18.5 all-to-all-start.2
  440.4 2668.3 %reduce-scatter.29.cloned.1.call-start = ((), (), s32[]{:S(2)}) async-start(), calls=%async_computation.27 | async-start | bytes 16384000 | tf_op jit(solution)/shard_map/reduce_scatter | solution.py:181
  458.2 74.0 %copy-start.22 = (f32[128,2560]{1,0:T(8,128)}, f32[128,2560]{1,0:T(8,128)S(1)}, u32[]{:S(2)}) copy-start(f32[128,2560]{1,0:T(8,128)S(1)} %copy.132) | copy-start | bytes 3932164
  755.1 2027.2 %copy-start.3 = (f32[128,2560]{1,0:T(8,128)}, f32[128,2560]{1,0:T(8,128)S(1)}, u32[]{:S(2)}) copy-start(f32[128,2560]{1,0:T(8,128)S(1)} %get-tuple-element.235) | copy-start | bytes 3932164
  2740.2 15.6 copy-start.18
  2808.9 37.6 all-to-all-start.3
  2813.3 421.4 %reduce-scatter.27.cloned.1.call-start = ((), (), s32[]{:S(2)}) async-start(), calls=%async_computation.26 | async-start | bytes 16384000 | tf_op jit(solution)/shard_map/reduce_scatter | solution.py:181
  2957.3 15.2 all-to-all-start.4
  2972.4 15.4 all-to-all-start.5
  2976.6 481.7 %reduce-scatter.25.cloned.1.call-start = ((), (), s32[]{:S(2)}) async-start(), calls=%async_computation.25 | async-start | bytes 16384000 | tf_op jit(solution)/shard_map/reduce_scatter | solution.py:181
  3014.1 3.1 collective-permute-start.1
  3024.9 1081.2 %reduce-scatter.31.cloned.1.call-start = ((), (), s32[]{:S(2)}) async-start(), calls=%async_computation.28 | async-start | bytes 49152000 | tf_op jit(solution)/shard_map/reduce_scatter | solution.py:181
  3043.9 1710.2 %reduce-scatter.33.cloned.1.call-start = ((), (), s32[]{:S(2)}) async-start(), calls=%async_computation.29 | async-start | bytes 49152000 | tf_op jit(solution)/shard_map/reduce_scatter | solution.py:181
  3062.4 2339.8 %reduce-scatter.35.cloned.1.call-start = ((), (), s32[]{:S(2)}) async-start(), calls=%async_computation.30 | async-start | bytes 49152000 | tf_op jit(solution)/shard_map/reduce_scatter | solution.py:181
  3081.6 2453.7 %all-reduce.8.cloned.1.call-start = ((), (), s32[]{:S(2)}) async-start(), calls=%async_computation.38 | async-start | bytes 221184 | tf_op jit(solution)/shard_map/psum | solution.py:366
  3082.8 8.8 copy-start.34
  3086.4 13.9 slice-start
  3089.6 10.7 slice-start.1
  3103.1 2587.1 %all-reduce.6.cloned.1.call-start = ((), (), s32[]{:S(2)}) async-start(), calls=%async_computation.31 | async-start | bytes 10485760 | tf_op jit(solution)/shard_map/psum | solution.py:366
  3108.6 2630.6 %reduce-scatter.41.cloned.1.call-start = ((), (), s32[]{:S(2)}) async-start(), calls=%async_computation.34 | async-start | bytes 3686400
  3114.3 2675.5 %reduce-scatter.39.cloned.1.call-start = ((), (), s32[]{:S(2)}) async-start(), calls=%async_computation.33 | async-start | bytes 3686400
  3240.4 2600.0 %reduce-scatter.37.cloned.1.call-start = ((), (), s32[]{:S(2)}) async-start(), calls=%async_computation.32 | async-start | bytes 3686400
  3464.0 2458.7 %reduce-scatter.43.cloned.1.call-start = ((), (), s32[]{:S(2)}) async-start(), calls=%async_computation.35 | async-start | bytes 11059200
  4120.6 1884.2 %reduce-scatter.45.cloned.1.call-start = ((), (), s32[]{:S(2)}) async-start(), calls=%async_computation.36 | async-start | bytes 11059200
  4768.6 1318.6 %reduce-scatter.47.cloned.1.call-start = ((), (), s32[]{:S(2)}) async-start(), calls=%async_computation.37 | async-start | bytes 11059200
  5417.9 16.6 copy-start.50
  5417.9 16.6 copy-start.12
  (36 other events, 116.7 us)
Sparse Core Ops, SparseCore 0:
  9.6 230.0 all-gather.13
  241.2 53.0 all-gather.15
  295.9 225.8 all-gather.11
  523.2 224.9 all-gather.17
  749.7 655.3 all-gather.19
  1406.5 655.5 all-gather.21
  2063.6 655.5 all-gather.23
  2792.3 218.6 reduce-scatter.28
  3013.3 221.3 reduce-scatter.26
  3236.9 221.3 reduce-scatter.24
  3460.7 645.3 reduce-scatter.30
  4108.5 645.5 reduce-scatter.32
  4756.5 645.5 reduce-scatter.34
  5410.7 124.4 all-reduce.7
  5541.6 148.5 all-reduce.5
  5693.8 45.3 reduce-scatter.40
  5742.9 46.8 reduce-scatter.38
  5793.5 46.8 reduce-scatter.36
  5844.3 78.2 reduce-scatter.42
  5926.5 78.2 reduce-scatter.44
  6008.8 78.2 reduce-scatter.46
where the time goes:
time: 6110 us; the launch traced here: 6100 us
  waiting for transfers between devices  5300 us (87%)
  matrix products  267 us (4%)
  local copies, waits for them, and re-layouts  258 us (4%)
  other arithmetic  126 us (2%)
  blocking collectives  105 us (2%)
    reduce_scatter x6, waiting for transfers between devices, weight_term(): lax.psum_scatter(fn(jnp.int32(0), rows * lax.axis_size('wshard')).astype(...  2250 us
    all_gather x1, waiting for transfers between devices, fetch_mlp(): lax.all_gather(w_gate, 'wshard', axis=0, tiled=True)  649 us
    all_gather x1, waiting for transfers between devices, fetch_down(): lax.all_gather(w_down, 'wshard', axis=0, tiled=True)  633 us
    all_gather x1, waiting for transfers between devices, fetch_mlp(): lax.all_gather(w_up, 'wshard', axis=0, tiled=True)  633 us
    unnamed x27, waiting for transfers between devices  382 us
    psum x2, waiting for transfers between devices, on_device(): lax.psum((grad_gain_one, grad_gain_two, grad_conv_w, grad_conv_b, grad_ga...  246 us
    all_gather x1, waiting for transfers between devices, fetch_out(): lax.all_gather(w_out, 'wshard', axis=0, tiled=True)  216 us
    all_gather x1, waiting for transfers between devices, fetch_branch(): lax.all_gather(w_x, 'wshard', axis=0, tiled=True)  156 us
  transfers between devices with their start and end apart: 29, of which 25 were waited for; matrix products, arithmetic and copies ran while one was open for 9% of the time, Pallas kernels for 0%

commit v1 on v0

v1 whole, which is shorter than its diff:
```python
import functools

import jax
import jax.numpy as jnp
from jax import lax
from jax.experimental import pallas as pl
from jax.experimental.pallas import tpu as pltpu
from jax.sharding import PartitionSpec as P

EPS = 1e-06
DECAY_SCALE = 8.0
HALF = 128
GELU_C = 0.7978845608028654
GELU_K = 0.044715
F32 = jnp.float32
BF16 = jnp.bfloat16


def relay_gather(part, axis="wshard"):
    count = lax.axis_size(axis)
    place = lax.axis_index(axis)
    up = down = part
    ups, downs = [part], [part]
    for k in range(1, count):
        up = lax.ppermute(up, axis, [(i, i + 1) for i in range(k - 1, count - 1)])
        down = lax.ppermute(down, axis, [(i + 1, i) for i in range(count - k)])
        ups.append(up)
        downs.append(down)
    return [part] + [jnp.where(place >= k, ups[k], downs[count - k]) for k in range(1, count)]


def relay_scatter(slots, axis="wshard"):
    count = lax.axis_size(axis)
    up = down = None
    for k in range(1, count):
        out_up = slots[k] if up is None else slots[k] + up.astype(F32)
        out_down = slots[count - k] if down is None else slots[count - k] + down.astype(F32)
        up = lax.ppermute(out_up.astype(BF16), axis, [(i, i + 1) for i in range(k)])
        down = lax.ppermute(
            out_down.astype(BF16), axis, [(i + 1, i) for i in range(count - 1 - k, count - 1)]
        )
    return slots[0] + up.astype(F32) + down.astype(F32)


def exchange_pair(value, axis, bit):
    count = lax.axis_size(axis)
    return lax.ppermute(value, axis, [(i, i ^ bit) for i in range(count)])


def bits_of(count):
    return [1 << i for i in range(count.bit_length() - 1)]


def sum_all(value, axis):
    for bit in bits_of(lax.axis_size(axis)):
        value = value + exchange_pair(value, axis, bit)
    return value


def from_slots(slots, axis="wshard"):
    count = lax.axis_size(axis)
    place = lax.axis_index(axis)
    back = jnp.stack(slots[::-1] + slots[::-1])
    return lax.dynamic_slice_in_dim(back, count - 1 - place, count, 0)


def all_parts(part, axis="wshard"):
    count = lax.axis_size(axis)
    slots = [part] + [
        lax.ppermute(part, axis, [(i, (i + k) % count) for i in range(count)])
        for k in range(1, count)
    ]
    return from_slots(slots, axis)


def swap_parts(parts, axis="wshard"):
    count = lax.axis_size(axis)
    place = lax.axis_index(axis)
    slots = []
    for k in range(count):
        mine = lax.dynamic_index_in_dim(parts, (place + k) % count, 0, keepdims=False)
        if k:
            mine = lax.ppermute(mine, axis, [(i, (i + k) % count) for i in range(count)])
        slots.append(mine)
    return from_slots(slots, axis)


def relative_order(count, order):
    offsets = [0]
    for bit in reversed(order):
        offsets = offsets + [o | bit for o in offsets]
    return offsets


def xor_columns(value, order, axis="seq"):
    count = lax.axis_size(axis)
    place = lax.axis_index(axis)
    width = value.shape[1] // count
    return jnp.concatenate(
        [
            lax.dynamic_slice_in_dim(value, (place ^ offset) * width, width, 1)
            for offset in relative_order(count, order)
        ],
        axis=1,
    )


def halving_grad(left, right, order, axis="seq"):
    rows = left.shape[1]
    size = right.shape[1]
    held = []

    def part(lo, hi):
        total = lax.dot_general(
            left, right[:, lo:hi], (((0,), (0,)), ((), ())), preferred_element_type=F32
        )
        for piece in held:
            total = total + piece[:, lo:hi].astype(F32)
        return total

    for bit in order:
        half = size // 2
        held.append(exchange_pair(part(half, size).astype(BF16), axis, bit))
        size = half
    return part(0, size)


def expm1_neg(v):
    poly = 1.0 + v / 9.0
    for n in range(8, 1, -1):
        poly = 1.0 + poly * v / float(n)
    return jnp.where(v > -0.5, v * poly, jnp.exp(v) - 1.0)


def gelu_parts(v):
    t = jnp.tanh(GELU_C * (v + GELU_K * v * v * v))
    value = 0.5 * v * (1.0 + t)
    slope = 0.5 * (1.0 + t) + 0.5 * v * (1.0 - t * t) * GELU_C * (1.0 + 3.0 * GELU_K * v * v)
    return value, slope


def gelu_value(v):
    return 0.5 * v * (1.0 + jnp.tanh(GELU_C * (v + GELU_K * v * v * v)))


def row_ids(shape):
    return lax.broadcasted_iota(jnp.int32, shape, 0)


def shift_down(v, k, fill, rows):
    count = v.shape[0]
    if k % 8 == 0:
        return jnp.concatenate([jnp.full((k, v.shape[1]), fill, F32), v[: count - k]], axis=0)
    return jnp.where(rows < k, fill, pltpu.roll(v, k, 0))


def shift_up(v, k, fill, rows):
    count = v.shape[0]
    if k % 8 == 0:
        return jnp.concatenate([v[k:], jnp.full((k, v.shape[1]), fill, F32)], axis=0)
    return jnp.where(rows >= count - k, fill, pltpu.roll(v, count - k, 0))


def run_scan(decay, value, shift, rows):
    k = 1
    while k < value.shape[0]:
        value = value + decay * shift(value, k, 0.0, rows)
        decay = decay * shift(decay, k, 1.0, rows)
        k *= 2
    return decay, value


def conv_kernel(bx_ref, halo_ref, vec_ref, conv_ref, low_ref, ext_ref):
    tokens = bx_ref.shape[1]
    ext_ref[0:8] = halo_ref[0]
    ext_ref[8:] = bx_ref[0].astype(F32)
    total = vec_ref[4:5] + jnp.zeros((tokens, bx_ref.shape[2]), F32)
    for k in range(4):
        total = total + vec_ref[k : k + 1] * ext_ref[8 - k : 8 - k + tokens]
    conv_ref[0] = total
    low_ref[0] = total.astype(BF16)


def gates_kernel(off_ref, win_ref, conv_ref, wg_ref, vec_ref, s0_ref, s1_ref, h_ref, a_ref, end_ref):
    tokens = win_ref.shape[1]
    rows = row_ids((tokens, HALF))
    for m in range(wg_ref.shape[0]):
        cols = slice(m * HALF, (m + 1) * HALF)
        src = pl.multiple_of(off_ref[m], HALF)
        logits = jnp.dot(
            win_ref[0, :, pl.ds(src, 2 * HALF)], wg_ref[m], preferred_element_type=F32
        )
        s0 = jax.nn.sigmoid(logits[:, :HALF] + vec_ref[0:1, cols])
        s1 = jax.nn.sigmoid(logits[:, HALF:] + vec_ref[1:2, cols])
        log_a = vec_ref[2:3, cols] * s0
        value = jnp.sqrt(-expm1_neg(2.0 * log_a)) * (conv_ref[0, :, cols] * s1)
        decay, state = run_scan(jnp.exp(log_a), value, shift_down, rows)
        s0_ref[0, :, cols] = s0
        s1_ref[0, :, cols] = s1
        h_ref[0, :, cols] = state
        a_ref[0, :, cols] = decay
        end_ref[0, 0:1, cols] = state[tokens - 1 :]
        end_ref[0, 1:2, cols] = decay[tokens - 1 :]


def back_scan_kernel(gm_ref, by_ref, st_ref, s0_ref, vec_ref, gy_ref, c_ref, a_ref, end_ref):
    tokens = gm_ref.shape[1]
    rows = row_ids((tokens, HALF))
    for m in range(gm_ref.shape[2] // HALF):
        cols = slice(m * HALF, (m + 1) * HALF)
        gm = gm_ref[0, :, cols]
        value, slope = gelu_parts(by_ref[0, :, cols])
        low = st_ref[0, :, cols].astype(BF16).astype(F32)
        gy_ref[0, :, cols] = (gm * low * slope).astype(BF16)
        grad = (gm * value).astype(BF16).astype(F32)
        decay = jnp.exp(vec_ref[2:3, cols] * s0_ref[0, :, cols])
        prod, carried = run_scan(shift_up(decay, 1, 1.0, rows), grad, shift_up, rows)
        c_ref[0, :, cols] = carried
        a_ref[0, :, cols] = prod
        end_ref[0, 0:1, cols] = decay[0:1] * carried[0:1]
        end_ref[0, 1:2, cols] = decay[0:1] * prod[0:1]


def back_gates_kernel(
    off_ref,
    c_ref,
    a_ref,
    edge_ref,
    s0_ref,
    s1_ref,
    conv_ref,
    st_ref,
    win_ref,
    wg_ref,
    vec_ref,
    gc_ref,
    dw_ref,
    sum_ref,
):
    tokens = c_ref.shape[1]
    rows = row_ids((tokens, HALF))

    @pl.when(pl.program_id(0) == 0)
    def _():
        dw_ref[...] = jnp.zeros_like(dw_ref)
        sum_ref[...] = jnp.zeros_like(sum_ref)

    gc_ref[...] = jnp.zeros_like(gc_ref)
    for m in range(wg_ref.shape[0]):
        cols = slice(m * HALF, (m + 1) * HALF)
        src = pl.multiple_of(off_ref[m], HALF)
        own = pl.multiple_of(off_ref[wg_ref.shape[0]] + m * HALF, HALF)
        carried = c_ref[0, :, cols] + a_ref[0, :, cols] * edge_ref[0, 1:2, cols]
        before = shift_down(st_ref[0, :, cols], 1, 0.0, rows)
        before = jnp.where(rows == 0, edge_ref[0, 0:1, cols], before)
        s0 = s0_ref[0, :, cols]
        s1 = s1_ref[0, :, cols]
        conv = conv_ref[0, :, cols]
        coef = vec_ref[2:3, cols]
        log_a = coef * s0
        root = jnp.sqrt(-expm1_neg(2.0 * log_a))
        g_log = carried * (jnp.exp(log_a) * before - jnp.exp(2.0 * log_a) * (conv * s1) / root)
        g_log = g_log.astype(BF16).astype(F32)
        g_in = (carried * root).astype(BF16).astype(F32)
        rec = (g_log * coef * s0 * (1.0 - s0)).astype(BF16)
        inp = (g_in * conv * s1 * (1.0 - s1)).astype(BF16)
        sum_ref[0:1, cols] += jnp.sum(g_log * s0, axis=0, keepdims=True)
        sum_ref[1:2, cols] += jnp.sum(rec.astype(F32), axis=0, keepdims=True)
        sum_ref[2:3, cols] += jnp.sum(inp.astype(F32), axis=0, keepdims=True)
        both = jnp.concatenate([rec, inp], axis=1)
        gc_ref[0, :, pl.ds(src, 2 * HALF)] += lax.dot_general(
            both, wg_ref[m], (((1,), (1,)), ((), ())), preferred_element_type=F32
        )
        gc_ref[0, :, pl.ds(own, HALF)] += g_in * s1
        dw_ref[m] += lax.dot_general(
            win_ref[0, :, pl.ds(src, 2 * HALF)],
            both,
            (((0,), (0,)), ((), ())),
            preferred_element_type=F32,
        )


def back_conv_kernel(gc_ref, after_ref, bx_ref, halo_ref, vec_ref, gx_ref, sum_ref, g_ext, x_ext):
    tokens = gc_ref.shape[1]

    @pl.when(pl.program_id(0) == 0)
    def _():
        sum_ref[...] = jnp.zeros_like(sum_ref)

    grad = gc_ref[0]
    g_ext[0:tokens] = grad
    g_ext[tokens:] = after_ref[0]
    x_ext[0:8] = halo_ref[0]
    x_ext[8:] = bx_ref[0].astype(F32)
    total = jnp.zeros_like(grad)
    for k in range(4):
        total = total + vec_ref[k : k + 1] * g_ext[k : k + tokens]
        sum_ref[k : k + 1] += jnp.sum(
            grad * x_ext[8 - k : 8 - k + tokens], axis=0, keepdims=True
        )
    sum_ref[4:5] += jnp.sum(grad, axis=0, keepdims=True)
    gx_ref[0] = total.astype(BF16)


def slot_spec(rows, width):
    return pl.BlockSpec((1, rows, width), lambda i: (i, 0, 0))


def whole_spec(shape):
    zero = (0,) * len(shape)
    return pl.BlockSpec(shape, lambda i: zero)


def call(kernel, slots, ins, in_specs, outs, out_specs, scratch=()):
    return pl.pallas_call(
        kernel,
        grid=(slots,),
        in_specs=in_specs,
        out_specs=out_specs,
        out_shape=outs,
        scratch_shapes=list(scratch),
    )(*ins)


def rms_scale(values):
    return lax.rsqrt(jnp.mean(values * values, axis=-1, keepdims=True) + EPS)


def dot_nt(a, b):
    return lax.dot_general(a, b, (((1,), (1,)), ((), ())), preferred_element_type=F32)


def dot_nn(a, b):
    return jnp.dot(a, b, preferred_element_type=F32)


def on_device(
    block_in,
    cotangent,
    w_x,
    w_y,
    w_out,
    w_gate,
    w_up,
    w_down,
    norm1_gain,
    norm2_gain,
    conv_weight,
    conv_bias,
    gate_weight,
    gate_bias,
    decay_param,
):
    slots = lax.axis_size("wshard")
    place = lax.axis_index("wshard")
    count = lax.axis_size("seq")
    spot = lax.axis_index("seq")
    x_own = block_in[0]
    g_own = cotangent[0]
    tokens, model = x_own.shape
    chans = w_x.shape[0]
    heads, inner = gate_weight.shape[1], gate_weight.shape[3]
    taps = conv_weight.shape[0]
    blocks = chans // HALF
    offset = (chans * place) % inner
    window = -(-(chans + (chans % inner)) // inner) * inner
    odd = offset != 0
    bits = bits_of(count)
    order_a = bits
    order_b = bits[:1] + bits[1:][::-1]
    slot_rows = slots * tokens

    def by_slot(v):
        return v.reshape(slots, tokens, v.shape[-1])

    def flat(v):
        return v.reshape(slot_rows, v.shape[-1])

    def split(v):
        return [v[k * tokens : (k + 1) * tokens] for k in range(slots)]

    gains = all_parts(jnp.stack([norm1_gain, norm2_gain]))
    gains = jnp.swapaxes(gains, 0, 1).reshape(2, model).astype(F32)
    gain_one, gain_two = gains[0:1], gains[1:2]
    conv_vec = jnp.concatenate(
        [conv_weight.astype(F32), conv_bias.astype(F32)[None], jnp.zeros((3, chans), F32)], axis=0
    )
    decay = decay_param.astype(F32)
    coef = -DECAY_SCALE * jax.nn.softplus(-decay)
    gate_vec = jnp.concatenate(
        [gate_bias.astype(F32), coef[None], jnp.zeros((5, chans), F32)], axis=0
    )
    offs = jnp.concatenate(
        [
            (offset + HALF * jnp.arange(blocks, dtype=jnp.int32)) // inner * inner,
            offset[None].astype(jnp.int32),
        ]
    ).astype(jnp.int32)

    x_all = jnp.concatenate(relay_gather(x_own), axis=0)
    g_all = jnp.concatenate(relay_gather(g_own), axis=0)
    x_f = x_all.astype(F32)
    x_hat = x_f * rms_scale(x_f)
    normed_one = (x_hat * gain_one).astype(BF16)

    gate_cols = jnp.transpose(gate_weight, (0, 2, 1, 3)).reshape(2, -1, slots, chans)
    gate_cols = swap_parts(jnp.moveaxis(gate_cols, 2, 0))
    gate_cols = jnp.moveaxis(gate_cols, 0, 1).reshape(2, inner, blocks, HALF)
    wg = jnp.transpose(gate_cols, (2, 1, 0, 3)).reshape(blocks, inner, 2 * HALF)

    branch_x = by_slot(dot_nt(normed_one, w_x).astype(BF16))
    halo = lax.ppermute(
        branch_x[:, tokens - 8 :], "seq", [(i, i + 1) for i in range(count - 1)]
    ).astype(F32)
    branch_y = by_slot(dot_nt(normed_one, w_y))
    conv, conv_low = call(
        conv_kernel,
        slots,
        (branch_x, halo, conv_vec),
        [slot_spec(tokens, chans), slot_spec(8, chans), whole_spec((8, chans))],
        (
            jax.ShapeDtypeStruct((slots, tokens, chans), F32),
            jax.ShapeDtypeStruct((slots, tokens, chans), BF16),
        ),
        (slot_spec(tokens, chans), slot_spec(tokens, chans)),
        [pltpu.VMEM((tokens + 8, chans), F32)],
    )
    extra = window - chans

    def partner(first, last):
        moved = jnp.where(odd, jnp.roll(first, -1, axis=0), jnp.roll(last, 1, axis=0))
        return exchange_pair(moved, "wshard", 1)

    lent = partner(conv_low[:, :, :extra], conv_low[:, :, chans - extra :])
    win = jnp.where(
        odd,
        jnp.concatenate([lent, conv_low], axis=2),
        jnp.concatenate([conv_low, lent], axis=2),
    )
    smem = pl.BlockSpec(memory_space=pltpu.SMEM)
    wide = jax.ShapeDtypeStruct((slots, tokens, chans), F32)
    edge = jax.ShapeDtypeStruct((slots, 8, chans), F32)
    s_rec, s_in, h_local, a_prod, ends = call(
        gates_kernel,
        slots,
        (offs, win, conv, wg, gate_vec),
        [
            smem,
            slot_spec(tokens, window),
            slot_spec(tokens, chans),
            whole_spec(wg.shape),
            whole_spec((8, chans)),
        ],
        (wide, wide, wide, wide, edge),
        (slot_spec(tokens, chans),) * 4 + (slot_spec(8, chans),),
    )
    ends = lax.all_gather(ends[:, :2], "seq", axis=0)
    carry = jnp.zeros((slots, chans), F32)
    for r in range(count - 1):
        carry = jnp.where(r < spot, ends[r, :, 0] + ends[r, :, 1] * carry, carry)
    state = h_local + a_prod * carry[:, None, :]
    gelu_y = gelu_value(branch_y)
    mixed = flat((gelu_y * state.astype(BF16).astype(F32)).astype(BF16))

    residual = x_own.astype(F32) + relay_scatter(split(dot_nn(mixed, w_out)))
    res_scale = rms_scale(residual)
    res_hat = residual * res_scale
    normed_two = jnp.concatenate(relay_gather((res_hat * gain_two).astype(BF16)), axis=0)

    gate = dot_nt(normed_two, w_gate)
    up = dot_nt(normed_two, w_up)
    grad_activ = dot_nt(g_all, w_down)
    gelu_g, slope_g = gelu_parts(gate)
    activ = (gelu_g * up).astype(BF16)
    grad_gate = (grad_activ * up * slope_g).astype(BF16)
    grad_up = (grad_activ * gelu_g).astype(BF16)
    grad_two = relay_scatter(split(dot_nn(grad_gate, w_gate) + dot_nn(grad_up, w_up)))
    block_out = (residual + relay_scatter(split(dot_nn(activ, w_down)))).astype(BF16)

    scaled = grad_two * gain_two
    grad_residual = g_own.astype(F32) + res_scale * (
        scaled - res_hat * jnp.mean(scaled * res_hat, axis=-1, keepdims=True)
    )
    grad_norm2 = jnp.sum(grad_two * res_hat, axis=0)
    grad_proj = jnp.concatenate(relay_gather(grad_residual.astype(BF16)), axis=0)

    g_cols = xor_columns(g_all, order_a)
    two_a = xor_columns(normed_two, order_a)
    two_b = xor_columns(normed_two, order_b)
    grad_w_down = halving_grad(activ, g_cols, order_a)
    grad_w_gate = halving_grad(grad_gate, two_b, order_b)
    grad_w_up = halving_grad(grad_up, two_a, order_a)

    grad_mixed = by_slot(dot_nt(grad_proj, w_out))
    grad_y, c_local, c_prod, back_ends = call(
        back_scan_kernel,
        slots,
        (grad_mixed, branch_y, state, s_rec, gate_vec),
        [slot_spec(tokens, chans)] * 4 + [whole_spec((8, chans))],
        (jax.ShapeDtypeStruct((slots, tokens, chans), BF16), wide, wide, edge),
        (slot_spec(tokens, chans),) * 3 + (slot_spec(8, chans),),
    )
    back_ends = lax.all_gather(back_ends[:, :2], "seq", axis=0)
    back = jnp.zeros((slots, chans), F32)
    for r in range(count - 1, 0, -1):
        back = jnp.where(r > spot, back_ends[r, :, 0] + back_ends[r, :, 1] * back, back)
    edges = jnp.concatenate(
        [carry[:, None], back[:, None], jnp.zeros((slots, 6, chans), F32)], axis=1
    )
    grad_win, grad_wg, gate_sums = call(
        back_gates_kernel,
        slots,
        (offs, c_local, c_prod, edges, s_rec, s_in, conv, state, win, wg, gate_vec),
        [smem]
        + [slot_spec(tokens, chans)] * 2
        + [slot_spec(8, chans)]
        + [slot_spec(tokens, chans)] * 4
        + [slot_spec(tokens, window), whole_spec(wg.shape), whole_spec((8, chans))],
        (
            jax.ShapeDtypeStruct((slots, tokens, window), F32),
            jax.ShapeDtypeStruct(wg.shape, F32),
            jax.ShapeDtypeStruct((8, chans), F32),
        ),
        (slot_spec(tokens, window), whole_spec(wg.shape), whole_spec((8, chans))),
    )
    near = jnp.where(odd, grad_win[:, :, extra:], grad_win[:, :, :chans])
    got = partner(grad_win[:, :, :extra], grad_win[:, :, chans:])
    blank = jnp.zeros((slots, tokens, chans - extra), F32)
    grad_conv = near + jnp.where(
        odd, jnp.concatenate([got, blank], axis=2), jnp.concatenate([blank, got], axis=2)
    )
    after = lax.ppermute(grad_conv[:, :8], "seq", [(i + 1, i) for i in range(count - 1)])
    grad_x_low, conv_sums = call(
        back_conv_kernel,
        slots,
        (grad_conv, after, branch_x, halo, conv_vec),
        [
            slot_spec(tokens, chans),
            slot_spec(8, chans),
            slot_spec(tokens, chans),
            slot_spec(8, chans),
            whole_spec((8, chans)),
        ],
        (
            jax.ShapeDtypeStruct((slots, tokens, chans), BF16),
            jax.ShapeDtypeStruct((8, chans), F32),
        ),
        (slot_spec(tokens, chans), whole_spec((8, chans))),
        [pltpu.VMEM((tokens + 8, chans), F32), pltpu.VMEM((tokens + 8, chans), F32)],
    )
    grad_x_low = flat(grad_x_low)
    grad_y = flat(grad_y)
    one_part = dot_nn(grad_x_low, w_x) + dot_nn(grad_y, w_y)
    grad_norm1 = jnp.sum(one_part * x_hat, axis=0)
    grad_one = relay_scatter(split(one_part))
    own_f = x_own.astype(F32)
    own_scale = rms_scale(own_f)
    own_hat = own_f * own_scale
    scaled_one = grad_one * gain_one
    grad_input = grad_residual + own_scale * (
        scaled_one - own_hat * jnp.mean(scaled_one * own_hat, axis=-1, keepdims=True)
    )

    proj_cols = xor_columns(grad_proj, order_b)
    one_a = xor_columns(normed_one, order_a)
    one_b = xor_columns(normed_one, order_b)
    grad_w_out = halving_grad(mixed, proj_cols, order_b)
    grad_w_x = halving_grad(grad_x_low, one_a, order_a)
    grad_w_y = halving_grad(grad_y, one_b, order_b)

    norms = sum_all(jnp.stack([grad_norm1, grad_norm2]), "wshard")
    norms = lax.dynamic_slice_in_dim(norms, place * chans, chans, 1)
    smalls = sum_all(jnp.concatenate([norms, gate_sums[:3], conv_sums[:5]], axis=0), "seq")
    gate_parts = grad_wg.reshape(blocks, inner, 2, HALF)
    gate_parts = jnp.transpose(gate_parts, (1, 2, 0, 3)).reshape(slots, -1, 2, chans)
    gate_parts = sum_all(swap_parts(gate_parts), "seq")
    gate_parts = jnp.transpose(gate_parts, (2, 1, 0, 3)).reshape(2, -1, heads, inner)
    grad_gates = jnp.transpose(gate_parts, (0, 2, 1, 3))

    return (
        block_out[None],
        grad_input[None],
        grad_w_x,
        grad_w_y,
        grad_w_out,
        grad_w_gate,
        grad_w_up,
        grad_w_down,
        smalls[0],
        smalls[1],
        smalls[5:9],
        smalls[9],
        grad_gates,
        smalls[3:5],
        DECAY_SCALE * jax.nn.sigmoid(-decay) * smalls[2],
    )


def solution(mesh):
    row = P("wshard", None)
    vec = P("wshard")
    tok = P("wshard", "seq", None)
    grad = P("wshard", "seq")
    return jax.shard_map(
        on_device,
        mesh=mesh,
        in_specs=(
            tok,
            tok,
            row,
            row,
            row,
            row,
            row,
            row,
            vec,
            vec,
            P(None, "wshard"),
            vec,
            P(None, None, "wshard", None),
            P(None, "wshard"),
            vec,
        ),
        out_specs=(
            tok,
            tok,
            grad,
            grad,
            grad,
            grad,
            grad,
            grad,
            vec,
            vec,
            P(None, "wshard"),
            vec,
            P(None, None, "wshard", None),
            P(None, "wshard"),
            vec,
        ),
        check_vma=False,
    )
```

time: 6110 us -> 939 us (0.15)
  waiting for transfers between devices: 5300 us -> 421 us
  local copies, waits for them, and re-layouts: 258 us -> 108 us
  starting transfers between devices: 29 us -> 151 us
  matrix products: 267 us -> 155 us
  blocking collectives: 105 us -> 18.6 us
  other arithmetic: 126 us -> 41.4 us
    all_gather x7 -> x0, waiting for transfers between devices: 2390 us -> none  [the longest x1 649 us: fetch_mlp(): lax.all_gather(w_gate, 'wshard', axis=0, tiled=True)]
    reduce_scatter x6 -> x0, waiting for transfers between devices: 2250 us -> none  [weight_term(): lax.psum_scatter(fn(jnp.int32(0), rows * lax.axis_size('wshard')).astype(...]
    ppermute x2 -> x87, waiting for transfers between devices: 2.58 us -> 421 us  [the longest x28 197 us: exchange_pair(): return lax.ppermute(value, axis, [(i, i ^ bit) for i in range(count)])]
    unnamed x27 -> x0, waiting for transfers between devices: 382 us -> none
    psum x2 -> x0, waiting for transfers between devices: 246 us -> none  [on_device(): lax.psum((grad_gain_one, grad_gain_two, grad_conv_w, grad_conv_b, grad_ga...]
    ppermute x2 -> x87, starting transfers between devices: 3.25 us -> 151 us  [the longest x12 42.4 us: relay_scatter(): up = lax.ppermute(out_up.astype(BF16), axis, [(i, i + 1) for i in range(k)])]
    dot_general x24 -> x36, matrix products: 267 us -> 155 us  [the longest x24 75.5 us: part(): lax.dot_general(left, right[:, lo:hi], (((0,), (0,)), ((), ())), preferre...]
    unnamed x136 -> x227, local copies, waits for them, and re-layouts: 112 us -> 24 us
  transfers between devices with their start and end apart: 29 -> 87, of which waited for: 25 -> 35; matrix products, arithmetic and copies ran while one was open for 9% -> 24% of each run, Pallas kernels for 0% -> 3%
where the time goes in v1:
time: 939 us; the launch traced here: 929 us
  waiting for transfers between devices  421 us (45%)
  matrix products  155 us (17%)
  starting transfers between devices  151 us (16%)
  local copies, waits for them, and re-layouts  108 us (12%)
  other arithmetic  41.4 us (4%)
  Pallas kernels  30.6 us (3%)
  blocking collectives  18.6 us (2%)
    ppermute x28, waiting for transfers between devices, exchange_pair(): return lax.ppermute(value, axis, [(i, i ^ bit) for i in range(count)])  197 us
    ppermute x12, waiting for transfers between devices, relay_scatter(): up = lax.ppermute(out_up.astype(BF16), axis, [(i, i + 1) for i in range(k)])  93.3 us
    ppermute x12, waiting for transfers between devices, relay_gather(): down = lax.ppermute(down, axis, [(i + 1, i) for i in range(count - k)])  81.5 us
    dot_general x24, matrix products, part(): lax.dot_general(left, right[:, lo:hi], (((0,), (0,)), ((), ())), preferre...  75.5 us
    dot_general x6, matrix products, dot_nt(): lax.dot_general(a, b, (((1,), (1,)), ((), ())), preferred_element_type=F32)  44.6 us
    ppermute x12, starting transfers between devices, relay_scatter(): up = lax.ppermute(out_up.astype(BF16), axis, [(i, i + 1) for i in range(k)])  42.4 us
    ppermute x12, starting transfers between devices, relay_gather(): up = lax.ppermute(up, axis, [(i, i + 1) for i in range(k - 1, count - 1)])  39.2 us
    dot_general x6, matrix products, dot_nn(): return jnp.dot(a, b, preferred_element_type=F32)  34.9 us
  transfers between devices with their start and end apart: 87, of which 35 were waited for; matrix products, arithmetic and copies ran while one was open for 24% of the time, Pallas kernels for 3%

profile of v1, /device:TPU:0, one launch (start us, length us, event | category | flops | bytes accessed | tf_op | source)
XLA Modules:
  0.0 929.3 jit_solution(15080108388024549447)
XLA Ops:
  2.4 5.1 collective-permute-start.6
  9.8 5.9 collective-permute-start
  34.1 5.4 collective-permute-start.32
  40.2 16.2 %collective-permute-done.11 = bf16[2,64,640]{2,1,0:T(8,128)(2,1)S(1)} collective-permute-done((bf16[2,64,640]{2,1,0:T(8,128)(2,1)}, bf16[2,64,640]{2,1,0:T(8,128)(2,1)S(1)}, u32[]{:S(2)}, u32[]{:S(2)}) %collective-permute-start.11) | collective-permute-done | bytes 163872 | tf_op jit(solution)/shard_map/ppermute | solution.py:83
  56.4 8.2 collective-permute-done.12
  66.1 6.3 collective-permute-done.13
  93.6 24.1 %collective-permute-done.3 = bf16[128,2560]{1,0:T(8,128)(2,1)S(1)} collective-permute-done((bf16[128,2560]{1,0:T(8,128)(2,1)}, bf16[128,2560]{1,0:T(8,128)(2,1)S(1)}, u32[]{:S(2)}, u32[]{:S(2)}) %collective-permute-start.3) | collective-permute-done | bytes 655392 | tf_op jit(solution)/shard_map/ppermute | solution.py:26
  142.2 6.0 fusion.158
  153.3 7.4 shard_map.263
  161.6 10.6 %all-gather = f32[32,2,640]{2,1,0:T(2,128)S(1)} all-gather(f32[4,2,640]{2,1,0:T(2,128)S(1)} %slice.346), channel_id=2, replica_groups=mesh['seq'=8,'wshard'=4] {'seq'}, dimensions={0}, use_global_device_ids=true | all-gather | bytes 184320 | tf_op jit(solution)/shard_map/all_gather | solution.py:457
  182.8 12.4 %collective-permute-done.14 = bf16[128,2560]{1,0:T(8,128)(2,1)S(1)} collective-permute-done((bf16[128,2560]{1,0:T(8,128)(2,1)S(1)}, bf16[128,2560]{1,0:T(8,128)(2,1)S(1)}, u32[]{:S(2)}, u32[]{:S(2)}) %collective-permute-start.14) | collective-permute-done | bytes 655392 | tf_op jit(solution)/shard_map/ppermute | solution.py:38
  203.5 10.2 %collective-permute-done.15 = bf16[128,2560]{1,0:T(8,128)(2,1)S(1)} collective-permute-done((bf16[128,2560]{1,0:T(8,128)(2,1)S(1)}, bf16[128,2560]{1,0:T(8,128)(2,1)S(1)}, u32[]{:S(2)}, u32[]{:S(2)}) %collective-permute-start.15) | collective-permute-done | bytes 655392 | tf_op jit(solution)/shard_map/ppermute | solution.py:38
  244.1 10.2 %collective-permute-done.16 = bf16[128,2560]{1,0:T(8,128)(2,1)S(1)} collective-permute-done((bf16[128,2560]{1,0:T(8,128)(2,1)}, bf16[128,2560]{1,0:T(8,128)(2,1)S(1)}, u32[]{:S(2)}, u32[]{:S(2)}) %collective-permute-start.16) | collective-permute-done | bytes 655392 | tf_op jit(solution)/shard_map/ppermute | solution.py:38
  254.3 6.1 collective-permute-done.19
  268.4 10.2 %collective-permute-done.21 = bf16[128,2560]{1,0:T(8,128)(2,1)S(1)} collective-permute-done((bf16[128,2560]{1,0:T(8,128)(2,1)S(1)}, bf16[128,2560]{1,0:T(8,128)(2,1)S(1)}, u32[]{:S(2)}, u32[]{:S(2)}) %collective-permute-start.21) | collective-permute-done | bytes 655392 | tf_op jit(solution)/shard_map/ppermute | solution.py:26
  281.2 12.7 %collective-permute-done.22 = bf16[128,2560]{1,0:T(8,128)(2,1)S(1)} collective-permute-done((bf16[128,2560]{1,0:T(8,128)(2,1)S(1)}, bf16[128,2560]{1,0:T(8,128)(2,1)S(1)}, u32[]{:S(2)}, u32[]{:S(2)}) %collective-permute-start.22) | collective-permute-done | bytes 655392 | tf_op jit(solution)/shard_map/ppermute | solution.py:26
  296.0 12.2 %collective-permute-done.23 = bf16[128,2560]{1,0:T(8,128)(2,1)S(1)} collective-permute-done((bf16[128,2560]{1,0:T(8,128)(2,1)S(1)}, bf16[128,2560]{1,0:T(8,128)(2,1)S(1)}, u32[]{:S(2)}, u32[]{:S(2)}) %collective-permute-start.23) | collective-permute-done | bytes 655392 | tf_op jit(solution)/shard_map/ppermute | solution.py:26
  308.4 10.1 %fusion.146 = f32[512,1920]{1,0:T(8,128)} fusion(bf16[1920,2560]{1,0:T(8,128)(2,1)} %param.21, bf16[128,2560]{1,0:T(8,128)(2,1)S(1)} %broadcast_select_fusion.2, bf16[128,2560]{1,0:T(8,128)(2,1)S(1)} %broadcast_select_fusion.6, bf16[128,2560]{1,0:T(8,128)(2,1)S(1)} %broadcast_select_fusion.10, bf16[128,2560]{1,0:T(8,128)(2,1)S(1)} %multiply_convert_fusion.2), kind=kOutput, calls=%fused_computation.371 | convolution fusion | flops 5043650560 | bytes 16384000 | tf_op jit(solution)/shard_map/dot_general | solution.py:330
  318.6 7.5 fusion.147
  326.1 15.4 %multiply_convert_fusion = (bf16[512,1920]{1,0:T(8,128)(2,1)}, bf16[512,1920]{1,0:T(8,128)(2,1)}, bf16[512,1920]{1,0:T(8,128)(2,1)}) fusion(f32[512,1920]{1,0:T(8,128)} %fusion.147, f32[512,1920]{1,0:T(8,128)} %fusion.146, bf16[1920,2560]{1,0:T(8,128)(2,1)} %param.22, bf16[128,2560]{1,0:T(8,128)(2,1)} %copy-done.31, ...), kind=kOutput, calls=%fused_computation.24 | convolution fusion | flops 5068226560 | bytes 26214400 | tf_op jit(solution)/shard_map/dot_general | solution.py:330
  341.6 9.0 fusion.160
  350.6 8.8 fusion.161
  359.4 5.6 convolution_add_fusion.1
  369.6 12.2 %collective-permute-done.38 = bf16[128,2560]{1,0:T(8,128)(2,1)S(1)} collective-permute-done((bf16[128,2560]{1,0:T(8,128)(2,1)S(1)}, bf16[128,2560]{1,0:T(8,128)(2,1)S(1)}, u32[]{:S(2)}, u32[]{:S(2)}) %collective-permute-start.38) | collective-permute-done | bytes 655392 | tf_op jit(solution)/shard_map/ppermute | solution.py:38
  386.4 9.4 %collective-permute-done.26 = bf16[128,2560]{1,0:T(8,128)(2,1)S(1)} collective-permute-done((bf16[128,2560]{1,0:T(8,128)(2,1)S(1)}, bf16[128,2560]{1,0:T(8,128)(2,1)S(1)}, u32[]{:S(2)}, u32[]{:S(2)}) %collective-permute-start.26) | collective-permute-done | bytes 655392 | tf_op jit(solution)/shard_map/ppermute | solution.py:38
  400.4 9.5 %collective-permute-done.39 = bf16[128,2560]{1,0:T(8,128)(2,1)S(1)} collective-permute-done((bf16[128,2560]{1,0:T(8,128)(2,1)S(1)}, bf16[128,2560]{1,0:T(8,128)(2,1)S(1)}, u32[]{:S(2)}, u32[]{:S(2)}) %collective-permute-start.39) | collective-permute-done | bytes 655392 | tf_op jit(solution)/shard_map/ppermute | solution.py:38
  410.9 7.0 collective-permute-done.27
  418.9 5.0 collective-permute-start.28
  431.9 14.2 %collective-permute-done.40 = bf16[128,2560]{1,0:T(8,128)(2,1)S(1)} collective-permute-done((bf16[128,2560]{1,0:T(8,128)(2,1)S(1)}, bf16[128,2560]{1,0:T(8,128)(2,1)S(1)}, u32[]{:S(2)}, u32[]{:S(2)}) %collective-permute-start.40) | collective-permute-done | bytes 655392 | tf_op jit(solution)/shard_map/ppermute | solution.py:38
  447.5 8.4 collective-permute-done.31
  459.3 14.8 %collective-permute-start.44 = (bf16[128,2560]{1,0:T(8,128)(2,1)}, bf16[128,2560]{1,0:T(8,128)(2,1)}, u32[]{:S(2)}, u32[]{:S(2)}) collective-permute-start(bf16[128,2560]{1,0:T(8,128)(2,1)} %get-tuple-element.85), channel_id=1, source_target_pairs={{0,1},{1,2},{2,3},{4,5},{5,6},{6,7},{8,9},{9,10},{10,11},{12,13},{... | collective-permute-start | bytes 1966088 | tf_op jit(solution)/shard_map/ppermute | solution.py:25
  484.7 7.3 convolution_convert_fusion
  504.8 6.5 collective-permute-done.46
  513.4 15.8 %collective-permute-done.47 = bf16[128,2560]{1,0:T(8,128)(2,1)S(1)} collective-permute-done((bf16[128,2560]{1,0:T(8,128)(2,1)S(1)}, bf16[128,2560]{1,0:T(8,128)(2,1)S(1)}, u32[]{:S(2)}, u32[]{:S(2)}) %collective-permute-start.47) | collective-permute-done | bytes 655392 | tf_op jit(solution)/shard_map/ppermute | solution.py:26
  535.9 5.9 shard_map.264
  542.6 8.0 all-gather.1
  551.4 8.8 shard_map.265
  598.0 4.9 add_convert_fusion.1
  602.9 4.9 add_convert_fusion.2
  608.3 4.7 add_convert_fusion
  630.8 4.9 fusion.3
  668.6 4.9 collective-permute-done.53
  682.5 64.9 %collective-permute-done.65 = bf16[640,640]{0,1:T(8,128)(2,1)S(1)} collective-permute-done((bf16[640,640]{0,1:T(8,128)(2,1)S(1)}, bf16[640,640]{0,1:T(8,128)(2,1)S(1)}, u32[]{:S(2)}, u32[]{:S(2)}) %collective-permute-start.65) | collective-permute-done | bytes 819232 | tf_op jit(solution)/shard_map/ppermute | solution.py:47
  750.1 11.8 %collective-permute-done.62 = bf16[640,640]{0,1:T(8,128)(2,1)S(1)} collective-permute-done((bf16[640,640]{0,1:T(8,128)(2,1)S(1)}, bf16[640,640]{0,1:T(8,128)(2,1)S(1)}, u32[]{:S(2)}, u32[]{:S(2)}) %collective-permute-start.62) | collective-permute-done | bytes 819232 | tf_op jit(solution)/shard_map/ppermute | solution.py:47
  780.1 41.4 %collective-permute-done.59 = bf16[640,640]{0,1:T(8,128)(2,1)S(1)} collective-permute-done((bf16[640,640]{0,1:T(8,128)(2,1)S(1)}, bf16[640,640]{0,1:T(8,128)(2,1)S(1)}, u32[]{:S(2)}, u32[]{:S(2)}) %collective-permute-start.59) | collective-permute-done | bytes 819232 | tf_op jit(solution)/shard_map/ppermute | solution.py:47
  823.6 6.6 collective-permute-done.66
  847.5 47.9 %collective-permute-done.60 = bf16[640,320]{0,1:T(8,128)(2,1)S(1)} collective-permute-done((bf16[640,320]{0,1:T(8,128)(2,1)S(1)}, bf16[640,320]{0,1:T(8,128)(2,1)S(1)}, u32[]{:S(2)}, u32[]{:S(2)}) %collective-permute-start.60) | collective-permute-done | bytes 409632 | tf_op jit(solution)/shard_map/ppermute | solution.py:47
  910.4 10.4 %collective-permute-done.86 = f32[4,64,2,640]{3,1,0,2:T(8,128)S(1)} collective-permute-done((f32[4,64,2,640]{3,1,0,2:T(8,128)S(1)}, f32[4,64,2,640]{3,1,0,2:T(8,128)S(1)}, u32[]{:S(2)}, u32[]{:S(2)}) %collective-permute-start.86) | collective-permute-done | bytes 1310752 | tf_op jit(solution)/shard_map/ppermute | solution.py:47
  (538 shorter events, 360.5 us)
Async XLA Ops:
  2.4 30.4 %collective-permute-start.6 = (bf16[2,640]{1,0:T(2,128)(2,1)S(1)}, bf16[2,640]{1,0:T(2,128)(2,1)S(1)}, u32[]{:S(2)}, u32[]{:S(2)}) collective-permute-start(bf16[2,640]{1,0:T(2,128)(2,1)S(1)} %pad_maximum_fusion.20), channel_id=1, source_target_pairs={{0,3},{1,0},{2,1},{3,2},{4,7},{5,4},{6,5},{7,6},{8,11},{9,8},{10,9... | collective-permute-start | bytes 7688 | tf_op jit(solution)/shard_map/ppermute | solution.py:70
  7.5 26.6 %collective-permute-start.7 = (bf16[2,640]{1,0:T(2,128)(2,1)S(1)}, bf16[2,640]{1,0:T(2,128)(2,1)S(1)}, u32[]{:S(2)}, u32[]{:S(2)}) collective-permute-start(bf16[2,640]{1,0:T(2,128)(2,1)S(1)} %pad_maximum_fusion.20), channel_id=1, source_target_pairs={{0,2},{1,3},{2,0},{3,1},{4,6},{5,7},{6,4},{7,5},{8,10},{9,11},{10,... | collective-permute-start | bytes 7688 | tf_op jit(solution)/shard_map/ppermute | solution.py:70
  7.5 32.0 %collective-permute-start.8 = (bf16[2,640]{1,0:T(2,128)(2,1)S(1)}, bf16[2,640]{1,0:T(2,128)(2,1)S(1)}, u32[]{:S(2)}, u32[]{:S(2)}) collective-permute-start(bf16[2,640]{1,0:T(2,128)(2,1)S(1)} %pad_maximum_fusion.20), channel_id=1, source_target_pairs={{0,1},{1,2},{2,3},{3,0},{4,5},{5,6},{6,7},{7,4},{8,9},{9,10},{10,1... | collective-permute-start | bytes 7688 | tf_op jit(solution)/shard_map/ppermute | solution.py:70
  8.5 64.9 %collective-permute-start.1 = (bf16[128,2560]{1,0:T(8,128)(2,1)}, bf16[128,2560]{1,0:T(8,128)(2,1)}, u32[]{:S(2)}, u32[]{:S(2)}) collective-permute-start(bf16[128,2560]{1,0:T(8,128)(2,1)} %bitcast.396), channel_id=1, source_target_pairs={{1,0},{2,1},{3,2},{5,4},{6,5},{7,6},{9,8},{10,9},{11,10},{13,12},{... | collective-permute-start | bytes 1966088 | tf_op jit(solution)/shard_map/ppermute | solution.py:26
  9.8 64.9 %collective-permute-start = (bf16[128,2560]{1,0:T(8,128)(2,1)}, bf16[128,2560]{1,0:T(8,128)(2,1)}, u32[]{:S(2)}, u32[]{:S(2)}) collective-permute-start(bf16[128,2560]{1,0:T(8,128)(2,1)} %bitcast.397), channel_id=1, source_target_pairs={{0,1},{1,2},{2,3},{4,5},{5,6},{6,7},{8,9},{9,10},{10,11},{12,13},{... | collective-permute-start | bytes 1966088 | tf_op jit(solution)/shard_map/ppermute | solution.py:25
  32.8 54.3 %collective-permute-start.33 = (bf16[128,2560]{1,0:T(8,128)(2,1)}, bf16[128,2560]{1,0:T(8,128)(2,1)}, u32[]{:S(2)}, u32[]{:S(2)}) collective-permute-start(bf16[128,2560]{1,0:T(8,128)(2,1)} %bitcast.409), channel_id=1, source_target_pairs={{1,0},{2,1},{3,2},{5,4},{6,5},{7,6},{9,8},{10,9},{11,10},{13,12},{... | collective-permute-start | bytes 1966088 | tf_op jit(solution)/shard_map/ppermute | solution.py:26
  34.1 42.2 %collective-permute-start.32 = (bf16[128,2560]{1,0:T(8,128)(2,1)}, bf16[128,2560]{1,0:T(8,128)(2,1)}, u32[]{:S(2)}, u32[]{:S(2)}) collective-permute-start(bf16[128,2560]{1,0:T(8,128)(2,1)} %bitcast.410), channel_id=1, source_target_pairs={{0,1},{1,2},{2,3},{4,5},{5,6},{6,7},{8,9},{9,10},{10,11},{12,13},{... | collective-permute-start | bytes 1966088 | tf_op jit(solution)/shard_map/ppermute | solution.py:25
  87.1 41.8 %collective-permute-start.34 = (bf16[128,2560]{1,0:T(8,128)(2,1)}, bf16[128,2560]{1,0:T(8,128)(2,1)}, u32[]{:S(2)}, u32[]{:S(2)}) collective-permute-start(bf16[128,2560]{1,0:T(8,128)(2,1)} %collective-permute-done.33), channel_id=1, source_target_pairs={{1,0},{2,1},{5,4},{6,5},{9,8},{10,9},{13,12},{14,13},{17,16},{18,1... | collective-permute-start | bytes 1966088 | tf_op jit(solution)/shard_map/ppermute | solution.py:26
  88.4 29.3 %collective-permute-start.3 = (bf16[128,2560]{1,0:T(8,128)(2,1)}, bf16[128,2560]{1,0:T(8,128)(2,1)S(1)}, u32[]{:S(2)}, u32[]{:S(2)}) collective-permute-start(bf16[128,2560]{1,0:T(8,128)(2,1)} %collective-permute-done.2), channel_id=1, source_target_pairs={{1,0},{5,4},{9,8},{13,12},{17,16},{21,20},{25,24},{29,28}} | collective-permute-start | bytes 1966088 | tf_op jit(solution)/shard_map/ppermute | solution.py:26
  89.7 28.1 %collective-permute-start.5 = (bf16[128,2560]{1,0:T(8,128)(2,1)}, bf16[128,2560]{1,0:T(8,128)(2,1)S(1)}, u32[]{:S(2)}, u32[]{:S(2)}) collective-permute-start(bf16[128,2560]{1,0:T(8,128)(2,1)} %collective-permute-done.4), channel_id=1, source_target_pairs={{2,3},{6,7},{10,11},{14,15},{18,19},{22,23},{26,27},{30,31}} | collective-permute-start | bytes 1966088 | tf_op jit(solution)/shard_map/ppermute | solution.py:25
  90.4 90.2 %collective-permute-start.37 = (bf16[128,2560]{1,0:T(8,128)(2,1)}, bf16[128,2560]{1,0:T(8,128)(2,1)}, u32[]{:S(2)}, u32[]{:S(2)}) collective-permute-start(bf16[128,2560]{1,0:T(8,128)(2,1)} %collective-permute-done.36), channel_id=1, source_target_pairs={{2,3},{6,7},{10,11},{14,15},{18,19},{22,23},{26,27},{30,31}} | collective-permute-start | bytes 1966088 | tf_op jit(solution)/shard_map/ppermute | solution.py:25
  131.0 68.8 %collective-permute-start.35 = (bf16[128,2560]{1,0:T(8,128)(2,1)}, bf16[128,2560]{1,0:T(8,128)(2,1)}, u32[]{:S(2)}, u32[]{:S(2)}) collective-permute-start(bf16[128,2560]{1,0:T(8,128)(2,1)} %collective-permute-done.34), channel_id=1, source_target_pairs={{1,0},{5,4},{9,8},{13,12},{17,16},{21,20},{25,24},{29,28}} | collective-permute-start | bytes 1966088 | tf_op jit(solution)/shard_map/ppermute | solution.py:26
  181.9 21.5 %collective-permute-start.17 = (bf16[128,2560]{1,0:T(8,128)(2,1)S(1)}, bf16[128,2560]{1,0:T(8,128)(2,1)S(1)}, u32[]{:S(2)}, u32[]{:S(2)}) collective-permute-start(bf16[128,2560]{1,0:T(8,128)(2,1)S(1)} %get-tuple-element.109), channel_id=1, source_target_pairs={{3,2},{7,6},{11,10},{15,14},{19,18},{23,22},{27,26},{31,30}} | collective-permute-start | bytes 1966088 | tf_op jit(solution)/shard_map/ppermute | solution.py:39
  215.0 26.1 %collective-permute-start.18 = (bf16[128,2560]{1,0:T(8,128)(2,1)}, bf16[128,2560]{1,0:T(8,128)(2,1)}, u32[]{:S(2)}, u32[]{:S(2)}) collective-permute-start(bf16[128,2560]{1,0:T(8,128)(2,1)} %get-tuple-element.107), channel_id=1, source_target_pairs={{2,1},{3,2},{6,5},{7,6},{10,9},{11,10},{14,13},{15,14},{18,17},{19... | collective-permute-start | bytes 1966088 | tf_op jit(solution)/shard_map/ppermute | solution.py:39
  366.8 29.0 %collective-permute-start.26 = (bf16[128,2560]{1,0:T(8,128)(2,1)S(1)}, bf16[128,2560]{1,0:T(8,128)(2,1)S(1)}, u32[]{:S(2)}, u32[]{:S(2)}) collective-permute-start(bf16[128,2560]{1,0:T(8,128)(2,1)S(1)} %get-tuple-element.104), channel_id=1, source_target_pairs={{0,1},{4,5},{8,9},{12,13},{16,17},{20,21},{24,25},{28,29}} | collective-permute-start | bytes 1966088 | tf_op jit(solution)/shard_map/ppermute | solution.py:38
  368.1 42.8 %collective-permute-start.29 = (bf16[128,2560]{1,0:T(8,128)(2,1)S(1)}, bf16[128,2560]{1,0:T(8,128)(2,1)S(1)}, u32[]{:S(2)}, u32[]{:S(2)}) collective-permute-start(bf16[128,2560]{1,0:T(8,128)(2,1)S(1)} %get-tuple-element.105), channel_id=1, source_target_pairs={{3,2},{7,6},{11,10},{15,14},{19,18},{23,22},{27,26},{31,30}} | collective-permute-start | bytes 1966088 | tf_op jit(solution)/shard_map/ppermute | solution.py:39
  368.9 31.5 %collective-permute-start.41 = (bf16[128,2560]{1,0:T(8,128)(2,1)S(1)}, bf16[128,2560]{1,0:T(8,128)(2,1)S(1)}, u32[]{:S(2)}, u32[]{:S(2)}) collective-permute-start(bf16[128,2560]{1,0:T(8,128)(2,1)S(1)} %get-tuple-element.101), channel_id=1, source_target_pairs={{3,2},{7,6},{11,10},{15,14},{19,18},{23,22},{27,26},{31,30}} | collective-permute-start | bytes 1966088 | tf_op jit(solution)/shard_map/ppermute | solution.py:39
  382.0 27.9 %collective-permute-start.39 = (bf16[128,2560]{1,0:T(8,128)(2,1)S(1)}, bf16[128,2560]{1,0:T(8,128)(2,1)S(1)}, u32[]{:S(2)}, u32[]{:S(2)}) collective-permute-start(bf16[128,2560]{1,0:T(8,128)(2,1)S(1)} %add_convert_fusion.13), channel_id=1, source_target_pairs={{0,1},{1,2},{4,5},{5,6},{8,9},{9,10},{12,13},{13,14},{16,17},{17,1... | collective-permute-start | bytes 1966088 | tf_op jit(solution)/shard_map/ppermute | solution.py:38
  396.0 21.9 %collective-permute-start.27 = (bf16[128,2560]{1,0:T(8,128)(2,1)S(1)}, bf16[128,2560]{1,0:T(8,128)(2,1)S(1)}, u32[]{:S(2)}, u32[]{:S(2)}) collective-permute-start(bf16[128,2560]{1,0:T(8,128)(2,1)S(1)} %add_convert_fusion.17), channel_id=1, source_target_pairs={{0,1},{1,2},{4,5},{5,6},{8,9},{9,10},{12,13},{13,14},{16,17},{17,1... | collective-permute-start | bytes 1966088 | tf_op jit(solution)/shard_map/ppermute | solution.py:38
  418.9 28.6 %collective-permute-start.28 = (bf16[128,2560]{1,0:T(8,128)(2,1)S(1)}, bf16[128,2560]{1,0:T(8,128)(2,1)S(1)}, u32[]{:S(2)}, u32[]{:S(2)}) collective-permute-start(bf16[128,2560]{1,0:T(8,128)(2,1)S(1)} %get-tuple-element.102), channel_id=1, source_target_pairs={{0,1},{1,2},{2,3},{4,5},{5,6},{6,7},{8,9},{9,10},{10,11},{12,13},{... | collective-permute-start | bytes 1966088 | tf_op jit(solution)/shard_map/ppermute | solution.py:38
  424.0 22.2 %collective-permute-start.40 = (bf16[128,2560]{1,0:T(8,128)(2,1)S(1)}, bf16[128,2560]{1,0:T(8,128)(2,1)S(1)}, u32[]{:S(2)}, u32[]{:S(2)}) collective-permute-start(bf16[128,2560]{1,0:T(8,128)(2,1)S(1)} %get-tuple-element.98), channel_id=1, source_target_pairs={{0,1},{1,2},{2,3},{4,5},{5,6},{6,7},{8,9},{9,10},{10,11},{12,13},{... | collective-permute-start | bytes 1966088 | tf_op jit(solution)/shard_map/ppermute | solution.py:38
  430.2 25.6 %collective-permute-start.31 = (bf16[128,2560]{1,0:T(8,128)(2,1)S(1)}, bf16[128,2560]{1,0:T(8,128)(2,1)S(1)}, u32[]{:S(2)}, u32[]{:S(2)}) collective-permute-start(bf16[128,2560]{1,0:T(8,128)(2,1)S(1)} %add_convert_fusion.14), channel_id=1, source_target_pairs={{1,0},{2,1},{3,2},{5,4},{6,5},{7,6},{9,8},{10,9},{11,10},{13,12},{... | collective-permute-start | bytes 1966088 | tf_op jit(solution)/shard_map/ppermute | solution.py:39
  458.0 34.0 %collective-permute-start.45 = (bf16[128,2560]{1,0:T(8,128)(2,1)}, bf16[128,2560]{1,0:T(8,128)(2,1)}, u32[]{:S(2)}, u32[]{:S(2)}) collective-permute-start(bf16[128,2560]{1,0:T(8,128)(2,1)} %get-tuple-element.85), channel_id=1, source_target_pairs={{1,0},{2,1},{3,2},{5,4},{6,5},{7,6},{9,8},{10,9},{11,10},{13,12},{... | collective-permute-start | bytes 1966088 | tf_op jit(solution)/shard_map/ppermute | solution.py:26
  459.3 34.3 %collective-permute-start.44 = (bf16[128,2560]{1,0:T(8,128)(2,1)}, bf16[128,2560]{1,0:T(8,128)(2,1)}, u32[]{:S(2)}, u32[]{:S(2)}) collective-permute-start(bf16[128,2560]{1,0:T(8,128)(2,1)} %get-tuple-element.85), channel_id=1, source_target_pairs={{0,1},{1,2},{2,3},{4,5},{5,6},{6,7},{8,9},{9,10},{10,11},{12,13},{... | collective-permute-start | bytes 1966088 | tf_op jit(solution)/shard_map/ppermute | solution.py:25
  492.0 115.8 %collective-permute-start.73 = (bf16[1920,1280]{0,1:T(8,128)(2,1)}, bf16[1920,1280]{0,1:T(8,128)(2,1)}, u32[]{:S(2)}, u32[]{:S(2)}) collective-permute-start(bf16[1920,1280]{0,1:T(8,128)(2,1)} %convolution_convert_fusion), channel_id=1, source_target_pairs={{0,4},{4,0},{8,12},{12,8},{16,20},{20,16},{24,28},{28,24},{1,5},{5... | collective-permute-start | bytes 14745608 | tf_op jit(solution)/shard_map/ppermute | solution.py:47
  492.0 19.2 %collective-permute-start.46 = (bf16[128,2560]{1,0:T(8,128)(2,1)}, bf16[128,2560]{1,0:T(8,128)(2,1)S(1)}, u32[]{:S(2)}, u32[]{:S(2)}) collective-permute-start(bf16[128,2560]{1,0:T(8,128)(2,1)} %collective-permute-done.45), channel_id=1, source_target_pairs={{1,0},{2,1},{5,4},{6,5},{9,8},{10,9},{13,12},{14,13},{17,16},{18,1... | collective-permute-start | bytes 1966088 | tf_op jit(solution)/shard_map/ppermute | solution.py:26
  499.0 97.0 %collective-permute-start.70 = (bf16[1920,1280]{0,1:T(8,128)(2,1)}, bf16[1920,1280]{0,1:T(8,128)(2,1)}, u32[]{:S(2)}, u32[]{:S(2)}) collective-permute-start(bf16[1920,1280]{0,1:T(8,128)(2,1)} %convolution_convert_fusion.1), channel_id=1, source_target_pairs={{0,4},{4,0},{8,12},{12,8},{16,20},{20,16},{24,28},{28,24},{1,5},{5... | collective-permute-start | bytes 14745608 | tf_op jit(solution)/shard_map/ppermute | solution.py:47
  503.9 99.0 %collective-permute-start.67 = (bf16[1920,1280]{0,1:T(8,128)(2,1)}, bf16[1920,1280]{0,1:T(8,128)(2,1)}, u32[]{:S(2)}, u32[]{:S(2)}) collective-permute-start(bf16[1920,1280]{0,1:T(8,128)(2,1)} %convolution_convert_fusion.2), channel_id=1, source_target_pairs={{0,4},{4,0},{8,12},{12,8},{16,20},{20,16},{24,28},{28,24},{1,5},{5... | collective-permute-start | bytes 14745608 | tf_op jit(solution)/shard_map/ppermute | solution.py:47
  571.5 41.6 %collective-permute-start.81 = (f32[64,2,640]{2,0,1:T(8,128)}, f32[64,2,640]{2,0,1:T(8,128)}, u32[]{:S(2)}, u32[]{:S(2)}) collective-permute-start(f32[64,2,640]{2,0,1:T(8,128)} %get-tuple-element.142), channel_id=1, source_target_pairs={{0,3},{1,0},{2,1},{3,2},{4,7},{5,4},{6,5},{7,6},{8,11},{9,8},{10,9... | collective-permute-start | bytes 983048 | tf_op jit(solution)/shard_map/ppermute | solution.py:83
  594.6 24.7 %collective-permute-start.82 = (f32[64,2,640]{2,0,1:T(8,128)S(1)}, f32[64,2,640]{2,0,1:T(8,128)S(1)}, u32[]{:S(2)}, u32[]{:S(2)}) collective-permute-start(f32[64,2,640]{2,0,1:T(8,128)S(1)} %copy-done.68), channel_id=1, source_target_pairs={{0,2},{1,3},{2,0},{3,1},{4,6},{5,7},{6,4},{7,5},{8,10},{9,11},{10,... | collective-permute-start | bytes 983048 | tf_op jit(solution)/shard_map/ppermute | solution.py:83
  596.0 24.0 %collective-permute-start.83 = (f32[64,2,640]{2,0,1:T(8,128)S(1)}, f32[64,2,640]{2,0,1:T(8,128)S(1)}, u32[]{:S(2)}, u32[]{:S(2)}) collective-permute-start(f32[64,2,640]{2,0,1:T(8,128)S(1)} %copy-done.67), channel_id=1, source_target_pairs={{0,1},{1,2},{2,3},{3,0},{4,5},{5,6},{6,7},{7,4},{8,9},{9,10},{10,1... | collective-permute-start | bytes 983048 | tf_op jit(solution)/shard_map/ppermute | solution.py:83
  602.9 61.5 %collective-permute-start.64 = (bf16[640,1280]{0,1:T(8,128)(2,1)}, bf16[640,1280]{0,1:T(8,128)(2,1)}, u32[]{:S(2)}, u32[]{:S(2)}) collective-permute-start(bf16[640,1280]{0,1:T(8,128)(2,1)} %convolution_convert_fusion.3), channel_id=1, source_target_pairs={{0,4},{4,0},{8,12},{12,8},{16,20},{20,16},{24,28},{28,24},{1,5},{5... | collective-permute-start | bytes 4915208 | tf_op jit(solution)/shard_map/ppermute | solution.py:47
  607.8 66.2 %collective-permute-start.61 = (bf16[640,1280]{0,1:T(8,128)(2,1)}, bf16[640,1280]{0,1:T(8,128)(2,1)}, u32[]{:S(2)}, u32[]{:S(2)}) collective-permute-start(bf16[640,1280]{0,1:T(8,128)(2,1)} %convolution_convert_fusion.4), channel_id=1, source_target_pairs={{0,4},{4,0},{8,12},{12,8},{16,20},{20,16},{24,28},{28,24},{1,5},{5... | collective-permute-start | bytes 4915208 | tf_op jit(solution)/shard_map/ppermute | solution.py:47
  666.9 100.9 %collective-permute-start.71 = (bf16[1920,640]{0,1:T(8,128)(2,1)S(1)}, bf16[1920,640]{0,1:T(8,128)(2,1)S(1)}, u32[]{:S(2)}, u32[]{:S(2)}) collective-permute-start(bf16[1920,640]{0,1:T(8,128)(2,1)S(1)} %copy-done.92), channel_id=1, source_target_pairs={{0,8},{4,12},{8,0},{12,4},{16,24},{20,28},{24,16},{28,20},{1,9},{5... | collective-permute-start | bytes 7372808 | tf_op jit(solution)/shard_map/ppermute | solution.py:47
  673.5 96.9 %collective-permute-start.68 = (bf16[1920,640]{0,1:T(8,128)(2,1)S(1)}, bf16[1920,640]{0,1:T(8,128)(2,1)S(1)}, u32[]{:S(2)}, u32[]{:S(2)}) collective-permute-start(bf16[1920,640]{0,1:T(8,128)(2,1)S(1)} %copy-done.93), channel_id=1, source_target_pairs={{0,16},{4,20},{8,24},{12,28},{16,0},{20,4},{24,8},{28,12},{1,17},{... | collective-permute-start | bytes 7372808 | tf_op jit(solution)/shard_map/ppermute | solution.py:47
  677.0 98.8 %collective-permute-start.74 = (bf16[1920,640]{0,1:T(8,128)(2,1)S(1)}, bf16[1920,640]{0,1:T(8,128)(2,1)S(1)}, u32[]{:S(2)}, u32[]{:S(2)}) collective-permute-start(bf16[1920,640]{0,1:T(8,128)(2,1)S(1)} %copy-done.94), channel_id=1, source_target_pairs={{0,8},{4,12},{8,0},{12,4},{16,24},{20,28},{24,16},{28,20},{1,9},{5... | collective-permute-start | bytes 7372808 | tf_op jit(solution)/shard_map/ppermute | solution.py:47
  679.2 68.2 %collective-permute-start.65 = (bf16[640,640]{0,1:T(8,128)(2,1)S(1)}, bf16[640,640]{0,1:T(8,128)(2,1)S(1)}, u32[]{:S(2)}, u32[]{:S(2)}) collective-permute-start(bf16[640,640]{0,1:T(8,128)(2,1)S(1)} %add_convert_fusion.3), channel_id=1, source_target_pairs={{0,16},{4,20},{8,24},{12,28},{16,0},{20,4},{24,8},{28,12},{1,17},{... | collective-permute-start | bytes 2457608 | tf_op jit(solution)/shard_map/ppermute | solution.py:47
  682.2 79.7 %collective-permute-start.62 = (bf16[640,640]{0,1:T(8,128)(2,1)S(1)}, bf16[640,640]{0,1:T(8,128)(2,1)S(1)}, u32[]{:S(2)}, u32[]{:S(2)}) collective-permute-start(bf16[640,640]{0,1:T(8,128)(2,1)S(1)} %add_convert_fusion.4), channel_id=1, source_target_pairs={{0,16},{4,20},{8,24},{12,28},{16,0},{20,4},{24,8},{28,12},{1,17},{... | collective-permute-start | bytes 2457608 | tf_op jit(solution)/shard_map/ppermute | solution.py:47
  747.4 95.4 %collective-permute-start.85 = (f32[4,64,2,640]{3,1,0,2:T(8,128)S(1)}, f32[4,64,2,640]{3,1,0,2:T(8,128)S(1)}, u32[]{:S(2)}, u32[]{:S(2)}) collective-permute-start(f32[4,64,2,640]{3,1,0,2:T(8,128)S(1)} %fusion.219), channel_id=1, source_target_pairs={{0,8},{4,12},{8,0},{12,4},{16,24},{20,28},{24,16},{28,20},{1,9},{5... | collective-permute-start | bytes 3932168 | tf_op jit(solution)/shard_map/ppermute | solution.py:47
  761.9 81.4 %collective-permute-start.54 = (bf16[128,2560]{1,0:T(8,128)(2,1)S(1)}, bf16[128,2560]{1,0:T(8,128)(2,1)S(1)}, u32[]{:S(2)}, u32[]{:S(2)}) collective-permute-start(bf16[128,2560]{1,0:T(8,128)(2,1)S(1)} %get-tuple-element.94), channel_id=1, source_target_pairs={{0,1},{1,2},{2,3},{4,5},{5,6},{6,7},{8,9},{9,10},{10,11},{12,13},{... | collective-permute-start | bytes 1966088 | tf_op jit(solution)/shard_map/ppermute | solution.py:38
  767.8 53.6 %collective-permute-start.59 = (bf16[640,640]{0,1:T(8,128)(2,1)S(1)}, bf16[640,640]{0,1:T(8,128)(2,1)S(1)}, u32[]{:S(2)}, u32[]{:S(2)}) collective-permute-start(bf16[640,640]{0,1:T(8,128)(2,1)S(1)} %add_convert_fusion.5), channel_id=1, source_target_pairs={{0,8},{4,12},{8,0},{12,4},{16,24},{20,28},{24,16},{28,20},{1,9},{5... | collective-permute-start | bytes 2457608 | tf_op jit(solution)/shard_map/ppermute | solution.py:47
  770.5 74.4 %collective-permute-start.57 = (bf16[128,2560]{1,0:T(8,128)(2,1)S(1)}, bf16[128,2560]{1,0:T(8,128)(2,1)S(1)}, u32[]{:S(2)}, u32[]{:S(2)}) collective-permute-start(bf16[128,2560]{1,0:T(8,128)(2,1)S(1)} %add_convert_fusion.6), channel_id=1, source_target_pairs={{1,0},{2,1},{3,2},{5,4},{6,5},{7,6},{9,8},{10,9},{11,10},{13,12},{... | collective-permute-start | bytes 1966088 | tf_op jit(solution)/shard_map/ppermute | solution.py:39
  775.8 54.4 %collective-permute-start.66 = (bf16[640,320]{0,1:T(8,128)(2,1)S(1)}, bf16[640,320]{0,1:T(8,128)(2,1)S(1)}, u32[]{:S(2)}, u32[]{:S(2)}) collective-permute-start(bf16[640,320]{0,1:T(8,128)(2,1)S(1)} %fusion.52), channel_id=1, source_target_pairs={{0,8},{4,12},{8,0},{12,4},{16,24},{20,28},{24,16},{28,20},{1,9},{5... | collective-permute-start | bytes 1228808 | tf_op jit(solution)/shard_map/ppermute | solution.py:47
  830.3 67.7 %collective-permute-start.75 = (bf16[1920,320]{0,1:T(8,128)(2,1)S(1)}, bf16[1920,320]{0,1:T(8,128)(2,1)S(1)}, u32[]{:S(2)}, u32[]{:S(2)}) collective-permute-start(bf16[1920,320]{0,1:T(8,128)(2,1)S(1)} %fusion.23), channel_id=1, source_target_pairs={{0,16},{4,20},{8,24},{12,28},{16,0},{20,4},{24,8},{28,12},{1,17},{... | collective-permute-start | bytes 3686408 | tf_op jit(solution)/shard_map/ppermute | solution.py:47
  838.1 64.0 %collective-permute-start.72 = (bf16[1920,320]{0,1:T(8,128)(2,1)S(1)}, bf16[1920,320]{0,1:T(8,128)(2,1)S(1)}, u32[]{:S(2)}, u32[]{:S(2)}) collective-permute-start(bf16[1920,320]{0,1:T(8,128)(2,1)S(1)} %fusion.22), channel_id=1, source_target_pairs={{0,16},{4,20},{8,24},{12,28},{16,0},{20,4},{24,8},{28,12},{1,17},{... | collective-permute-start | bytes 3686408 | tf_op jit(solution)/shard_map/ppermute | solution.py:47
  842.8 63.5 %collective-permute-start.69 = (bf16[1920,320]{0,1:T(8,128)(2,1)S(1)}, bf16[1920,320]{0,1:T(8,128)(2,1)S(1)}, u32[]{:S(2)}, u32[]{:S(2)}) collective-permute-start(bf16[1920,320]{0,1:T(8,128)(2,1)S(1)} %fusion.21), channel_id=1, source_target_pairs={{0,8},{4,12},{8,0},{12,4},{16,24},{20,28},{24,16},{28,20},{1,9},{5... | collective-permute-start | bytes 3686408 | tf_op jit(solution)/shard_map/ppermute | solution.py:47
  843.3 52.0 %collective-permute-start.60 = (bf16[640,320]{0,1:T(8,128)(2,1)S(1)}, bf16[640,320]{0,1:T(8,128)(2,1)S(1)}, u32[]{:S(2)}, u32[]{:S(2)}) collective-permute-start(bf16[640,320]{0,1:T(8,128)(2,1)S(1)} %fusion.51), channel_id=1, source_target_pairs={{0,16},{4,20},{8,24},{12,28},{16,0},{20,4},{24,8},{28,12},{1,17},{... | collective-permute-start | bytes 1228808 | tf_op jit(solution)/shard_map/ppermute | solution.py:47
  844.9 75.9 %collective-permute-start.86 = (f32[4,64,2,640]{3,1,0,2:T(8,128)S(1)}, f32[4,64,2,640]{3,1,0,2:T(8,128)S(1)}, u32[]{:S(2)}, u32[]{:S(2)}) collective-permute-start(f32[4,64,2,640]{3,1,0,2:T(8,128)S(1)} %add.710), channel_id=1, source_target_pairs={{0,16},{4,20},{8,24},{12,28},{16,0},{20,4},{24,8},{28,12},{1,17},{... | collective-permute-start | bytes 3932168 | tf_op jit(solution)/shard_map/ppermute | solution.py:47
  (140 other events, 1899.7 us)

commit v2 on v1

v2 whole, which is shorter than its diff:
```python
import functools

import jax
import jax.numpy as jnp
from jax import lax
from jax.experimental import pallas as pl
from jax.experimental.pallas import tpu as pltpu
from jax.sharding import PartitionSpec as P

EPS = 1e-06
DECAY_SCALE = 8.0
HALF = 128
GELU_C = 0.7978845608028654
GELU_K = 0.044715
F32 = jnp.float32
BF16 = jnp.bfloat16
OWN, FAR, LEND, SLOT, REL = 16, 17, 18, 19, 20


def ring(value, axis="wshard"):
    count = lax.axis_size(axis)
    return lax.ppermute(value, axis, [(i, (i + 1) % count) for i in range(count)])


def ring_gather(part, axis="wshard"):
    slots = [part]
    for _ in range(1, lax.axis_size(axis)):
        slots.append(ring(slots[-1], axis))
    return slots


def join(*values):
    return lax.optimization_barrier(values)


def ring_add(slot, total, axis="wshard"):
    mine = slot if total is None else slot.astype(F32) + total.astype(F32)
    mine = mine.astype(BF16)
    return mine, ring(mine, axis)


def ring_scatter(slots, axis="wshard"):
    total = None
    for slot in slots[1:]:
        _, total = ring_add(slot, total, axis)
    return slots[0] + total.astype(F32)


def tie(value, *others):
    return lax.optimization_barrier((value,) + others)[0]


def exchange_pair(value, axis, bit):
    count = lax.axis_size(axis)
    return lax.ppermute(value, axis, [(i, i ^ bit) for i in range(count)])


def bits_of(count):
    return [1 << i for i in range(count.bit_length() - 1)]


def sum_all(value, axis):
    for bit in bits_of(lax.axis_size(axis)):
        value = value + exchange_pair(value, axis, bit)
    return value


def from_slots(slots, axis="wshard"):
    count = lax.axis_size(axis)
    place = lax.axis_index(axis)
    back = jnp.stack(slots[::-1] + slots[::-1])
    return lax.dynamic_slice_in_dim(back, count - 1 - place, count, 0)


def all_parts(part, axis="wshard"):
    count = lax.axis_size(axis)
    slots = [part] + [
        lax.ppermute(part, axis, [(i, (i + k) % count) for i in range(count)])
        for k in range(1, count)
    ]
    return from_slots(slots, axis)


def swap_parts(parts, axis="wshard"):
    count = lax.axis_size(axis)
    place = lax.axis_index(axis)
    slots = []
    for k in range(count):
        mine = lax.dynamic_index_in_dim(parts, (place + k) % count, 0, keepdims=False)
        if k:
            mine = lax.ppermute(mine, axis, [(i, (i + k) % count) for i in range(count)])
        slots.append(mine)
    return from_slots(slots, axis)


def relative_order(count, order):
    offsets = [0]
    for bit in reversed(order):
        offsets = offsets + [o | bit for o in offsets]
    return offsets


def prefix_step(state, bit, back, axis="seq"):
    total, before = state
    other = exchange_pair(total, axis, bit)
    high = (lax.axis_index(axis) & bit) != 0
    first = high != back
    before = jnp.stack(
        [
            jnp.where(first, before[:, 0] + before[:, 1] * other[:, 0], before[:, 0]),
            jnp.where(first, before[:, 1] * other[:, 1], before[:, 1]),
        ],
        axis=1,
    )
    total = jnp.stack(
        [
            jnp.where(
                first,
                total[:, 0] + total[:, 1] * other[:, 0],
                other[:, 0] + other[:, 1] * total[:, 0],
            ),
            total[:, 1] * other[:, 1],
        ],
        axis=1,
    )
    return total, before


def prefix_start(ends):
    ones = jnp.ones_like(ends[:, 0])
    return ends, jnp.stack([jnp.zeros_like(ones), ones], axis=1)


def rank_of(offset, order):
    rank = jnp.int32(0)
    for i, bit in enumerate(order):
        rank = rank + jnp.where((offset & bit) != 0, 1 << (len(order) - 1 - i), 0)
    return rank


def turn_kernel(at_ref, *refs, slots):
    outs, held_ref = refs[slots:-1], refs[-1]
    row = 0
    for ref in refs[:slots]:
        for col in range(0, ref.shape[1], HALF):
            held_ref[col : col + HALF, row : row + ref.shape[0]] = ref[:, col : col + HALF].T
        row += ref.shape[0]
    count = at_ref.shape[1]
    width = held_ref.shape[0] // count
    for out, ref in enumerate(outs):
        for q in range(count):
            start = pl.multiple_of(at_ref[out, q], 16)
            ref[q * width : (q + 1) * width] = held_ref[pl.ds(start, width)]


def turned(parts, orders, axis="seq"):
    count = lax.axis_size(axis)
    place = lax.axis_index(axis)
    model = parts[0].shape[1]
    rows = sum(part.shape[0] for part in parts)
    width = model // count
    at = [(place ^ jnp.array(relative_order(count, order), jnp.int32)) * width for order in orders]
    vmem = pl.BlockSpec(memory_space=pltpu.VMEM)
    return pl.pallas_call(
        functools.partial(turn_kernel, slots=len(parts)),
        in_specs=[pl.BlockSpec(memory_space=pltpu.SMEM)] + [vmem] * len(parts),
        out_specs=(vmem,) * len(orders),
        out_shape=(jax.ShapeDtypeStruct((model, rows), parts[0].dtype),) * len(orders),
        scratch_shapes=[pltpu.VMEM((model, rows), parts[0].dtype)],
    )(jnp.stack(at).astype(jnp.int32), *parts)


class Halving:
    def __init__(self, left, right, order, extra=None, axis="seq"):
        self.left, self.right, self.order, self.axis = left, right, list(order), axis
        self.extra = extra
        self.held = []
        self.size = left.shape[0]

    def part(self, lo, hi, after):
        width = self.right.shape[1]
        right = tie(self.right, *after) if after else self.right
        total = dot_nn(self.left[lo:hi], right)
        for piece in self.held:
            total = total + piece[lo:hi, :width].astype(F32)
        if self.extra is None:
            return total, None
        more = self.extra[lo:hi]
        for piece in self.held:
            more = more + piece[lo:hi, width:].astype(F32)
        return total, more

    def give(self, *after):
        total, more = self.part(self.size // 2, self.size, after)
        total = total.astype(BF16)
        return total if more is None else jnp.concatenate([total, more.astype(BF16)], axis=1)

    def send(self, half):
        self.held.append(exchange_pair(half, self.axis, self.order.pop(0)))
        self.size //= 2

    def finish(self, *after):
        while self.order:
            self.send(self.give(*after))
        total, more = self.part(0, self.size, after)
        return (total.T,) if more is None else (total.T, more)


def norm_kernel(x_ref, part_ref, out_ref):
    @pl.when(pl.program_id(0) == 0)
    def _():
        out_ref[...] = jnp.zeros_like(out_ref)

    values = x_ref[...].astype(F32)
    out_ref[...] += jnp.sum(part_ref[...] * (values * rms_scale(values)), axis=0, keepdims=True)


def norm_grad(x, part, slots):
    spec = pl.BlockSpec((x.shape[0] // slots, x.shape[1]), lambda i: (i, 0))
    return pl.pallas_call(
        norm_kernel,
        grid=(slots,),
        in_specs=[spec, spec],
        out_specs=pl.BlockSpec((1, x.shape[1]), lambda i: (0, 0)),
        out_shape=jax.ShapeDtypeStruct((1, x.shape[1]), F32),
    )(x, part)


def expm1_neg(v):
    poly = 1.0 + v / 9.0
    for n in range(8, 1, -1):
        poly = 1.0 + poly * v / float(n)
    return jnp.where(v > -0.5, v * poly, jnp.exp(v) - 1.0)


def gelu_parts(v):
    t = jnp.tanh(GELU_C * (v + GELU_K * v * v * v))
    value = 0.5 * v * (1.0 + t)
    slope = 0.5 * (1.0 + t) + 0.5 * v * (1.0 - t * t) * GELU_C * (1.0 + 3.0 * GELU_K * v * v)
    return value, slope


def gelu_value(v):
    return 0.5 * v * (1.0 + jnp.tanh(GELU_C * (v + GELU_K * v * v * v)))


def row_ids(shape):
    return lax.broadcasted_iota(jnp.int32, shape, 0)


def shift_down(v, k, fill, rows):
    count = v.shape[0]
    if k % 8 == 0:
        return jnp.concatenate([jnp.full((k, v.shape[1]), fill, F32), v[: count - k]], axis=0)
    return jnp.where(rows < k, fill, pltpu.roll(v, k, 0))


def shift_up(v, k, fill, rows):
    count = v.shape[0]
    if k % 8 == 0:
        return jnp.concatenate([v[k:], jnp.full((k, v.shape[1]), fill, F32)], axis=0)
    return jnp.where(rows >= count - k, fill, pltpu.roll(v, count - k, 0))


def run_scan(decay, value, shift, rows):
    k = 1
    while k < value.shape[0]:
        value = value + decay * shift(value, k, 0.0, rows)
        decay = decay * shift(decay, k, 1.0, rows)
        k *= 2
    return decay, value


def assemble_kernel(at_ref, *refs):
    out_ref = refs[-1]
    for i, ref in enumerate(refs[:-1]):
        for j in range(ref.shape[0]):
            row = pl.multiple_of(at_ref[i, j], 16)
            for m in range(out_ref.shape[0]):
                for g in range(2):
                    out_ref[m, pl.ds(row, 16), g * HALF : (g + 1) * HALF] = ref[
                        j, g, :, m * HALF : (m + 1) * HALF
                    ]


def branch_kernel(x_ref, gain_ref, wx_ref, wy_ref, *refs):
    n_ref, bx_ref, by_ref = refs[-3:]
    values = x_ref[...].astype(F32)
    low = (values * rms_scale(values) * gain_ref[...]).astype(BF16)
    n_ref[...] = low
    bx_ref[0] = dot_nt(low, wx_ref[...]).astype(BF16)
    by_ref[0] = dot_nt(low, wy_ref[...])


def branch_call(x, gain, w_x, w_y, held, slots, place):
    rows, model = x.shape
    chans = w_x.shape[0]
    kept = pl.BlockSpec(memory_space=pl.ANY)
    whole = lambda shape: pl.BlockSpec(shape, lambda i: (0,) * len(shape))
    out = pl.BlockSpec((1, rows, chans), lambda i: (place, 0, 0))
    return pl.pallas_call(
        branch_kernel,
        grid=(1,),
        in_specs=[whole(x.shape), whole(gain.shape), whole(w_x.shape), whole(w_y.shape)]
        + [kept] * len(held),
        out_specs=(pl.BlockSpec((rows, model), lambda i: (place, 0)), out, out),
        out_shape=(
            jax.ShapeDtypeStruct((slots * rows, model), BF16),
            jax.ShapeDtypeStruct((slots, rows, chans), BF16),
            jax.ShapeDtypeStruct((slots, rows, chans), F32),
        ),
        input_output_aliases={4 + i: i for i in range(len(held))},
    )(x, gain, w_x, w_y, *held)


def conv_kernel(off_ref, bx_ref, halo_ref, vec_ref, conv_ref, low_ref, lend_ref, ext_ref):
    tokens = bx_ref.shape[1]
    ext_ref[0:8] = halo_ref[0]
    ext_ref[8:] = bx_ref[0].astype(F32)
    total = vec_ref[4:5] + jnp.zeros((tokens, bx_ref.shape[2]), F32)
    for k in range(4):
        total = total + vec_ref[k : k + 1] * ext_ref[8 - k : 8 - k + tokens]
    conv_ref[0] = total
    low_ref[0] = total.astype(BF16)
    lend_ref[0] = low_ref[0, :, pl.ds(pl.multiple_of(off_ref[LEND], HALF), lend_ref.shape[2])]


def gates_kernel(
    off_ref, low_ref, lent_ref, conv_ref, wg_ref, vec_ref,
    s0_ref, s1_ref, h_ref, a_ref, end_ref, win_ref,
):
    tokens = win_ref.shape[1]
    rows = row_ids((tokens, HALF))
    own = pl.multiple_of(off_ref[OWN], HALF)
    far = pl.multiple_of(off_ref[FAR], HALF)
    win_ref[0, :, pl.ds(own, low_ref.shape[2])] = low_ref[0]
    win_ref[0, :, pl.ds(far, lent_ref.shape[2])] = lent_ref[0]
    for m in range(wg_ref.shape[0]):
        cols = slice(m * HALF, (m + 1) * HALF)
        src = pl.multiple_of(off_ref[m], HALF)
        logits = jnp.dot(
            win_ref[0, :, pl.ds(src, 2 * HALF)], wg_ref[m], preferred_element_type=F32
        )
        s0 = jax.nn.sigmoid(logits[:, :HALF] + vec_ref[0:1, cols])
        s1 = jax.nn.sigmoid(logits[:, HALF:] + vec_ref[1:2, cols])
        log_a = vec_ref[2:3, cols] * s0
        value = jnp.sqrt(-expm1_neg(2.0 * log_a)) * (conv_ref[0, :, cols] * s1)
        decay, state = run_scan(jnp.exp(log_a), value, shift_down, rows)
        s0_ref[0, :, cols] = s0
        s1_ref[0, :, cols] = s1
        h_ref[0, :, cols] = state
        a_ref[0, :, cols] = decay
        end_ref[0, 0:1, cols] = state[tokens - 1 :]
        end_ref[0, 1:2, cols] = decay[tokens - 1 :]


def back_scan_kernel(
    off_ref, gm_ref, by_ref, st_ref, s0_ref, vec_ref, gy_ref, c_ref, a_ref, end_ref
):
    tokens = gm_ref.shape[1]
    rows = row_ids((tokens, HALF))
    for m in range(gm_ref.shape[2] // HALF):
        cols = slice(m * HALF, (m + 1) * HALF)
        gm = gm_ref[0, :, cols]
        value, slope = gelu_parts(by_ref[0, :, cols])
        low = st_ref[0, :, cols].astype(BF16).astype(F32)
        gy_ref[0, :, cols] = (gm * low * slope).astype(BF16)
        grad = (gm * value).astype(BF16).astype(F32)
        decay = jnp.exp(vec_ref[2:3, cols] * s0_ref[0, :, cols])
        prod, carried = run_scan(shift_up(decay, 1, 1.0, rows), grad, shift_up, rows)
        c_ref[0, :, cols] = carried
        a_ref[0, :, cols] = prod
        end_ref[0, 0:1, cols] = decay[0:1] * carried[0:1]
        end_ref[0, 1:2, cols] = decay[0:1] * prod[0:1]


def back_gates_kernel(
    off_ref,
    c_ref,
    a_ref,
    edge_ref,
    s0_ref,
    s1_ref,
    conv_ref,
    st_ref,
    win_ref,
    wg_ref,
    vec_ref,
    near_ref,
    far_ref,
    piece_ref,
    sum_ref,
    dw_ref,
    gc_ref,
    *,
    count,
    planes,
):
    tokens = c_ref.shape[1]
    rows = row_ids((tokens, HALF))

    @pl.when(pl.program_id(0) == 0)
    def _():
        dw_ref[...] = jnp.zeros_like(dw_ref)
        sum_ref[...] = jnp.zeros_like(sum_ref)

    gc_ref[...] = jnp.zeros_like(gc_ref)
    for m in range(wg_ref.shape[0]):
        cols = slice(m * HALF, (m + 1) * HALF)
        src = pl.multiple_of(off_ref[m], HALF)
        own = pl.multiple_of(off_ref[OWN] + m * HALF, HALF)
        carried = c_ref[0, :, cols] + a_ref[0, :, cols] * edge_ref[0, 1:2, cols]
        before = shift_down(st_ref[0, :, cols], 1, 0.0, rows)
        before = jnp.where(rows == 0, edge_ref[0, 0:1, cols], before)
        s0 = s0_ref[0, :, cols]
        s1 = s1_ref[0, :, cols]
        conv = conv_ref[0, :, cols]
        coef = vec_ref[2:3, cols]
        log_a = coef * s0
        root = jnp.sqrt(-expm1_neg(2.0 * log_a))
        g_log = carried * (jnp.exp(log_a) * before - jnp.exp(2.0 * log_a) * (conv * s1) / root)
        g_log = g_log.astype(BF16).astype(F32)
        g_in = (carried * root).astype(BF16).astype(F32)
        rec = (g_log * coef * s0 * (1.0 - s0)).astype(BF16)
        inp = (g_in * conv * s1 * (1.0 - s1)).astype(BF16)
        sum_ref[0:1, cols] += jnp.sum(g_log * s0, axis=0, keepdims=True)
        sum_ref[1:2, cols] += jnp.sum(rec.astype(F32), axis=0, keepdims=True)
        sum_ref[2:3, cols] += jnp.sum(inp.astype(F32), axis=0, keepdims=True)
        both = jnp.concatenate([rec, inp], axis=1)
        gc_ref[:, pl.ds(src, 2 * HALF)] += lax.dot_general(
            both, wg_ref[m], (((1,), (1,)), ((), ())), preferred_element_type=F32
        )
        gc_ref[:, pl.ds(own, HALF)] += g_in * s1
        dw_ref[m] += lax.dot_general(
            win_ref[0, :, pl.ds(src, 2 * HALF)],
            both,
            (((0,), (0,)), ((), ())),
            preferred_element_type=F32,
        )

    own = pl.multiple_of(off_ref[OWN], HALF)
    far = pl.multiple_of(off_ref[FAR], HALF)
    near_ref[0] = gc_ref[:, pl.ds(own, near_ref.shape[2])]
    far_ref[0] = gc_ref[:, pl.ds(far, far_ref.shape[2])]

    @pl.when(pl.program_id(0) == pl.num_programs(0) - 1)
    def _():
        blocks = dw_ref.shape[0]
        width = dw_ref.shape[1] // (planes * count)
        if width % 8:
            piece_ref[...] = dw_ref[...]
            return
        row = 0
        for q in range(count):
            for j in range(planes):
                first = pl.multiple_of((j * count + off_ref[REL + q]) * width, width)
                for g in range(2):
                    for m in range(blocks):
                        piece_ref[row : row + width] = dw_ref[
                            m, pl.ds(first, width), g * HALF : (g + 1) * HALF
                        ]
                        row += width


def back_conv_kernel(
    off_ref, gc_ref, got_ref, after_ref, bx_ref, halo_ref, vec_ref, gx_ref, sum_ref, g_ext, x_ext
):
    tokens = gc_ref.shape[1]

    @pl.when(pl.program_id(0) == 0)
    def _():
        sum_ref[...] = jnp.zeros_like(sum_ref)

    lend = pl.multiple_of(off_ref[LEND], HALF)
    g_ext[0:tokens] = gc_ref[0]
    g_ext[0:tokens, pl.ds(lend, got_ref.shape[2])] += got_ref[0]
    grad = g_ext[0:tokens]
    g_ext[tokens:] = after_ref[0]
    x_ext[0:8] = halo_ref[0]
    x_ext[8:] = bx_ref[0].astype(F32)
    total = jnp.zeros_like(grad)
    for k in range(4):
        total = total + vec_ref[k : k + 1] * g_ext[k : k + tokens]
        sum_ref[k : k + 1] += jnp.sum(
            grad * x_ext[8 - k : 8 - k + tokens], axis=0, keepdims=True
        )
    sum_ref[4:5] += jnp.sum(grad, axis=0, keepdims=True)
    gx_ref[0] = total.astype(BF16)


def ffn_kernel(two_ref, g_ref, wg_ref, wu_ref, wd_ref, *refs):
    act_ref, gate_ref, up_ref, part_ref, total_ref = refs[-5:]
    step = pl.program_id(0)
    gate = dot_nt(two_ref[...], wg_ref[...])
    up = dot_nt(two_ref[...], wu_ref[...])
    grad = dot_nt(g_ref[...], wd_ref[...])
    value, slope = gelu_parts(gate)
    act_ref[...] = (value * up).astype(BF16)
    grad_gate = (grad * up * slope).astype(BF16)
    grad_up = (grad * value).astype(BF16)
    gate_ref[...] = grad_gate
    up_ref[...] = grad_up
    part = dot_nn(grad_gate, wg_ref[...]) + dot_nn(grad_up, wu_ref[...])

    @pl.when(step == 0)
    def _():
        total_ref[...] = part

    @pl.when(step > 0)
    def _():
        total_ref[...] += part

    @pl.when(step == pl.num_programs(0) - 1)
    def _():
        part_ref[...] = total_ref[...].astype(part_ref.dtype)


def ffn_call(two, grad, w_gate, w_up, w_down, held, slots, place, kind):
    rows, model = two.shape
    hidden = w_gate.shape[0]
    width = next(w for w in (384, 256, HALF) if hidden % w == 0)
    tok = pl.BlockSpec((rows, model), lambda i: (0, 0))
    weight = pl.BlockSpec((width, model), lambda i: (i, 0))
    wide = pl.BlockSpec((rows, width), lambda i: (place, i))
    kept = pl.BlockSpec(memory_space=pl.ANY)
    return pl.pallas_call(
        ffn_kernel,
        grid=(hidden // width,),
        in_specs=[tok, tok, weight, weight, weight] + [kept] * len(held),
        out_specs=(wide,) * 3 + (tok,),
        out_shape=(jax.ShapeDtypeStruct((slots * rows, hidden), BF16),) * 3
        + (jax.ShapeDtypeStruct((rows, model), kind),),
        scratch_shapes=[pltpu.VMEM((rows, model), F32)],
        input_output_aliases={5 + i: i for i in range(len(held))},
    )(two, grad, w_gate, w_up, w_down, *held)


def slot_spec(rows, width):
    return pl.BlockSpec((1, rows, width), lambda i, off: (i, 0, 0))


def partner_spec(rows, width, slots):
    return pl.BlockSpec((1, rows, width), lambda i, off: ((i + off[SLOT]) % slots, 0, 0))


def whole_spec(shape):
    zero = (0,) * len(shape)
    return pl.BlockSpec(shape, lambda i, off: zero)


def call(kernel, slots, offs, ins, in_specs, outs, out_specs, scratch=()):
    return pl.pallas_call(
        kernel,
        grid_spec=pltpu.PrefetchScalarGridSpec(
            num_scalar_prefetch=1,
            grid=(slots,),
            in_specs=in_specs,
            out_specs=out_specs,
            scratch_shapes=list(scratch),
        ),
        out_shape=outs,
    )(offs, *ins)


def rms_scale(values):
    return lax.rsqrt(jnp.mean(values * values, axis=-1, keepdims=True) + EPS)


def dot_nt(a, b):
    return lax.dot_general(a, b, (((1,), (1,)), ((), ())), preferred_element_type=F32)


def dot_nn(a, b):
    return jnp.dot(a, b, preferred_element_type=F32)


def on_device(
    block_in,
    cotangent,
    w_x,
    w_y,
    w_out,
    w_gate,
    w_up,
    w_down,
    norm1_gain,
    norm2_gain,
    conv_weight,
    conv_bias,
    gate_weight,
    gate_bias,
    decay_param,
):
    slots = lax.axis_size("wshard")
    place = lax.axis_index("wshard")
    count = lax.axis_size("seq")
    spot = lax.axis_index("seq")
    x_own = block_in[0]
    g_own = cotangent[0]
    tokens, model = x_own.shape
    chans = w_x.shape[0]
    heads, inner = gate_weight.shape[1], gate_weight.shape[3]
    taps = conv_weight.shape[0]
    blocks = chans // HALF
    offset = (chans * place) % inner
    window = -(-(chans + (chans % inner)) // inner) * inner
    odd = offset != 0
    bits = bits_of(count)
    order_a = bits
    order_b = bits[:1] + bits[1:][::-1]
    slot_rows = slots * tokens

    def by_slot(v):
        return v.reshape(slots, tokens, v.shape[-1])

    def flat(v):
        return v.reshape(slot_rows, v.shape[-1])

    def split(v):
        return [v[k * tokens : (k + 1) * tokens] for k in range(slots)]

    x_slots = [x_own, ring(x_own)]
    gains = all_parts(tie(jnp.stack([norm1_gain, norm2_gain]), x_slots[1]))
    gains = jnp.swapaxes(gains, 0, 1).reshape(2, model).astype(F32)
    gain_one, gain_two = gains[0:1], gains[1:2]
    conv_vec = jnp.concatenate(
        [conv_weight.astype(F32), conv_bias.astype(F32)[None], jnp.zeros((3, chans), F32)], axis=0
    )
    decay = decay_param.astype(F32)
    coef = -DECAY_SCALE * jax.nn.softplus(-decay)
    gate_vec = jnp.concatenate(
        [gate_bias.astype(F32), coef[None], jnp.zeros((5, chans), F32)], axis=0
    )
    extra = window - chans
    offs = jnp.concatenate(
        [
            (offset + HALF * jnp.arange(OWN, dtype=jnp.int32)) // inner * inner,
            jnp.stack(
                [
                    offset,
                    jnp.where(odd, 0, chans),
                    jnp.where(odd, 0, chans - extra),
                    jnp.where(odd, slots - 1, 1),
                ]
            ),
            spot ^ jnp.array(relative_order(count, order_b), jnp.int32),
        ]
    ).astype(jnp.int32)

    groups = gate_weight.shape[2] // 16
    group = spot // 2 % groups
    gate_cols = lax.dynamic_slice_in_dim(tie(gate_weight, x_slots[1]), group * 16, 16, 2)
    gate_cols = jnp.transpose(gate_cols, (0, 2, 1, 3)).reshape(2, 16, slots, chans)
    gate_cols = jnp.moveaxis(gate_cols, 2, 0)
    pieces = []
    for k in range(slots):
        piece = lax.dynamic_index_in_dim(gate_cols, (place + k) % slots, 0, keepdims=False)
        if k:
            piece = lax.ppermute(piece, "wshard", [(i, (i + k) % slots) for i in range(slots)])
        pieces.append(piece)
    pieces = [jnp.stack(pieces)]
    for bit in (2, 4):
        pieces = pieces + [exchange_pair(piece, "seq", bit) for piece in pieces]
    rows = inner // slots * ((place - jnp.arange(slots, dtype=jnp.int32)) % slots)
    rows = jnp.stack([rows + 16 * (group ^ (o >> 1)) for o in (0, 2, 4, 6)]).astype(jnp.int32)
    wg = pl.pallas_call(
        assemble_kernel,
        in_specs=[pl.BlockSpec(memory_space=pltpu.SMEM)]
        + [pl.BlockSpec(memory_space=pltpu.VMEM)] * len(pieces),
        out_specs=pl.BlockSpec(memory_space=pltpu.VMEM),
        out_shape=jax.ShapeDtypeStruct((blocks, inner, 2 * HALF), BF16),
    )(rows, *pieces)
    held = ()
    for k in range(slots):
        if 1 <= k < slots - 1:
            x_slots.append(ring(x_slots[k]))
        held = branch_call(x_slots[k], gain_one, w_x, w_y, held, slots, k)
        if k + 1 < slots:
            x_slots[k + 1], *held = join(x_slots[k + 1], *held)
    normed_one, branch_x, branch_y = held
    g_slots = [g_own, ring(tie(g_own, x_slots[-1]))]
    halo = lax.ppermute(
        branch_x[:, tokens - 8 :], "seq", [(i, i + 1) for i in range(count - 1)]
    ).astype(F32)
    wide = jax.ShapeDtypeStruct((slots, tokens, chans), F32)
    low = jax.ShapeDtypeStruct((slots, tokens, chans), BF16)
    pair = jax.ShapeDtypeStruct((slots, 2, chans), F32)
    own_spec = slot_spec(tokens, chans)
    vec_spec = whole_spec((8, chans))
    conv, conv_low, lend = call(
        conv_kernel,
        slots,
        offs,
        (branch_x, halo, conv_vec),
        [own_spec, slot_spec(8, chans), vec_spec],
        (wide, low, jax.ShapeDtypeStruct((slots, tokens, extra), BF16)),
        (own_spec, own_spec, slot_spec(tokens, extra)),
        [pltpu.VMEM((tokens + 8, chans), F32)],
    )
    lent = exchange_pair(lend, "wshard", 1)
    lent, g_slots[1] = join(lent, g_slots[1])
    g_slots.append(ring(g_slots[1]))
    s_rec, s_in, h_local, a_prod, ends, win = call(
        gates_kernel,
        slots,
        offs,
        (conv_low, lent, conv, wg, gate_vec),
        [own_spec, partner_spec(tokens, extra, slots), own_spec, whole_spec(wg.shape), vec_spec],
        (wide,) * 4 + (pair, jax.ShapeDtypeStruct((slots, tokens, window), BF16)),
        (own_spec,) * 4 + (slot_spec(2, chans), slot_spec(tokens, window)),
    )
    scan = prefix_start(ends)
    for bit in bits:
        scan = prefix_step(scan, bit, False)
        if bit == 1:
            *scan, g_slots[2] = join(*scan, g_slots[2])
            g_slots.append(ring(g_slots[2]))
    carry = scan[1][:, 0]
    state = h_local + a_prod * carry[:, None, :]
    gelu_y = gelu_value(branch_y)
    mixed = flat((gelu_y * state.astype(BF16).astype(F32)).astype(BF16))

    out_part, g_slots[3] = join(dot_nn(mixed, w_out), g_slots[3])
    out_slots = split(out_part)
    sent, total = ring_add(out_slots[1], None)
    g_a, g_b = turned([tie(g_slots[0], sent)] + g_slots[1:], (order_a, order_b))
    total, g_a, g_b = join(total, g_a, g_b)
    sent, total = ring_add(out_slots[2], total)
    one_a, one_b = turned([tie(normed_one, sent)], (order_a, order_b))
    x_all = jnp.concatenate([tie(x_own, sent)] + x_slots[1:], axis=0)
    total, one_a, one_b, x_all = join(total, one_a, one_b, x_all)
    _, total = ring_add(out_slots[3], total)
    residual = x_own.astype(F32) + out_slots[0] + total.astype(F32)
    res_scale = rms_scale(residual)
    res_hat = residual * res_scale

    two = [(res_hat * gain_two).astype(BF16)]
    held, total, sent = (), None, None
    for k in range(slots):
        if k + 1 < slots:
            two.append(ring(two[k]))
        here = two[k] if sent is None else tie(two[k], sent)
        *held, part = ffn_call(
            here, g_slots[k], w_gate, w_up, w_down, held, slots, k, BF16 if k == 1 else F32
        )
        if k == 0:
            part_0 = part
            two[1], part = join(two[1], part)
        else:
            if total is not None:
                total, part = join(total, part)
            sent, total = ring_add(part, total)
    act, grad_gate, grad_up = held

    two_a, two_b = turned([tie(two[0], sent)] + two[1:], (order_a, order_b))
    gate_grad = Halving(two_a, grad_gate, order_a)
    up_grad = Halving(two_b, grad_up, order_b)
    cut = act.shape[1] // 2 // HALF * HALF
    down_a = Halving(g_a, act[:, :cut], order_a)
    down_b = Halving(g_b, act[:, cut:], order_b)
    total, half_gate, half_up = join(total, gate_grad.give(), up_grad.give())
    grad_two = part_0 + total.astype(F32)
    gate_grad.send(half_gate)
    up_grad.send(half_up)

    scaled = grad_two * gain_two
    grad_residual = g_own.astype(F32) + res_scale * (
        scaled - res_hat * jnp.mean(scaled * res_hat, axis=-1, keepdims=True)
    )
    grad_norm2 = jnp.sum(grad_two * res_hat, axis=0)
    proj = [grad_residual.astype(BF16)]
    proj.append(ring(proj[0]))
    proj[1], half_a, half_b, half_gate, half_up = join(
        proj[1],
        down_a.give(proj[0]),
        down_b.give(proj[0]),
        gate_grad.give(proj[0]),
        up_grad.give(proj[0]),
    )
    proj.append(ring(proj[1]))
    gate_grad.send(half_gate)
    up_grad.send(half_up)
    down_a.send(half_a)
    down_b.send(half_b)
    proj[2], mlp_part = join(proj[2], dot_nn(tie(act, proj[1]), w_down))
    down_slots = split(mlp_part)
    proj.append(ring(proj[2]))
    proj[3], half_a, half_b = join(proj[3], down_a.give(proj[2]), down_b.give(proj[2]))
    grad_proj = jnp.concatenate(proj, axis=0)
    _, mlp = ring_add(tie(down_slots[1], proj[3]), None)

    grad_mixed = by_slot(dot_nt(grad_proj, w_out))
    grad_y, c_local, c_prod, back_ends = call(
        back_scan_kernel,
        slots,
        offs,
        (grad_mixed, branch_y, state, s_rec, gate_vec),
        [own_spec] * 4 + [vec_spec],
        (low, wide, wide, pair),
        (own_spec,) * 3 + (slot_spec(2, chans),),
    )
    scan = prefix_start(back_ends)
    for bit in bits:
        scan = prefix_step(scan, bit, True)
        if bit == 1:
            *scan, mlp, gate_grad.held[-1], up_grad.held[-1] = join(
                *scan, mlp, gate_grad.held[-1], up_grad.held[-1]
            )
    scan, half_gate, half_up = join(scan[1], gate_grad.give(), up_grad.give())
    gate_grad.send(half_gate)
    up_grad.send(half_up)
    edges = jnp.stack([carry, scan[:, 0]], axis=1)
    pieces = (2 * inner * blocks, HALF)
    whole_pieces = inner // slots // count % 8 != 0
    if whole_pieces:
        pieces = wg.shape
    near, far, gate_parts, gate_sums = call(
        functools.partial(back_gates_kernel, count=count, planes=slots),
        slots,
        offs,
        (c_local, c_prod, edges, s_rec, s_in, conv, state, win, wg, gate_vec),
        [own_spec] * 2
        + [slot_spec(2, chans)]
        + [own_spec] * 4
        + [slot_spec(tokens, window), whole_spec(wg.shape), vec_spec],
        (
            wide,
            jax.ShapeDtypeStruct((slots, tokens, extra), F32),
            jax.ShapeDtypeStruct(pieces, F32),
            jax.ShapeDtypeStruct((8, chans), F32),
        ),
        (own_spec, slot_spec(tokens, extra), whole_spec(pieces), vec_spec),
        [pltpu.VMEM(wg.shape, F32), pltpu.VMEM((tokens, window), F32)],
    )
    if whole_pieces:
        gate_parts = gate_parts.reshape(blocks, slots, count, -1, 2, HALF)
        gate_parts = jnp.transpose(gate_parts, (2, 1, 4, 0, 3, 5))
        gate_parts = jnp.concatenate(
            [
                lax.dynamic_index_in_dim(gate_parts, spot ^ o, 0, keepdims=False)
                for o in relative_order(count, order_b)
            ]
        ).reshape(-1, HALF)
    got = exchange_pair(far, "wshard", 1)
    (proj_a,) = turned([tie(grad_proj, far)], (order_a,))
    out_grad = Halving(proj_a, mixed, order_a)
    y_grad = Halving(one_b, flat(grad_y), order_b, extra=gate_parts)
    got, half_out, half_y, gate_grad.held[-1], up_grad.held[-1] = join(
        got, out_grad.give(), y_grad.give(far), gate_grad.held[-1], up_grad.held[-1]
    )
    out_grad.send(half_out)
    y_grad.send(half_y)
    lent_rows = jnp.concatenate([got[:, :8], got[:, :8]], axis=0)
    lent_rows = lax.dynamic_slice_in_dim(lent_rows, jnp.where(odd, slots - 1, 1), slots, 0)
    blank = jnp.zeros((slots, 8, chans - extra), F32)
    head = near[:, :8] + jnp.where(
        odd,
        jnp.concatenate([lent_rows, blank], axis=2),
        jnp.concatenate([blank, lent_rows], axis=2),
    )
    after = lax.ppermute(head, "seq", [(i + 1, i) for i in range(count - 1)])
    after, half_y, half_out = join(after, y_grad.give(head), out_grad.give(head))
    y_grad.send(half_y)
    out_grad.send(half_out)
    grad_x, conv_sums = call(
        back_conv_kernel,
        slots,
        offs,
        (near, got, after, branch_x, halo, conv_vec),
        [
            own_spec,
            partner_spec(tokens, extra, slots),
            slot_spec(8, chans),
            own_spec,
            slot_spec(8, chans),
            vec_spec,
        ],
        (low, jax.ShapeDtypeStruct((8, chans), F32)),
        (own_spec, vec_spec),
        [pltpu.VMEM((tokens + 8, chans), F32), pltpu.VMEM((tokens + 8, chans), F32)],
    )
    one_part = dot_nn(flat(grad_x), w_x) + dot_nn(flat(grad_y), w_y)
    one_slots = split(one_part)
    sent, total = ring_add(one_slots[1], None)

    down_a.send(tie(half_a, one_part))
    down_b.send(tie(half_b, one_part))
    x_grad = Halving(one_a, flat(grad_x), order_a)
    total, norm1, half_x, y_grad.held[-1], out_grad.held[-1] = join(
        total,
        norm_grad(tie(x_all, sent), one_part, slots),
        x_grad.give(sent),
        y_grad.held[-1],
        out_grad.held[-1],
    )
    sent, total = ring_add(one_slots[2], total)
    x_grad.send(half_x)
    norms = jnp.concatenate([norm1, grad_norm2[None]], axis=0)
    other = exchange_pair(norms, "wshard", 1)

    total, other, half_x, half_y, half_out, down_a.held[-1], down_b.held[-1] = join(
        total,
        other,
        x_grad.give(sent),
        y_grad.give(sent),
        out_grad.give(sent),
        down_a.held[-1],
        down_b.held[-1],
    )
    sent, total = ring_add(one_slots[3], total)
    x_grad.send(half_x)
    y_grad.send(half_y)
    out_grad.send(half_out)
    norms = norms + other
    other = exchange_pair(norms, "wshard", 2)

    total, other, grad_w_gate, half_a, half_b, y_grad.held[-1], out_grad.held[-1] = join(
        total,
        other,
        *gate_grad.finish(sent),
        down_a.give(sent),
        down_b.give(sent),
        y_grad.held[-1],
        out_grad.held[-1],
    )
    sent, mlp = ring_add(down_slots[2], tie(mlp, total))
    down_a.send(half_a)
    down_b.send(half_b)
    norms = lax.dynamic_slice_in_dim(norms + other, place * chans, chans, 1)
    smalls = jnp.concatenate([norms, gate_sums[:3], conv_sums[:5]], axis=0)
    other = exchange_pair(smalls, "seq", bits[0])
    grad_one = one_slots[0] + total.astype(F32)
    own_f = x_own.astype(F32)
    own_scale = rms_scale(own_f)
    own_hat = own_f * own_scale
    scaled_one = grad_one * gain_one
    grad_input = grad_residual + own_scale * (
        scaled_one - own_hat * jnp.mean(scaled_one * own_hat, axis=-1, keepdims=True)
    )
    grad_w_y, gate_parts = y_grad.finish(sent)
    mlp, other, grad_input, grad_w_y, grad_w_up, gate_parts, x_grad.held[-1] = join(
        mlp, other, grad_input, grad_w_y, *up_grad.finish(sent), gate_parts, x_grad.held[-1]
    )
    sent, mlp = ring_add(down_slots[3], mlp)
    smalls = smalls + other
    for bit in bits[1:]:
        smalls = smalls + exchange_pair(smalls, "seq", bit)

    gate_parts = swap_parts(gate_parts.reshape(slots, -1, HALF).astype(BF16))[None]
    for bit in order_b[::-1]:
        gate_parts = jnp.concatenate([gate_parts, exchange_pair(gate_parts, "seq", bit)], axis=0)
    gate_parts = jnp.stack(
        [
            lax.dynamic_index_in_dim(gate_parts, at, 0, keepdims=False)
            for at in [rank_of(j ^ spot, order_b) for j in range(count)]
        ]
    ).astype(F32)
    gate_parts = gate_parts.reshape(count, slots, 2, blocks, -1, HALF)
    gate_parts = jnp.transpose(gate_parts, (2, 0, 4, 1, 3, 5)).reshape(2, -1, heads, inner)
    grad_gates = jnp.transpose(gate_parts, (0, 2, 1, 3))
    (grad_w_x,) = x_grad.finish(sent)
    (grad_w_out,) = out_grad.finish(sent)
    grad_w_down = jnp.concatenate([*down_a.finish(sent), *down_b.finish(sent)], axis=0)
    block_out = (residual + down_slots[0] + mlp.astype(F32)).astype(BF16)

    return (
        block_out[None],
        grad_input[None],
        grad_w_x,
        grad_w_y,
        grad_w_out,
        grad_w_gate,
        grad_w_up,
        grad_w_down,
        smalls[0],
        smalls[1],
        smalls[5:9],
        smalls[9],
        grad_gates,
        smalls[3:5],
        DECAY_SCALE * jax.nn.sigmoid(-decay) * smalls[2],
    )


def solution(mesh):
    row = P("wshard", None)
    vec = P("wshard")
    tok = P("wshard", "seq", None)
    grad = P("wshard", "seq")
    return jax.shard_map(
        on_device,
        mesh=mesh,
        in_specs=(
            tok,
            tok,
            row,
            row,
            row,
            row,
            row,
            row,
            vec,
            vec,
            P(None, "wshard"),
            vec,
            P(None, None, "wshard", None),
            P(None, "wshard"),
            vec,
        ),
        out_specs=(
            tok,
            tok,
            grad,
            grad,
            grad,
            grad,
            grad,
            grad,
            vec,
            vec,
            P(None, "wshard"),
            vec,
            P(None, None, "wshard", None),
            P(None, "wshard"),
            vec,
        ),
        check_vma=False,
    )
```

time: 939 us -> 618 us (0.66)
  waiting for transfers between devices: 421 us -> 193 us
  Pallas kernels: 30.6 us -> 168 us
  starting transfers between devices: 151 us -> 62.7 us
  local copies, waits for them, and re-layouts: 108 us -> 33.1 us
  matrix products: 155 us -> 96.9 us
  blocking collectives: 18.6 us -> 0 us
  other arithmetic: 41.4 us -> 51 us
    pallas_call x5 -> x19, Pallas kernels: 30.6 us -> 168 us  [the longest x4 83.3 us: ffn_call(): pl.pallas_call(ffn_kernel, grid=(hidden // width,), in_specs=[tok, tok, w...]
    ppermute x28 -> x40, waiting for transfers between devices: 197 us -> 65.7 us  [exchange_pair(): return lax.ppermute(value, axis, [(i, i ^ bit) for i in range(count)])]
    ppermute x49 -> x28, starting transfers between devices: 111 us -> 21.6 us  [the longest x24 15.7 us: ring(): lax.ppermute(value, axis, [(i, (i + 1) % count) for i in range(count)])]
    dot_general x24 -> x0, matrix products: 75.5 us -> none  [part(): lax.dot_general(left, right[:, lo:hi], (((0,), (0,)), ((), ())), preferre...]
    ppermute x49 -> x28, waiting for transfers between devices: 190 us -> 120 us  [the longest x24 120 us: ring(): lax.ppermute(value, axis, [(i, (i + 1) % count) for i in range(count)])]
    dot_general x6 -> x32, matrix products: 34.9 us -> 93.6 us  [dot_nn(): return jnp.dot(a, b, preferred_element_type=F32)]
    dot_general x6 -> x1, matrix products: 44.6 us -> 3.29 us  [dot_nt(): lax.dot_general(a, b, (((1,), (1,)), ((), ())), preferred_element_type=F32)]
    ppermute x6 -> x3, waiting for transfers between devices: 33.9 us -> 3.33 us  [swap_parts(): lax.ppermute(mine, axis, [(i, (i + k) % count) for i in range(count)])]
  transfers between devices with their start and end apart: 87 -> 75, of which waited for: 35 -> 39; matrix products, arithmetic and copies ran while one was open for 24% -> 26% of each run, Pallas kernels for 3% -> 26%
where the time goes in v2:
time: 618 us; the launch traced here: 608 us
  waiting for transfers between devices  193 us (31%)
  Pallas kernels  168 us (27%)
  matrix products  96.9 us (16%)
  starting transfers between devices  62.7 us (10%)
  other arithmetic  51 us (8%)
  local copies, waits for them, and re-layouts  33.1 us (5%)
    ppermute x24, waiting for transfers between devices, ring(): lax.ppermute(value, axis, [(i, (i + 1) % count) for i in range(count)])  120 us
    dot_general x32, matrix products, dot_nn(): return jnp.dot(a, b, preferred_element_type=F32)  93.6 us
    pallas_call x4, Pallas kernels, ffn_call(): pl.pallas_call(ffn_kernel, grid=(hidden // width,), in_specs=[tok, tok, w...  83.3 us
    ppermute x40, waiting for transfers between devices, exchange_pair(): return lax.ppermute(value, axis, [(i, i ^ bit) for i in range(count)])  65.7 us
    pallas_call x5, Pallas kernels, call(): pl.pallas_call(kernel, grid_spec=pltpu.PrefetchScalarGridSpec(num_scalar_...  34.2 us
    ppermute x40, starting transfers between devices, exchange_pair(): return lax.ppermute(value, axis, [(i, i ^ bit) for i in range(count)])  34 us
    pallas_call x4, Pallas kernels, branch_call(): pl.pallas_call(branch_kernel, grid=(1,), in_specs=[whole(x.shape), whole(...  24.4 us
    pallas_call x4, Pallas kernels, turned(): pl.pallas_call(functools.partial(turn_kernel, slots=len(parts)), in_specs...  18.9 us
  transfers between devices with their start and end apart: 75, of which 39 were waited for; matrix products, arithmetic and copies ran while one was open for 26% of the time, Pallas kernels for 26%

profile of v2, /device:TPU:0, one launch (start us, length us, event | category | flops | bytes accessed | tf_op | source)
XLA Modules:
  0.0 607.9 jit_solution(12767975970130863435)
XLA Ops:
  5.1 15.7 %collective-permute-done.x_ref = bf16[128,2560]{1,0:T(8,128)(2,1)} collective-permute-done((bf16[128,2560]{1,0:T(8,128)(2,1)}, bf16[128,2560]{1,0:T(8,128)(2,1)}, u32[]{:S(2)}, u32[]{:S(2)}) %collective-permute-start) | collective-permute-done | bytes 655392 | tf_op jit(solution)/shard_map/ppermute | solution.py:22
  29.3 6.1 %shard_map.334 = (bf16[512,2560]{1,0:T(8,128)(2,1)}, bf16[4,128,640]{2,1,0:T(8,128)(2,1)}, f32[4,128,640]{2,1,0:T(8,128)}) custom-call(bf16[128,2560]{1,0:T(8,128)(2,1)} %bitcast.146, f32[1,2560]{1,0:T(1,128)} %bitcast.182, bf16[640,2560]{1,0:T(8,128)(2,1)} %wx_ref.7, bf16[640,2560]{1,0:T(8,128)(2,1)} %wy_ref.7), custom_call_target="tpu_custom_call" | custom-call | tf_op jit(solution)/shard_map/pallas_call | solution.py:301
  36.0 6.1 %shard_map.335 = (bf16[512,2560]{1,0:T(8,128)(2,1)}, bf16[4,128,640]{2,1,0:T(8,128)(2,1)}, f32[4,128,640]{2,1,0:T(8,128)}) custom-call(bf16[128,2560]{1,0:T(8,128)(2,1)} %collective-permute-done.x_ref, f32[1,2560]{1,0:T(1,128)} %bitcast.183, bf16[640,2560]{1,0:T(8,128)(2,1)} %wx_ref.7, ...), custom_call_target="tpu_custom_call", output_to_operand_aliasing={{0}: (4, {}), {1}: (5, {}), {2}: (6, {})} | custom-call | tf_op jit(solution)/shard_map/pallas_call | solution.py:301
  42.1 9.5 %collective-permute-done.4.x_ref = bf16[128,2560]{1,0:T(8,128)(2,1)} collective-permute-done((bf16[128,2560]{1,0:T(8,128)(2,1)}, bf16[128,2560]{1,0:T(8,128)(2,1)}, u32[]{:S(2)}, u32[]{:S(2)}) %collective-permute-start.4) | collective-permute-done | bytes 655392 | tf_op jit(solution)/shard_map/ppermute | solution.py:22
  55.8 6.1 %shard_map.336 = (bf16[512,2560]{1,0:T(8,128)(2,1)}, bf16[4,128,640]{2,1,0:T(8,128)(2,1)}, f32[4,128,640]{2,1,0:T(8,128)}) custom-call(bf16[128,2560]{1,0:T(8,128)(2,1)} %collective-permute-done.4.x_ref, f32[1,2560]{1,0:T(1,128)} %bitcast.184, bf16[640,2560]{1,0:T(8,128)(2,1)} %wx_ref.7, ...), custom_call_target="tpu_custom_call", output_to_operand_aliasing={{0}: (4, {}), {1}: (5, {}), {2}: (6, {})} | custom-call | tf_op jit(solution)/shard_map/pallas_call | solution.py:301
  61.9 5.1 collective-permute-done.5.x_ref
  68.6 4.4 collective-permute-start.10
  76.1 6.1 %shard_map.337 = (bf16[512,2560]{1,0:T(8,128)(2,1)}, bf16[4,128,640]{2,1,0:T(8,128)(2,1)}, f32[4,128,640]{2,1,0:T(8,128)}) custom-call(bf16[128,2560]{1,0:T(8,128)(2,1)} %collective-permute-done.5.x_ref, f32[1,2560]{1,0:T(1,128)} %bitcast.185, bf16[640,2560]{1,0:T(8,128)(2,1)} %wx_ref.7, ...), custom_call_target="tpu_custom_call", output_to_operand_aliasing={{0}: (4, {}), {1}: (5, {}), {2}: (6, {})} | custom-call | tf_op jit(solution)/shard_map/pallas_call | solution.py:301
  88.6 4.6 shard_map.338
  108.9 8.3 %shard_map.340 = (f32[4,128,640]{2,1,0:T(8,128)}, f32[4,128,640]{2,1,0:T(8,128)}, f32[4,128,640]{2,1,0:T(8,128)}, f32[4,128,640]{2,1,0:T(8,128)}, f32[4,2,640]{2,1,0:T(2,128)}, /*index=5*/bf16[4,128,768]{2,1,0:T(8,128)(2,1)}) custom-call(s32[28]{0:T(128)} %concatenate.54.off_ref, bf16[4,128,640]{2,1,0:T(8,128)(2,1)} %get-tuple-element.216.low_ref, ...), custom_call_target="tpu_custom_call" | custom-call | tf_op jit(solution)/shard_map/pallas_call | solution.py:552
  133.3 8.1 %collective-permute-done.19.refs_3_.g_ref = bf16[128,2560]{1,0:T(8,128)(2,1)S(1)} collective-permute-done((bf16[128,2560]{1,0:T(8,128)(2,1)}, bf16[128,2560]{1,0:T(8,128)(2,1)S(1)}, u32[]{:S(2)}, u32[]{:S(2)}) %collective-permute-start.19) | collective-permute-done | bytes 655392 | tf_op jit(solution)/shard_map/ppermute | solution.py:22
  143.1 5.0 shard_map.341
  148.1 11.0 %collective-permute-done.20 = bf16[128,2560]{1,0:T(8,128)(2,1)} collective-permute-done((bf16[128,2560]{1,0:T(8,128)(2,1)}, bf16[128,2560]{1,0:T(8,128)(2,1)}, u32[]{:S(2)}, u32[]{:S(2)}) %collective-permute-start.20) | collective-permute-done | bytes 655392 | tf_op jit(solution)/shard_map/ppermute | solution.py:22
  161.6 4.9 shard_map.342
  169.4 7.8 %collective-permute-done.21 = bf16[128,2560]{1,0:T(8,128)(2,1)} collective-permute-done((bf16[128,2560]{1,0:T(8,128)(2,1)}, bf16[128,2560]{1,0:T(8,128)(2,1)}, u32[]{:S(2)}, u32[]{:S(2)}) %collective-permute-start.21) | collective-permute-done | bytes 655392 | tf_op jit(solution)/shard_map/ppermute | solution.py:22
  179.7 14.7 %collective-permute-done.22 = bf16[128,2560]{1,0:T(8,128)(2,1)} collective-permute-done((bf16[128,2560]{1,0:T(8,128)(2,1)}, bf16[128,2560]{1,0:T(8,128)(2,1)}, u32[]{:S(2)}, u32[]{:S(2)}) %collective-permute-start.22) | collective-permute-done | bytes 655392 | tf_op jit(solution)/shard_map/ppermute | solution.py:22
  198.7 20.9 %shard_map.343 = (bf16[512,1920]{1,0:T(8,128)(2,1)}, bf16[512,1920]{1,0:T(8,128)(2,1)}, bf16[512,1920]{1,0:T(8,128)(2,1)}, f32[128,2560]{1,0:T(8,128)}) custom-call(bf16[128,2560]{1,0:T(8,128)(2,1)} %multiply_convert_fusion.two_ref.refs_0_, bf16[128,2560]{1,0:T(8,128)(2,1)} %bitcast.151, bf16[1920,2560]{1,0:T(8,128)(2,1)} %wg_ref.7, ...), custom_call_target="tpu_custom_call" | custom-call | tf_op jit(solution)/shard_map/pallas_call | solution.py:526
  219.6 20.7 %shard_map.344 = (bf16[512,1920]{1,0:T(8,128)(2,1)}, bf16[512,1920]{1,0:T(8,128)(2,1)}, bf16[512,1920]{1,0:T(8,128)(2,1)}, bf16[128,2560]{1,0:T(8,128)(2,1)}) custom-call(bf16[128,2560]{1,0:T(8,128)(2,1)} %collective-permute-done.23.two_ref.refs_1_, ...), custom_call_target="tpu_custom_call", output_to_operand_aliasing={{0}: (5, {}), {1}: (6, {}), {2}: (7, {})} | custom-call | tf_op jit(solution)/shard_map/pallas_call | solution.py:526
  241.2 20.9 %shard_map.345 = (bf16[512,1920]{1,0:T(8,128)(2,1)}, bf16[512,1920]{1,0:T(8,128)(2,1)}, bf16[512,1920]{1,0:T(8,128)(2,1)}, f32[128,2560]{1,0:T(8,128)}) custom-call(bf16[128,2560]{1,0:T(8,128)(2,1)} %collective-permute-done.25.two_ref.refs_2_, ...), custom_call_target="tpu_custom_call", output_to_operand_aliasing={{0}: (5, {}), {1}: (6, {}), {2}: (7, {})} | custom-call | tf_op jit(solution)/shard_map/pallas_call | solution.py:526
  262.1 4.3 collective-permute-start.27
  268.9 13.0 %collective-permute-done.27.two_ref.refs_3_ = bf16[128,2560]{1,0:T(8,128)(2,1)} collective-permute-done((bf16[128,2560]{1,0:T(8,128)(2,1)}, bf16[128,2560]{1,0:T(8,128)(2,1)}, u32[]{:S(2)}, u32[]{:S(2)}) %collective-permute-start.27) | collective-permute-done | bytes 655392 | tf_op jit(solution)/shard_map/ppermute | solution.py:22
  281.9 20.9 %shard_map.346 = (bf16[512,1920]{1,0:T(8,128)(2,1)}, bf16[512,1920]{1,0:T(8,128)(2,1)}, bf16[512,1920]{1,0:T(8,128)(2,1)}, f32[128,2560]{1,0:T(8,128)}) custom-call(bf16[128,2560]{1,0:T(8,128)(2,1)} %collective-permute-done.27.two_ref.refs_3_, bf16[128,2560]{1,0:T(8,128)(2,1)} %copy-done.27, ...), custom_call_target="tpu_custom_call", output_to_operand_aliasing={{0}: (5, {}), {1}: (6, {}), {2}: (7, {})} | custom-call | tf_op jit(solution)/shard_map/pallas_call | solution.py:526
  307.7 4.9 shard_map.347
  312.7 5.0 convolution_convert_fusion.1
  317.7 4.5 convolution_convert_fusion
  337.4 4.8 add_convert_fusion.1
  351.1 5.6 fusion.105
  356.6 10.8 %collective-permute-done.32 = bf16[128,2560]{1,0:T(8,128)(2,1)S(1)} collective-permute-done((bf16[128,2560]{1,0:T(8,128)(2,1)S(1)}, bf16[128,2560]{1,0:T(8,128)(2,1)S(1)}, u32[]{:S(2)}, u32[]{:S(2)}) %collective-permute-start.32) | collective-permute-done | bytes 655392 | tf_op jit(solution)/shard_map/ppermute | solution.py:22
  373.7 11.3 %collective-permute-done.33 = bf16[128,2560]{1,0:T(8,128)(2,1)S(1)} collective-permute-done((bf16[128,2560]{1,0:T(8,128)(2,1)S(1)}, bf16[128,2560]{1,0:T(8,128)(2,1)S(1)}, u32[]{:S(2)}, u32[]{:S(2)}) %collective-permute-start.33) | collective-permute-done | bytes 655392 | tf_op jit(solution)/shard_map/ppermute | solution.py:22
  388.7 6.5 %shard_map.348 = (bf16[4,128,640]{2,1,0:T(8,128)(2,1)}, f32[4,128,640]{2,1,0:T(8,128)}, f32[4,128,640]{2,1,0:T(8,128)}, f32[4,2,640]{2,1,0:T(2,128)}) custom-call(s32[28]{0:T(128)} %concatenate.54.off_ref, f32[4,128,640]{2,1,0:T(8,128)} %bitcast.165, f32[4,128,640]{2,1,0:T(8,128)} %get-tuple-element.214.by_ref, f32[4,128,640]{2,1,0:T(8,128)} %get-tuple-element.412.st_ref, ...), custom_call_target="tpu_custom_call" | custom-call | tf_op jit(solution)/shard_map/pallas_call | solution.py:552
  397.6 6.9 %collective-permute-done.38 = bf16[640,1920]{1,0:T(8,128)(2,1)} collective-permute-done((bf16[640,1920]{1,0:T(8,128)(2,1)}, bf16[640,1920]{1,0:T(8,128)(2,1)}, u32[]{:S(2)}, u32[]{:S(2)}) %collective-permute-start.38) | collective-permute-done | bytes 2457632 | tf_op jit(solution)/shard_map/ppermute | solution.py:55
  406.3 4.3 fusion.8
  418.8 9.6 %shard_map.349 = (f32[4,128,640]{2,1,0:T(8,128)}, f32[4,128,128]{2,1,0:T(8,128)}, f32[2560,128]{1,0:T(8,128)}, f32[8,640]{1,0:T(8,128)}) custom-call(s32[28]{0:T(128)} %concatenate.54.off_ref, f32[4,128,640]{2,1,0:T(8,128)} %get-tuple-element.291.c_ref, f32[4,128,640]{2,1,0:T(8,128)} %get-tuple-element.292.a_ref, f32[4,2,640]{2,1,0:T(2,128)} %pad_maximum_fusion.18.edge_ref, ...), custom_call_target="tpu_custom_call" | custom-call | tf_op jit(solution)/shard_map/pallas_call | solution.py:552
  428.5 4.1 shard_map.350
  438.0 5.6 collective-permute-done.43
  444.5 4.5 fusion.107
  458.2 5.2 shard_map.351
  467.0 5.9 convolution_add_fusion.part_ref
  476.2 5.1 shard_map.352
  485.7 8.1 %collective-permute-done.48 = bf16[128,2560]{1,0:T(8,128)(2,1)} collective-permute-done((bf16[128,2560]{1,0:T(8,128)(2,1)}, bf16[128,2560]{1,0:T(8,128)(2,1)}, u32[]{:S(2)}, u32[]{:S(2)}) %collective-permute-start.48) | collective-permute-done | bytes 655392 | tf_op jit(solution)/shard_map/ppermute | solution.py:22
  501.9 8.9 %collective-permute-done.52 = f32[2,2560]{1,0:T(2,128)S(1)} collective-permute-done((f32[2,2560]{1,0:T(2,128)S(1)}, f32[2,2560]{1,0:T(2,128)S(1)}, u32[]{:S(2)}, u32[]{:S(2)}) %collective-permute-start.52) | collective-permute-done | bytes 20512 | tf_op jit(solution)/shard_map/ppermute | solution.py:55
  510.9 6.8 %collective-permute-done.55 = bf16[640,1024]{1,0:T(8,128)(2,1)S(1)} collective-permute-done((bf16[640,1024]{1,0:T(8,128)(2,1)}, bf16[640,1024]{1,0:T(8,128)(2,1)S(1)}, u32[]{:S(2)}, u32[]{:S(2)}) %collective-permute-start.55) | collective-permute-done | bytes 1310752 | tf_op jit(solution)/shard_map/ppermute | solution.py:55
  518.0 3.8 collective-permute-start.57
  524.4 4.6 fusion.7
  532.6 3.8 collective-permute-done.57
  545.3 4.6 fusion.6
  559.2 6.4 %collective-permute-done.66 = bf16[320,1024]{1,0:T(8,128)(2,1)S(1)} collective-permute-done((bf16[320,1024]{1,0:T(8,128)(2,1)S(1)}, bf16[320,1024]{1,0:T(8,128)(2,1)S(1)}, u32[]{:S(2)}, u32[]{:S(2)}) %collective-permute-start.66) | collective-permute-done | bytes 655392 | tf_op jit(solution)/shard_map/ppermute | solution.py:55
  584.6 4.8 collective-permute-done.68
  (442 shorter events, 224.5 us)
Async XLA Ops:
  0.7 20.2 %collective-permute-start = (bf16[128,2560]{1,0:T(8,128)(2,1)}, bf16[128,2560]{1,0:T(8,128)(2,1)}, u32[]{:S(2)}, u32[]{:S(2)}) collective-permute-start(bf16[128,2560]{1,0:T(8,128)(2,1)} %bitcast.145), channel_id=1, source_target_pairs={{0,1},{1,2},{2,3},{3,0},{4,5},{5,6},{6,7},{7,4},{8,9},{9,10},{10,1... | collective-permute-start | bytes 1966088 | tf_op jit(solution)/shard_map/ppermute | solution.py:22
  35.4 16.3 %collective-permute-start.4 = (bf16[128,2560]{1,0:T(8,128)(2,1)}, bf16[128,2560]{1,0:T(8,128)(2,1)}, u32[]{:S(2)}, u32[]{:S(2)}) collective-permute-start(bf16[128,2560]{1,0:T(8,128)(2,1)} %collective-permute-done.x_ref), channel_id=1, source_target_pairs={{0,1},{1,2},{2,3},{3,0},{4,5},{5,6},{6,7},{7,4},{8,9},{9,10},{10,1... | collective-permute-start | bytes 1966088 | tf_op jit(solution)/shard_map/ppermute | solution.py:22
  51.6 15.4 %collective-permute-start.5 = (bf16[128,2560]{1,0:T(8,128)(2,1)}, bf16[128,2560]{1,0:T(8,128)(2,1)}, u32[]{:S(2)}, u32[]{:S(2)}) collective-permute-start(bf16[128,2560]{1,0:T(8,128)(2,1)} %collective-permute-done.4.x_ref), channel_id=1, source_target_pairs={{0,1},{1,2},{2,3},{3,0},{4,5},{5,6},{6,7},{7,4},{8,9},{9,10},{10,1... | collective-permute-start | bytes 1966088 | tf_op jit(solution)/shard_map/ppermute | solution.py:22
  67.0 32.4 %collective-permute-start.8 = (bf16[128,2560]{1,0:T(8,128)(2,1)}, bf16[128,2560]{1,0:T(8,128)(2,1)}, u32[]{:S(2)}, u32[]{:S(2)}) collective-permute-start(bf16[128,2560]{1,0:T(8,128)(2,1)} %bitcast.149), channel_id=1, source_target_pairs={{0,1},{1,2},{2,3},{3,0},{4,5},{5,6},{6,7},{7,4},{8,9},{9,10},{10,1... | collective-permute-start | bytes 1966088 | tf_op jit(solution)/shard_map/ppermute | solution.py:22
  68.6 15.6 %collective-permute-start.9 = (bf16[2,16,640]{2,1,0:T(8,128)(2,1)}, bf16[2,16,640]{2,1,0:T(8,128)(2,1)S(1)}, u32[]{:S(2)}, u32[]{:S(2)}) collective-permute-start(bf16[2,16,640]{2,1,0:T(8,128)(2,1)} %bitcast.137), channel_id=1, source_target_pairs={{0,1},{1,2},{2,3},{3,0},{4,5},{5,6},{6,7},{7,4},{8,9},{9,10},{10,1... | collective-permute-start | bytes 122888 | tf_op jit(solution)/shard_map/ppermute | solution.py:659
  68.6 15.6 %collective-permute-start.10 = (bf16[2,16,640]{2,1,0:T(8,128)(2,1)}, bf16[2,16,640]{2,1,0:T(8,128)(2,1)S(1)}, u32[]{:S(2)}, u32[]{:S(2)}) collective-permute-start(bf16[2,16,640]{2,1,0:T(8,128)(2,1)} %bitcast.136), channel_id=1, source_target_pairs={{0,2},{1,3},{2,0},{3,1},{4,6},{5,7},{6,4},{7,5},{8,10},{9,11},{10,... | collective-permute-start | bytes 122888 | tf_op jit(solution)/shard_map/ppermute | solution.py:659
  99.4 20.1 %collective-permute-start.16 = (bf16[128,2560]{1,0:T(8,128)(2,1)}, bf16[128,2560]{1,0:T(8,128)(2,1)}, u32[]{:S(2)}, u32[]{:S(2)}) collective-permute-start(bf16[128,2560]{1,0:T(8,128)(2,1)} %collective-permute-done.8.refs_1_.g_ref), channel_id=1, source_target_pairs={{0,1},{1,2},{2,3},{3,0},{4,5},{5,6},{6,7},{7,4},{8,9},{9,10},{10,1... | collective-permute-start | bytes 1966088 | tf_op jit(solution)/shard_map/ppermute | solution.py:22
  123.8 17.6 %collective-permute-start.19 = (bf16[128,2560]{1,0:T(8,128)(2,1)}, bf16[128,2560]{1,0:T(8,128)(2,1)S(1)}, u32[]{:S(2)}, u32[]{:S(2)}) collective-permute-start(bf16[128,2560]{1,0:T(8,128)(2,1)} %collective-permute-done.16.refs_2_.g_ref), channel_id=1, source_target_pairs={{0,1},{1,2},{2,3},{3,0},{4,5},{5,6},{6,7},{7,4},{8,9},{9,10},{10,1... | collective-permute-start | bytes 1966088 | tf_op jit(solution)/shard_map/ppermute | solution.py:22
  142.5 16.6 %collective-permute-start.20 = (bf16[128,2560]{1,0:T(8,128)(2,1)}, bf16[128,2560]{1,0:T(8,128)(2,1)}, u32[]{:S(2)}, u32[]{:S(2)}) collective-permute-start(bf16[128,2560]{1,0:T(8,128)(2,1)} %slice.780), channel_id=1, source_target_pairs={{0,1},{1,2},{2,3},{3,0},{4,5},{5,6},{6,7},{7,4},{8,9},{9,10},{10,1... | collective-permute-start | bytes 1966088 | tf_op jit(solution)/shard_map/ppermute | solution.py:22
  161.6 15.7 %collective-permute-start.21 = (bf16[128,2560]{1,0:T(8,128)(2,1)}, bf16[128,2560]{1,0:T(8,128)(2,1)}, u32[]{:S(2)}, u32[]{:S(2)}) collective-permute-start(bf16[128,2560]{1,0:T(8,128)(2,1)} %add_convert_fusion.13), channel_id=1, source_target_pairs={{0,1},{1,2},{2,3},{3,0},{4,5},{5,6},{6,7},{7,4},{8,9},{9,10},{10,1... | collective-permute-start | bytes 1966088 | tf_op jit(solution)/shard_map/ppermute | solution.py:22
  179.7 14.8 %collective-permute-start.22 = (bf16[128,2560]{1,0:T(8,128)(2,1)}, bf16[128,2560]{1,0:T(8,128)(2,1)}, u32[]{:S(2)}, u32[]{:S(2)}) collective-permute-start(bf16[128,2560]{1,0:T(8,128)(2,1)} %add_convert_fusion.12), channel_id=1, source_target_pairs={{0,1},{1,2},{2,3},{3,0},{4,5},{5,6},{6,7},{7,4},{8,9},{9,10},{10,1... | collective-permute-start | bytes 1966088 | tf_op jit(solution)/shard_map/ppermute | solution.py:22
  198.7 20.9 %collective-permute-start.23 = (bf16[128,2560]{1,0:T(8,128)(2,1)}, bf16[128,2560]{1,0:T(8,128)(2,1)}, u32[]{:S(2)}, u32[]{:S(2)}) collective-permute-start(bf16[128,2560]{1,0:T(8,128)(2,1)} %multiply_convert_fusion.two_ref.refs_0_), channel_id=1, source_target_pairs={{0,1},{1,2},{2,3},{3,0},{4,5},{5,6},{6,7},{7,4},{8,9},{9,10},{10,1... | collective-permute-start | bytes 1966088 | tf_op jit(solution)/shard_map/ppermute | solution.py:22
  219.6 21.6 %collective-permute-start.25 = (bf16[128,2560]{1,0:T(8,128)(2,1)}, bf16[128,2560]{1,0:T(8,128)(2,1)}, u32[]{:S(2)}, u32[]{:S(2)}) collective-permute-start(bf16[128,2560]{1,0:T(8,128)(2,1)} %collective-permute-done.23.two_ref.refs_1_), channel_id=1, source_target_pairs={{0,1},{1,2},{2,3},{3,0},{4,5},{5,6},{6,7},{7,4},{8,9},{9,10},{10,1... | collective-permute-start | bytes 1966088 | tf_op jit(solution)/shard_map/ppermute | solution.py:22
  240.3 21.8 %collective-permute-start.24 = (bf16[128,2560]{1,0:T(8,128)(2,1)}, bf16[128,2560]{1,0:T(8,128)(2,1)}, u32[]{:S(2)}, u32[]{:S(2)}) collective-permute-start(bf16[128,2560]{1,0:T(8,128)(2,1)} %get-tuple-element.246), channel_id=1, source_target_pairs={{0,1},{1,2},{2,3},{3,0},{4,5},{5,6},{6,7},{7,4},{8,9},{9,10},{10,1... | collective-permute-start | bytes 1966088 | tf_op jit(solution)/shard_map/ppermute | solution.py:22
  262.1 19.8 %collective-permute-start.27 = (bf16[128,2560]{1,0:T(8,128)(2,1)}, bf16[128,2560]{1,0:T(8,128)(2,1)}, u32[]{:S(2)}, u32[]{:S(2)}) collective-permute-start(bf16[128,2560]{1,0:T(8,128)(2,1)} %collective-permute-done.25.two_ref.refs_2_), channel_id=1, source_target_pairs={{0,1},{1,2},{2,3},{3,0},{4,5},{5,6},{6,7},{7,4},{8,9},{9,10},{10,1... | collective-permute-start | bytes 1966088 | tf_op jit(solution)/shard_map/ppermute | solution.py:22
  268.9 33.9 %collective-permute-start.26 = (bf16[128,2560]{1,0:T(8,128)(2,1)}, bf16[128,2560]{1,0:T(8,128)(2,1)}, u32[]{:S(2)}, u32[]{:S(2)}) collective-permute-start(bf16[128,2560]{1,0:T(8,128)(2,1)} %add_convert_fusion.11), channel_id=1, source_target_pairs={{0,1},{1,2},{2,3},{3,0},{4,5},{5,6},{6,7},{7,4},{8,9},{9,10},{10,1... | collective-permute-start | bytes 1966088 | tf_op jit(solution)/shard_map/ppermute | solution.py:22
  305.3 17.0 %collective-permute-start.28 = (bf16[128,2560]{1,0:T(8,128)(2,1)}, bf16[128,2560]{1,0:T(8,128)(2,1)}, u32[]{:S(2)}, u32[]{:S(2)}) collective-permute-start(bf16[128,2560]{1,0:T(8,128)(2,1)} %add_convert_fusion.10), channel_id=1, source_target_pairs={{0,1},{1,2},{2,3},{3,0},{4,5},{5,6},{6,7},{7,4},{8,9},{9,10},{10,1... | collective-permute-start | bytes 1966088 | tf_op jit(solution)/shard_map/ppermute | solution.py:22
  322.2 15.2 %collective-permute-start.30 = (bf16[1280,1920]{1,0:T(8,128)(2,1)S(1)}, bf16[1280,1920]{1,0:T(8,128)(2,1)S(1)}, u32[]{:S(2)}, u32[]{:S(2)}) collective-permute-start(bf16[1280,1920]{1,0:T(8,128)(2,1)S(1)} %convolution_convert_fusion.1), channel_id=1, source_target_pairs={{0,4},{4,0},{8,12},{12,8},{16,20},{20,16},{24,28},{28,24},{1,5},{5... | collective-permute-start | bytes 14745608 | tf_op jit(solution)/shard_map/ppermute | solution.py:55
  322.2 20.0 %collective-permute-start.31 = (bf16[1280,1920]{1,0:T(8,128)(2,1)}, bf16[1280,1920]{1,0:T(8,128)(2,1)S(1)}, u32[]{:S(2)}, u32[]{:S(2)}) collective-permute-start(bf16[1280,1920]{1,0:T(8,128)(2,1)} %convolution_convert_fusion), channel_id=1, source_target_pairs={{0,4},{4,0},{8,12},{12,8},{16,20},{20,16},{24,28},{28,24},{1,5},{5... | collective-permute-start | bytes 14745608 | tf_op jit(solution)/shard_map/ppermute | solution.py:55
  329.6 18.8 %collective-permute-start.29 = (bf16[128,2560]{1,0:T(8,128)(2,1)S(1)}, bf16[128,2560]{1,0:T(8,128)(2,1)S(1)}, u32[]{:S(2)}, u32[]{:S(2)}) collective-permute-start(bf16[128,2560]{1,0:T(8,128)(2,1)S(1)} %get-tuple-element.407), channel_id=1, source_target_pairs={{0,1},{1,2},{2,3},{3,0},{4,5},{5,6},{6,7},{7,4},{8,9},{9,10},{10,1... | collective-permute-start | bytes 1966088 | tf_op jit(solution)/shard_map/ppermute | solution.py:22
  348.5 21.7 %collective-permute-start.35 = (bf16[1280,1024]{1,0:T(8,128)(2,1)}, bf16[1280,1024]{1,0:T(8,128)(2,1)S(1)}, u32[]{:S(2)}, u32[]{:S(2)}) collective-permute-start(bf16[1280,1024]{1,0:T(8,128)(2,1)} %convolution_convert_fusion.2), channel_id=1, source_target_pairs={{0,4},{4,0},{8,12},{12,8},{16,20},{20,16},{24,28},{28,24},{1,5},{5... | collective-permute-start | bytes 7864328 | tf_op jit(solution)/shard_map/ppermute | solution.py:55
  348.5 19.9 %collective-permute-start.34 = (bf16[1280,896]{1,0:T(8,128)(2,1)}, bf16[1280,896]{1,0:T(8,128)(2,1)S(1)}, u32[]{:S(2)}, u32[]{:S(2)}) collective-permute-start(bf16[1280,896]{1,0:T(8,128)(2,1)} %convolution_convert_fusion.3), channel_id=1, source_target_pairs={{0,4},{4,0},{8,12},{12,8},{16,20},{20,16},{24,28},{28,24},{1,5},{5... | collective-permute-start | bytes 6881288 | tf_op jit(solution)/shard_map/ppermute | solution.py:55
  349.0 18.4 %collective-permute-start.32 = (bf16[128,2560]{1,0:T(8,128)(2,1)S(1)}, bf16[128,2560]{1,0:T(8,128)(2,1)S(1)}, u32[]{:S(2)}, u32[]{:S(2)}) collective-permute-start(bf16[128,2560]{1,0:T(8,128)(2,1)S(1)} %collective-permute-done.29), channel_id=1, source_target_pairs={{0,1},{1,2},{2,3},{3,0},{4,5},{5,6},{6,7},{7,4},{8,9},{9,10},{10,1... | collective-permute-start | bytes 1966088 | tf_op jit(solution)/shard_map/ppermute | solution.py:22
  349.0 55.6 %collective-permute-start.38 = (bf16[640,1920]{1,0:T(8,128)(2,1)}, bf16[640,1920]{1,0:T(8,128)(2,1)}, u32[]{:S(2)}, u32[]{:S(2)}) collective-permute-start(bf16[640,1920]{1,0:T(8,128)(2,1)} %add_convert_fusion.1), channel_id=1, source_target_pairs={{0,8},{4,12},{8,0},{12,4},{16,24},{20,28},{24,16},{28,20},{1,9},{5... | collective-permute-start | bytes 7372808 | tf_op jit(solution)/shard_map/ppermute | solution.py:55
  350.6 55.3 %collective-permute-start.39 = (bf16[640,1920]{1,0:T(8,128)(2,1)}, bf16[640,1920]{1,0:T(8,128)(2,1)}, u32[]{:S(2)}, u32[]{:S(2)}) collective-permute-start(bf16[640,1920]{1,0:T(8,128)(2,1)} %add_convert_fusion), channel_id=1, source_target_pairs={{0,16},{4,20},{8,24},{12,28},{16,0},{20,4},{24,8},{28,12},{1,17},{... | collective-permute-start | bytes 7372808 | tf_op jit(solution)/shard_map/ppermute | solution.py:55
  367.4 17.6 %collective-permute-start.33 = (bf16[128,2560]{1,0:T(8,128)(2,1)S(1)}, bf16[128,2560]{1,0:T(8,128)(2,1)S(1)}, u32[]{:S(2)}, u32[]{:S(2)}) collective-permute-start(bf16[128,2560]{1,0:T(8,128)(2,1)S(1)} %collective-permute-done.32), channel_id=1, source_target_pairs={{0,1},{1,2},{2,3},{3,0},{4,5},{5,6},{6,7},{7,4},{8,9},{9,10},{10,1... | collective-permute-start | bytes 1966088 | tf_op jit(solution)/shard_map/ppermute | solution.py:22
  385.0 20.9 %collective-permute-start.37 = (bf16[128,2560]{1,0:T(8,128)(2,1)}, bf16[128,2560]{1,0:T(8,128)(2,1)}, u32[]{:S(2)}, u32[]{:S(2)}) collective-permute-start(bf16[128,2560]{1,0:T(8,128)(2,1)} %slice.454), channel_id=1, source_target_pairs={{0,1},{1,2},{2,3},{3,0},{4,5},{5,6},{6,7},{7,4},{8,9},{9,10},{10,1... | collective-permute-start | bytes 1966088 | tf_op jit(solution)/shard_map/ppermute | solution.py:22
  416.0 27.6 %collective-permute-start.43 = (bf16[320,1920]{1,0:T(8,128)(2,1)}, bf16[320,1920]{1,0:T(8,128)(2,1)}, u32[]{:S(2)}, u32[]{:S(2)}) collective-permute-start(bf16[320,1920]{1,0:T(8,128)(2,1)} %fusion.8), channel_id=1, source_target_pairs={{0,16},{4,20},{8,24},{12,28},{16,0},{20,4},{24,8},{28,12},{1,17},{... | collective-permute-start | bytes 3686408 | tf_op jit(solution)/shard_map/ppermute | solution.py:55
  416.6 27.4 %collective-permute-start.44 = (bf16[320,1920]{1,0:T(8,128)(2,1)}, bf16[320,1920]{1,0:T(8,128)(2,1)}, u32[]{:S(2)}, u32[]{:S(2)}) collective-permute-start(bf16[320,1920]{1,0:T(8,128)(2,1)} %fusion.9), channel_id=1, source_target_pairs={{0,8},{4,12},{8,0},{12,4},{16,24},{20,28},{24,16},{28,20},{1,9},{5... | collective-permute-start | bytes 3686408 | tf_op jit(solution)/shard_map/ppermute | solution.py:55
  463.4 30.4 %collective-permute-start.50 = (bf16[640,640]{1,0:T(8,128)(2,1)}, bf16[640,640]{1,0:T(8,128)(2,1)}, u32[]{:S(2)}, u32[]{:S(2)}) collective-permute-start(bf16[640,640]{1,0:T(8,128)(2,1)} %add_convert_fusion.5), channel_id=1, source_target_pairs={{0,8},{4,12},{8,0},{12,4},{16,24},{20,28},{24,16},{28,20},{1,9},{5... | collective-permute-start | bytes 2457608 | tf_op jit(solution)/shard_map/ppermute | solution.py:55
  465.7 28.1 %collective-permute-start.49 = (bf16[640,768]{1,0:T(8,128)(2,1)}, bf16[640,768]{1,0:T(8,128)(2,1)}, u32[]{:S(2)}, u32[]{:S(2)}) collective-permute-start(bf16[640,768]{1,0:T(8,128)(2,1)} %pad_maximum_fusion.4), channel_id=1, source_target_pairs={{0,16},{4,20},{8,24},{12,28},{16,0},{20,4},{24,8},{28,12},{1,17},{... | collective-permute-start | bytes 2949128 | tf_op jit(solution)/shard_map/ppermute | solution.py:55
  476.1 17.7 %collective-permute-start.48 = (bf16[128,2560]{1,0:T(8,128)(2,1)}, bf16[128,2560]{1,0:T(8,128)(2,1)}, u32[]{:S(2)}, u32[]{:S(2)}) collective-permute-start(bf16[128,2560]{1,0:T(8,128)(2,1)} %slice.779), channel_id=1, source_target_pairs={{0,1},{1,2},{2,3},{3,0},{4,5},{5,6},{6,7},{7,4},{8,9},{9,10},{10,1... | collective-permute-start | bytes 1966088 | tf_op jit(solution)/shard_map/ppermute | solution.py:22
  481.3 29.5 %collective-permute-start.54 = (bf16[640,896]{1,0:T(8,128)(2,1)}, bf16[640,896]{1,0:T(8,128)(2,1)S(1)}, u32[]{:S(2)}, u32[]{:S(2)}) collective-permute-start(bf16[640,896]{1,0:T(8,128)(2,1)} %add_convert_fusion.3), channel_id=1, source_target_pairs={{0,8},{4,12},{8,0},{12,4},{16,24},{20,28},{24,16},{28,20},{1,9},{5... | collective-permute-start | bytes 3440648 | tf_op jit(solution)/shard_map/ppermute | solution.py:55
  482.9 34.8 %collective-permute-start.55 = (bf16[640,1024]{1,0:T(8,128)(2,1)}, bf16[640,1024]{1,0:T(8,128)(2,1)S(1)}, u32[]{:S(2)}, u32[]{:S(2)}) collective-permute-start(bf16[640,1024]{1,0:T(8,128)(2,1)} %add_convert_fusion.2), channel_id=1, source_target_pairs={{0,16},{4,20},{8,24},{12,28},{16,0},{20,4},{24,8},{28,12},{1,17},{... | collective-permute-start | bytes 3932168 | tf_op jit(solution)/shard_map/ppermute | solution.py:55
  495.4 22.2 %collective-permute-start.51 = (bf16[128,2560]{1,0:T(8,128)(2,1)S(1)}, bf16[128,2560]{1,0:T(8,128)(2,1)S(1)}, u32[]{:S(2)}, u32[]{:S(2)}) collective-permute-start(bf16[128,2560]{1,0:T(8,128)(2,1)S(1)} %fusion.35), channel_id=1, source_target_pairs={{0,1},{1,2},{2,3},{3,0},{4,5},{5,6},{6,7},{7,4},{8,9},{9,10},{10,1... | collective-permute-start | bytes 1966088 | tf_op jit(solution)/shard_map/ppermute | solution.py:22
  495.5 15.3 %collective-permute-start.52 = (f32[2,2560]{1,0:T(2,128)S(1)}, f32[2,2560]{1,0:T(2,128)S(1)}, u32[]{:S(2)}, u32[]{:S(2)}) collective-permute-start(f32[2,2560]{1,0:T(2,128)S(1)} %pad_maximum_fusion.19), channel_id=1, source_target_pairs={{0,1},{1,0},{2,3},{3,2},{4,5},{5,4},{6,7},{7,6},{8,9},{9,8},{10,11... | collective-permute-start | bytes 61448 | tf_op jit(solution)/shard_map/ppermute | solution.py:55
  517.8 18.7 %collective-permute-start.56 = (bf16[128,2560]{1,0:T(8,128)(2,1)S(1)}, bf16[128,2560]{1,0:T(8,128)(2,1)S(1)}, u32[]{:S(2)}, u32[]{:S(2)}) collective-permute-start(bf16[128,2560]{1,0:T(8,128)(2,1)S(1)} %fusion.36), channel_id=1, source_target_pairs={{0,1},{1,2},{2,3},{3,0},{4,5},{5,6},{6,7},{7,4},{8,9},{9,10},{10,1... | collective-permute-start | bytes 1966088 | tf_op jit(solution)/shard_map/ppermute | solution.py:22
  518.0 18.4 %collective-permute-start.57 = (f32[2,2560]{1,0:T(2,128)S(1)}, f32[2,2560]{1,0:T(2,128)S(1)}, u32[]{:S(2)}, u32[]{:S(2)}) collective-permute-start(f32[2,2560]{1,0:T(2,128)S(1)} %fusion.101), channel_id=1, source_target_pairs={{0,2},{1,3},{2,0},{3,1},{4,6},{5,7},{6,4},{7,5},{8,10},{9,11},{10,... | collective-permute-start | bytes 61448 | tf_op jit(solution)/shard_map/ppermute | solution.py:55
  521.8 14.6 %collective-permute-start.59 = (bf16[320,640]{1,0:T(8,128)(2,1)S(1)}, bf16[320,640]{1,0:T(8,128)(2,1)S(1)}, u32[]{:S(2)}, u32[]{:S(2)}) collective-permute-start(bf16[320,640]{1,0:T(8,128)(2,1)S(1)} %add_convert_fusion.14), channel_id=1, source_target_pairs={{0,16},{4,20},{8,24},{12,28},{16,0},{20,4},{24,8},{28,12},{1,17},{... | collective-permute-start | bytes 1228808 | tf_op jit(solution)/shard_map/ppermute | solution.py:55
  522.4 14.2 %collective-permute-start.58 = (bf16[320,768]{1,0:T(8,128)(2,1)S(1)}, bf16[320,768]{1,0:T(8,128)(2,1)S(1)}, u32[]{:S(2)}, u32[]{:S(2)}) collective-permute-start(bf16[320,768]{1,0:T(8,128)(2,1)S(1)} %pad_maximum_fusion.6), channel_id=1, source_target_pairs={{0,8},{4,12},{8,0},{12,4},{16,24},{20,28},{24,16},{28,20},{1,9},{5... | collective-permute-start | bytes 1474568 | tf_op jit(solution)/shard_map/ppermute | solution.py:55
  523.8 30.3 %collective-permute-start.62 = (bf16[640,640]{1,0:T(8,128)(2,1)S(1)}, bf16[640,640]{1,0:T(8,128)(2,1)S(1)}, u32[]{:S(2)}, u32[]{:S(2)}) collective-permute-start(bf16[640,640]{1,0:T(8,128)(2,1)S(1)} %add_convert_fusion.4), channel_id=1, source_target_pairs={{0,8},{4,12},{8,0},{12,4},{16,24},{20,28},{24,16},{28,20},{1,9},{5... | collective-permute-start | bytes 2457608 | tf_op jit(solution)/shard_map/ppermute | solution.py:55
  537.8 18.4 %collective-permute-start.60 = (bf16[128,2560]{1,0:T(8,128)(2,1)S(1)}, bf16[128,2560]{1,0:T(8,128)(2,1)S(1)}, u32[]{:S(2)}, u32[]{:S(2)}) collective-permute-start(bf16[128,2560]{1,0:T(8,128)(2,1)S(1)} %add_convert_fusion.9), channel_id=1, source_target_pairs={{0,1},{1,2},{2,3},{3,0},{4,5},{5,6},{6,7},{7,4},{8,9},{9,10},{10,1... | collective-permute-start | bytes 1966088 | tf_op jit(solution)/shard_map/ppermute | solution.py:22
  539.0 28.6 %collective-permute-start.65 = (bf16[320,896]{1,0:T(8,128)(2,1)S(1)}, bf16[320,896]{1,0:T(8,128)(2,1)S(1)}, u32[]{:S(2)}, u32[]{:S(2)}) collective-permute-start(bf16[320,896]{1,0:T(8,128)(2,1)S(1)} %fusion.21), channel_id=1, source_target_pairs={{0,16},{4,20},{8,24},{12,28},{16,0},{20,4},{24,8},{28,12},{1,17},{... | collective-permute-start | bytes 1720328 | tf_op jit(solution)/shard_map/ppermute | solution.py:55
  540.5 25.1 %collective-permute-start.66 = (bf16[320,1024]{1,0:T(8,128)(2,1)S(1)}, bf16[320,1024]{1,0:T(8,128)(2,1)S(1)}, u32[]{:S(2)}, u32[]{:S(2)}) collective-permute-start(bf16[320,1024]{1,0:T(8,128)(2,1)S(1)} %fusion.20), channel_id=1, source_target_pairs={{0,8},{4,12},{8,0},{12,4},{16,24},{20,28},{24,16},{28,20},{1,9},{5... | collective-permute-start | bytes 1966088 | tf_op jit(solution)/shard_map/ppermute | solution.py:55
  557.1 47.7 %collective-permute-start.63 = (bf16[128,2560]{1,0:T(8,128)(2,1)}, bf16[128,2560]{1,0:T(8,128)(2,1)}, u32[]{:S(2)}, u32[]{:S(2)}) collective-permute-start(bf16[128,2560]{1,0:T(8,128)(2,1)} %add_convert_fusion.8), channel_id=1, source_target_pairs={{0,1},{1,2},{2,3},{3,0},{4,5},{5,6},{6,7},{7,4},{8,9},{9,10},{10,1... | collective-permute-start | bytes 1966088 | tf_op jit(solution)/shard_map/ppermute | solution.py:22
  557.4 21.4 %collective-permute-start.67 = (f32[10,640]{1,0:T(8,128)S(1)}, f32[10,640]{1,0:T(8,128)S(1)}, u32[]{:S(2)}, u32[]{:S(2)}) collective-permute-start(f32[10,640]{1,0:T(8,128)S(1)} %fusion.100), channel_id=1, source_target_pairs={{0,8},{4,12},{8,0},{12,4},{16,24},{20,28},{24,16},{28,20},{1,9},{5... | collective-permute-start | bytes 76808 | tf_op jit(solution)/shard_map/ppermute | solution.py:55
  557.8 18.7 %collective-permute-start.71 = (bf16[80,128]{1,0:T(8,128)(2,1)S(1)}, bf16[80,128]{1,0:T(8,128)(2,1)S(1)}, u32[]{:S(2)}, u32[]{:S(2)}) collective-permute-start(bf16[80,128]{1,0:T(8,128)(2,1)S(1)} %get-tuple-element.426), channel_id=1, source_target_pairs={{0,1},{1,2},{2,3},{3,0},{4,5},{5,6},{6,7},{7,4},{8,9},{9,10},{10,1... | collective-permute-start | bytes 61448 | tf_op jit(solution)/shard_map/ppermute | solution.py:91
  576.2 17.7 %collective-permute-start.64 = (bf16[320,640]{1,0:T(8,128)(2,1)S(1)}, bf16[320,640]{1,0:T(8,128)(2,1)S(1)}, u32[]{:S(2)}, u32[]{:S(2)}) collective-permute-start(bf16[320,640]{1,0:T(8,128)(2,1)S(1)} %fusion.52), channel_id=1, source_target_pairs={{0,16},{4,20},{8,24},{12,28},{16,0},{20,4},{24,8},{28,12},{1,17},{... | collective-permute-start | bytes 1228808 | tf_op jit(solution)/shard_map/ppermute | solution.py:55
  (100 other events, 1001.5 us)

commit v3 on v2

--- a/solution.py
+++ b/solution.py
@@ -441,7 +441,7 @@
     own = pl.multiple_of(off_ref[OWN], HALF)
     far = pl.multiple_of(off_ref[FAR], HALF)
     near_ref[0] = gc_ref[:, pl.ds(own, near_ref.shape[2])]
-    far_ref[0] = gc_ref[:, pl.ds(far, far_ref.shape[2])]
+    far_ref[0] = gc_ref[:, pl.ds(far, far_ref.shape[2])].astype(BF16)
 
     @pl.when(pl.program_id(0) == pl.num_programs(0) - 1)
     def _():
@@ -473,7 +473,7 @@
 
     lend = pl.multiple_of(off_ref[LEND], HALF)
     g_ext[0:tokens] = gc_ref[0]
-    g_ext[0:tokens, pl.ds(lend, got_ref.shape[2])] += got_ref[0]
+    g_ext[0:tokens, pl.ds(lend, got_ref.shape[2])] += got_ref[0].astype(F32)
     grad = g_ext[0:tokens]
     g_ext[tokens:] = after_ref[0]
     x_ext[0:8] = halo_ref[0]
@@ -533,6 +533,23 @@
         scratch_shapes=[pltpu.VMEM((rows, model), F32)],
         input_output_aliases={5 + i: i for i in range(len(held))},
     )(two, grad, w_gate, w_up, w_down, *held)
+
+
+def gate_out_kernel(off_ref, in_ref, out_ref):
+    count, planes, rows = in_ref.shape[:3]
+    per = out_ref.shape[3] // HALF
+    blocks = out_ref.shape[1] * per // planes
+    width = rows // (2 * blocks)
+    for r in range(count):
+        row = pl.multiple_of(off_ref[REL + r] * width, width)
+        for j in range(planes):
+            values = in_ref[r, j].astype(F32)
+            for g in range(2):
+                for m in range(blocks):
+                    at = blocks * j + m
+                    first = (g * blocks + m) * width
+                    cols = slice(at % per * HALF, (at % per + 1) * HALF)
+                    out_ref[g, at // per, pl.ds(row, width), cols] = values[first : first + width]
 
 
 def slot_spec(rows, width):
@@ -649,33 +666,41 @@
 
     groups = gate_weight.shape[2] // 16
     group = spot // 2 % groups
-    gate_cols = lax.dynamic_slice_in_dim(tie(gate_weight, x_slots[1]), group * 16, 16, 2)
-    gate_cols = jnp.transpose(gate_cols, (0, 2, 1, 3)).reshape(2, 16, slots, chans)
-    gate_cols = jnp.moveaxis(gate_cols, 2, 0)
-    pieces = []
-    for k in range(slots):
-        piece = lax.dynamic_index_in_dim(gate_cols, (place + k) % slots, 0, keepdims=False)
-        if k:
-            piece = lax.ppermute(piece, "wshard", [(i, (i + k) % slots) for i in range(slots)])
-        pieces.append(piece)
-    pieces = [jnp.stack(pieces)]
-    for bit in (2, 4):
-        pieces = pieces + [exchange_pair(piece, "seq", bit) for piece in pieces]
-    rows = inner // slots * ((place - jnp.arange(slots, dtype=jnp.int32)) % slots)
-    rows = jnp.stack([rows + 16 * (group ^ (o >> 1)) for o in (0, 2, 4, 6)]).astype(jnp.int32)
-    wg = pl.pallas_call(
-        assemble_kernel,
-        in_specs=[pl.BlockSpec(memory_space=pltpu.SMEM)]
-        + [pl.BlockSpec(memory_space=pltpu.VMEM)] * len(pieces),
-        out_specs=pl.BlockSpec(memory_space=pltpu.VMEM),
-        out_shape=jax.ShapeDtypeStruct((blocks, inner, 2 * HALF), BF16),
-    )(rows, *pieces)
+
+    def fetch(after):
+        gate_cols = lax.dynamic_slice_in_dim(tie(gate_weight, after), group * 16, 16, 2)
+        gate_cols = jnp.transpose(gate_cols, (0, 2, 1, 3)).reshape(2, 16, slots, chans)
+        gate_cols = jnp.moveaxis(gate_cols, 2, 0)
+        pieces = []
+        for k in range(slots):
+            piece = lax.dynamic_index_in_dim(gate_cols, (place + k) % slots, 0, keepdims=False)
+            if k:
+                piece = lax.ppermute(piece, "wshard", [(i, (i + k) % slots) for i in range(slots)])
+            pieces.append(piece)
+        return pieces
+
+    def assemble(pieces):
+        pieces = [jnp.stack(pieces)]
+        for bit in (2, 4):
+            pieces = pieces + [exchange_pair(piece, "seq", bit) for piece in pieces]
+        rows = inner // slots * ((place - jnp.arange(slots, dtype=jnp.int32)) % slots)
+        rows = jnp.stack([rows + 16 * (group ^ (o >> 1)) for o in (0, 2, 4, 6)]).astype(jnp.int32)
+        return pl.pallas_call(
+            assemble_kernel,
+            in_specs=[pl.BlockSpec(memory_space=pltpu.SMEM)]
+            + [pl.BlockSpec(memory_space=pltpu.VMEM)] * len(pieces),
+            out_specs=pl.BlockSpec(memory_space=pltpu.VMEM),
+            out_shape=jax.ShapeDtypeStruct((blocks, inner, 2 * HALF), BF16),
+        )(rows, *pieces)
+
     held = ()
     for k in range(slots):
         if 1 <= k < slots - 1:
             x_slots.append(ring(x_slots[k]))
+        if k == slots - 2:
+            pieces = fetch(x_slots[k])
         held = branch_call(x_slots[k], gain_one, w_x, w_y, held, slots, k)
-        if k + 1 < slots:
+        if 1 <= k < slots - 1:
             x_slots[k + 1], *held = join(x_slots[k + 1], *held)
     normed_one, branch_x, branch_y = held
     g_slots = [g_own, ring(tie(g_own, x_slots[-1]))]
@@ -697,8 +722,10 @@
         (own_spec, own_spec, slot_spec(tokens, extra)),
         [pltpu.VMEM((tokens + 8, chans), F32)],
     )
+    lend, *pieces = join(lend, *pieces)
+    wg = assemble(pieces)
     lent = exchange_pair(lend, "wshard", 1)
-    lent, g_slots[1] = join(lent, g_slots[1])
+    lent, g_slots[1], wg = join(lent, g_slots[1], wg)
     g_slots.append(ring(g_slots[1]))
     s_rec, s_in, h_local, a_prod, ends, win = call(
         gates_kernel,
@@ -720,15 +747,14 @@
     gelu_y = gelu_value(branch_y)
     mixed = flat((gelu_y * state.astype(BF16).astype(F32)).astype(BF16))
 
-    out_part, g_slots[3] = join(dot_nn(mixed, w_out), g_slots[3])
-    out_slots = split(out_part)
+    out_slots = split(dot_nn(mixed, w_out))
     sent, total = ring_add(out_slots[1], None)
+    one_a, one_b = turned([tie(normed_one, sent)], (order_a, order_b))
+    x_all = jnp.concatenate([tie(x_own, sent)] + x_slots[1:], axis=0)
+    total, one_a, one_b, x_all, g_slots[3] = join(total, one_a, one_b, x_all, g_slots[3])
+    sent, total = ring_add(out_slots[2], total)
     g_a, g_b = turned([tie(g_slots[0], sent)] + g_slots[1:], (order_a, order_b))
     total, g_a, g_b = join(total, g_a, g_b)
-    sent, total = ring_add(out_slots[2], total)
-    one_a, one_b = turned([tie(normed_one, sent)], (order_a, order_b))
-    x_all = jnp.concatenate([tie(x_own, sent)] + x_slots[1:], axis=0)
-    total, one_a, one_b, x_all = join(total, one_a, one_b, x_all)
     _, total = ring_add(out_slots[3], total)
     residual = x_own.astype(F32) + out_slots[0] + total.astype(F32)
     res_scale = rms_scale(residual)
@@ -749,6 +775,8 @@
         else:
             if total is not None:
                 total, part = join(total, part)
+            if k + 1 < slots:
+                two[k + 1], part = join(two[k + 1], part)
             sent, total = ring_add(part, total)
     act, grad_gate, grad_up = held
 
@@ -825,7 +853,7 @@
         + [slot_spec(tokens, window), whole_spec(wg.shape), vec_spec],
         (
             wide,
-            jax.ShapeDtypeStruct((slots, tokens, extra), F32),
+            jax.ShapeDtypeStruct((slots, tokens, extra), BF16),
             jax.ShapeDtypeStruct(pieces, F32),
             jax.ShapeDtypeStruct((8, chans), F32),
         ),
@@ -850,7 +878,7 @@
     )
     out_grad.send(half_out)
     y_grad.send(half_y)
-    lent_rows = jnp.concatenate([got[:, :8], got[:, :8]], axis=0)
+    lent_rows = jnp.concatenate([got[:, :8], got[:, :8]], axis=0).astype(F32)
     lent_rows = lax.dynamic_slice_in_dim(lent_rows, jnp.where(odd, slots - 1, 1), slots, 0)
     blank = jnp.zeros((slots, 8, chans - extra), F32)
     head = near[:, :8] + jnp.where(
@@ -898,14 +926,8 @@
     norms = jnp.concatenate([norm1, grad_norm2[None]], axis=0)
     other = exchange_pair(norms, "wshard", 1)
 
-    total, other, half_x, half_y, half_out, down_a.held[-1], down_b.held[-1] = join(
-        total,
-        other,
-        x_grad.give(sent),
-        y_grad.give(sent),
-        out_grad.give(sent),
-        down_a.held[-1],
-        down_b.held[-1],
+    total, other, half_x, half_y, half_out = join(
+        total, other, x_grad.give(sent), y_grad.give(sent), out_grad.give(sent)
     )
     sent, total = ring_add(one_slots[3], total)
     x_grad.send(half_x)
@@ -914,18 +936,18 @@
     norms = norms + other
     other = exchange_pair(norms, "wshard", 2)
 
-    total, other, grad_w_gate, half_a, half_b, y_grad.held[-1], out_grad.held[-1] = join(
+    total, other, grad_w_gate, *held = join(
         total,
         other,
         *gate_grad.finish(sent),
-        down_a.give(sent),
-        down_b.give(sent),
         y_grad.held[-1],
         out_grad.held[-1],
-    )
+        down_a.held[-1],
+        down_b.held[-1],
+    )
+    for w, piece in zip((y_grad, out_grad, down_a, down_b), held):
+        w.held[-1] = piece
     sent, mlp = ring_add(down_slots[2], tie(mlp, total))
-    down_a.send(half_a)
-    down_b.send(half_b)
     norms = lax.dynamic_slice_in_dim(norms + other, place * chans, chans, 1)
     smalls = jnp.concatenate([norms, gate_sums[:3], conv_sums[:5]], axis=0)
     other = exchange_pair(smalls, "seq", bits[0])
@@ -938,26 +960,48 @@
         scaled_one - own_hat * jnp.mean(scaled_one * own_hat, axis=-1, keepdims=True)
     )
     grad_w_y, gate_parts = y_grad.finish(sent)
-    mlp, other, grad_input, grad_w_y, grad_w_up, gate_parts, x_grad.held[-1] = join(
-        mlp, other, grad_input, grad_w_y, *up_grad.finish(sent), gate_parts, x_grad.held[-1]
-    )
+    mlp, other, grad_input, grad_w_y, half_a, half_b, gate_parts, x_grad.held[-1] = join(
+        mlp,
+        other,
+        grad_input,
+        grad_w_y,
+        down_a.give(sent),
+        down_b.give(sent),
+        gate_parts,
+        x_grad.held[-1],
+    )
+    down_a.send(half_a)
+    down_b.send(half_b)
+    gate_parts = swap_parts(gate_parts.reshape(slots, -1, HALF).astype(BF16))[None]
+    gate_parts, mlp = join(gate_parts, mlp)
     sent, mlp = ring_add(down_slots[3], mlp)
+    (grad_w_up,) = up_grad.finish(sent)
     smalls = smalls + other
     for bit in bits[1:]:
         smalls = smalls + exchange_pair(smalls, "seq", bit)
 
-    gate_parts = swap_parts(gate_parts.reshape(slots, -1, HALF).astype(BF16))[None]
     for bit in order_b[::-1]:
         gate_parts = jnp.concatenate([gate_parts, exchange_pair(gate_parts, "seq", bit)], axis=0)
-    gate_parts = jnp.stack(
-        [
-            lax.dynamic_index_in_dim(gate_parts, at, 0, keepdims=False)
-            for at in [rank_of(j ^ spot, order_b) for j in range(count)]
-        ]
-    ).astype(F32)
-    gate_parts = gate_parts.reshape(count, slots, 2, blocks, -1, HALF)
-    gate_parts = jnp.transpose(gate_parts, (2, 0, 4, 1, 3, 5)).reshape(2, -1, heads, inner)
-    grad_gates = jnp.transpose(gate_parts, (0, 2, 1, 3))
+    if whole_pieces:
+        gate_parts = jnp.stack(
+            [
+                lax.dynamic_index_in_dim(gate_parts, at, 0, keepdims=False)
+                for at in [rank_of(j ^ spot, order_b) for j in range(count)]
+            ]
+        ).astype(F32)
+        gate_parts = gate_parts.reshape(count, slots, 2, blocks, -1, HALF)
+        gate_parts = jnp.transpose(gate_parts, (2, 0, 4, 1, 3, 5)).reshape(2, -1, heads, inner)
+        grad_gates = jnp.transpose(gate_parts, (0, 2, 1, 3))
+    else:
+        grad_gates = pl.pallas_call(
+            gate_out_kernel,
+            in_specs=[
+                pl.BlockSpec(memory_space=pltpu.SMEM),
+                pl.BlockSpec(memory_space=pltpu.VMEM),
+            ],
+            out_specs=pl.BlockSpec(memory_space=pltpu.VMEM),
+            out_shape=jax.ShapeDtypeStruct((2, heads, inner // slots, inner), F32),
+        )(offs, gate_parts)
     (grad_w_x,) = x_grad.finish(sent)
     (grad_w_out,) = out_grad.finish(sent)
     grad_w_down = jnp.concatenate([*down_a.finish(sent), *down_b.finish(sent)], axis=0)

time: 618 us -> 593 us (0.960)
  waiting for transfers between devices: 193 us -> 160 us
  other arithmetic: 51 us -> 61.2 us
    ppermute x24, waiting for transfers between devices: 120 us -> 99.8 us  [ring(): lax.ppermute(value, axis, [(i, (i + 1) % count) for i in range(count)])]
    ppermute x40, waiting for transfers between devices: 65.7 us -> 56.4 us  [exchange_pair(): return lax.ppermute(value, axis, [(i, i ^ bit) for i in range(count)])]
    transpose x1 -> x3, other arithmetic: 2.06 us -> 9.94 us  [finish(): return (total.T,) if more is None else (total.T, more)]
    unnamed x173 -> x155, local copies, waits for them, and re-layouts: 14 us -> 13 us
  transfers between devices with their start and end apart: 75 -> 75, of which waited for: 39 -> 32; matrix products, arithmetic and copies ran while one was open for 26% -> 27% of each run, Pallas kernels for 26% -> 28%
where the time goes in v3:
time: 593 us; the launch traced here: 583 us
  Pallas kernels  170 us (29%)
  waiting for transfers between devices  160 us (27%)
  matrix products  94.3 us (16%)
  starting transfers between devices  67.2 us (11%)
  other arithmetic  61.2 us (10%)
  local copies, waits for them, and re-layouts  27 us (5%)
    ppermute x24, waiting for transfers between devices, ring(): lax.ppermute(value, axis, [(i, (i + 1) % count) for i in range(count)])  99.8 us
    dot_general x32, matrix products, dot_nn(): return jnp.dot(a, b, preferred_element_type=F32)  91 us
    pallas_call x4, Pallas kernels, ffn_call(): pl.pallas_call(ffn_kernel, grid=(hidden // width,), in_specs=[tok, tok, w...  83.3 us
    ppermute x40, waiting for transfers between devices, exchange_pair(): return lax.ppermute(value, axis, [(i, i ^ bit) for i in range(count)])  56.4 us
    pallas_call x5, Pallas kernels, call(): pl.pallas_call(kernel, grid_spec=pltpu.PrefetchScalarGridSpec(num_scalar_...  34.2 us
    ppermute x40, starting transfers between devices, exchange_pair(): return lax.ppermute(value, axis, [(i, i ^ bit) for i in range(count)])  32.8 us
    pallas_call x4, Pallas kernels, branch_call(): pl.pallas_call(branch_kernel, grid=(1,), in_specs=[whole(x.shape), whole(...  24.4 us
    ppermute x24, starting transfers between devices, ring(): lax.ppermute(value, axis, [(i, (i + 1) % count) for i in range(count)])  20.7 us
  transfers between devices with their start and end apart: 75, of which 32 were waited for; matrix products, arithmetic and copies ran while one was open for 27% of the time, Pallas kernels for 28%

profile of v3, /device:TPU:0, one launch (start us, length us, event | category | flops | bytes accessed | tf_op | source)
XLA Modules:
  0.0 582.8 jit_solution(13889904535111233865)
XLA Ops:
  5.1 15.7 %collective-permute-done.x_ref = bf16[128,2560]{1,0:T(8,128)(2,1)} collective-permute-done((bf16[128,2560]{1,0:T(8,128)(2,1)}, bf16[128,2560]{1,0:T(8,128)(2,1)}, u32[]{:S(2)}, u32[]{:S(2)}) %collective-permute-start) | collective-permute-done | bytes 655392 | tf_op jit(solution)/shard_map/ppermute | solution.py:22
  25.0 3.4 collective-permute-start.1
  30.2 6.1 %shard_map.334 = (bf16[512,2560]{1,0:T(8,128)(2,1)}, bf16[4,128,640]{2,1,0:T(8,128)(2,1)}, f32[4,128,640]{2,1,0:T(8,128)}) custom-call(bf16[128,2560]{1,0:T(8,128)(2,1)} %bitcast.136, f32[1,2560]{1,0:T(1,128)} %bitcast.163, bf16[640,2560]{1,0:T(8,128)(2,1)} %wx_ref.7, bf16[640,2560]{1,0:T(8,128)(2,1)} %wy_ref.7), custom_call_target="tpu_custom_call" | custom-call | tf_op jit(solution)/shard_map/pallas_call | solution.py:301
  36.3 6.1 %shard_map.335 = (bf16[512,2560]{1,0:T(8,128)(2,1)}, bf16[4,128,640]{2,1,0:T(8,128)(2,1)}, f32[4,128,640]{2,1,0:T(8,128)}) custom-call(bf16[128,2560]{1,0:T(8,128)(2,1)} %collective-permute-done.x_ref, f32[1,2560]{1,0:T(1,128)} %bitcast.164, bf16[640,2560]{1,0:T(8,128)(2,1)} %wx_ref.7, ...), custom_call_target="tpu_custom_call", output_to_operand_aliasing={{0}: (4, {}), {1}: (5, {}), {2}: (6, {})} | custom-call | tf_op jit(solution)/shard_map/pallas_call | solution.py:301
  55.1 6.1 %shard_map.336 = (bf16[512,2560]{1,0:T(8,128)(2,1)}, bf16[4,128,640]{2,1,0:T(8,128)(2,1)}, f32[4,128,640]{2,1,0:T(8,128)}) custom-call(bf16[128,2560]{1,0:T(8,128)(2,1)} %collective-permute-done.1.x_ref, f32[1,2560]{1,0:T(1,128)} %bitcast.165, bf16[640,2560]{1,0:T(8,128)(2,1)} %wx_ref.7, ...), custom_call_target="tpu_custom_call", output_to_operand_aliasing={{0}: (4, {}), {1}: (5, {}), {2}: (6, {})} | custom-call | tf_op jit(solution)/shard_map/pallas_call | solution.py:301
  61.2 6.1 %shard_map.337 = (bf16[512,2560]{1,0:T(8,128)(2,1)}, bf16[4,128,640]{2,1,0:T(8,128)(2,1)}, f32[4,128,640]{2,1,0:T(8,128)}) custom-call(bf16[128,2560]{1,0:T(8,128)(2,1)} %collective-permute-done.5.x_ref, f32[1,2560]{1,0:T(1,128)} %bitcast.166, bf16[640,2560]{1,0:T(8,128)(2,1)} %wx_ref.7, ...), custom_call_target="tpu_custom_call", output_to_operand_aliasing={{0}: (4, {}), {1}: (5, {}), {2}: (6, {})} | custom-call | tf_op jit(solution)/shard_map/pallas_call | solution.py:301
  73.9 4.6 shard_map.338
  84.3 3.4 collective-permute-done.12.refs_1_
  90.9 3.5 collective-permute-done.14.refs_3_
  97.8 8.3 %shard_map.340 = (f32[4,128,640]{2,1,0:T(8,128)}, f32[4,128,640]{2,1,0:T(8,128)}, f32[4,128,640]{2,1,0:T(8,128)}, f32[4,128,640]{2,1,0:T(8,128)}, f32[4,2,640]{2,1,0:T(2,128)}, /*index=5*/bf16[4,128,768]{2,1,0:T(8,128)(2,1)}) custom-call(s32[28]{0:T(128)} %concatenate.53.off_ref, bf16[4,128,640]{2,1,0:T(8,128)(2,1)} %get-tuple-element.218.low_ref, ...), custom_call_target="tpu_custom_call" | custom-call | tf_op jit(solution)/shard_map/pallas_call | solution.py:569
  108.4 6.4 %collective-permute-done.16.refs_2_.g_ref = bf16[128,2560]{1,0:T(8,128)(2,1)} collective-permute-done((bf16[128,2560]{1,0:T(8,128)(2,1)}, bf16[128,2560]{1,0:T(8,128)(2,1)}, u32[]{:S(2)}, u32[]{:S(2)}) %collective-permute-start.16) | collective-permute-done | bytes 655392 | tf_op jit(solution)/shard_map/ppermute | solution.py:22
  122.5 3.7 fusion.23
  132.3 4.9 shard_map.341
  140.2 10.7 %collective-permute-done.19 = bf16[128,2560]{1,0:T(8,128)(2,1)} collective-permute-done((bf16[128,2560]{1,0:T(8,128)(2,1)}, bf16[128,2560]{1,0:T(8,128)(2,1)}, u32[]{:S(2)}, u32[]{:S(2)}) %collective-permute-start.19) | collective-permute-done | bytes 655392 | tf_op jit(solution)/shard_map/ppermute | solution.py:22
  153.3 4.9 shard_map.342
  158.2 10.6 %collective-permute-done.21 = bf16[128,2560]{1,0:T(8,128)(2,1)} collective-permute-done((bf16[128,2560]{1,0:T(8,128)(2,1)}, bf16[128,2560]{1,0:T(8,128)(2,1)}, u32[]{:S(2)}, u32[]{:S(2)}) %collective-permute-start.21) | collective-permute-done | bytes 655392 | tf_op jit(solution)/shard_map/ppermute | solution.py:22
  171.3 14.6 %collective-permute-done.22 = bf16[128,2560]{1,0:T(8,128)(2,1)} collective-permute-done((bf16[128,2560]{1,0:T(8,128)(2,1)}, bf16[128,2560]{1,0:T(8,128)(2,1)}, u32[]{:S(2)}, u32[]{:S(2)}) %collective-permute-start.22) | collective-permute-done | bytes 655392 | tf_op jit(solution)/shard_map/ppermute | solution.py:22
  190.0 20.9 %shard_map.343 = (bf16[512,1920]{1,0:T(8,128)(2,1)}, bf16[512,1920]{1,0:T(8,128)(2,1)}, bf16[512,1920]{1,0:T(8,128)(2,1)}, f32[128,2560]{1,0:T(8,128)}) custom-call(bf16[128,2560]{1,0:T(8,128)(2,1)} %multiply_convert_fusion.two_ref.refs_0_, bf16[128,2560]{1,0:T(8,128)(2,1)} %bitcast.140, bf16[1920,2560]{1,0:T(8,128)(2,1)} %wg_ref.7, ...), custom_call_target="tpu_custom_call" | custom-call | tf_op jit(solution)/shard_map/pallas_call | solution.py:526
  211.0 20.7 %shard_map.344 = (bf16[512,1920]{1,0:T(8,128)(2,1)}, bf16[512,1920]{1,0:T(8,128)(2,1)}, bf16[512,1920]{1,0:T(8,128)(2,1)}, bf16[128,2560]{1,0:T(8,128)(2,1)}) custom-call(bf16[128,2560]{1,0:T(8,128)(2,1)} %collective-permute-done.23.two_ref.refs_1_, ...), custom_call_target="tpu_custom_call", output_to_operand_aliasing={{0}: (5, {}), {1}: (6, {}), {2}: (7, {})} | custom-call | tf_op jit(solution)/shard_map/pallas_call | solution.py:526
  232.3 4.7 collective-permute-start.25
  237.0 20.9 %shard_map.345 = (bf16[512,1920]{1,0:T(8,128)(2,1)}, bf16[512,1920]{1,0:T(8,128)(2,1)}, bf16[512,1920]{1,0:T(8,128)(2,1)}, f32[128,2560]{1,0:T(8,128)}) custom-call(bf16[128,2560]{1,0:T(8,128)(2,1)} %collective-permute-done.24.two_ref.refs_2_, ...), custom_call_target="tpu_custom_call", output_to_operand_aliasing={{0}: (5, {}), {1}: (6, {}), {2}: (7, {})} | custom-call | tf_op jit(solution)/shard_map/pallas_call | solution.py:526
  263.1 20.9 %shard_map.346 = (bf16[512,1920]{1,0:T(8,128)(2,1)}, bf16[512,1920]{1,0:T(8,128)(2,1)}, bf16[512,1920]{1,0:T(8,128)(2,1)}, f32[128,2560]{1,0:T(8,128)}) custom-call(bf16[128,2560]{1,0:T(8,128)(2,1)} %collective-permute-done.25.two_ref.refs_3_, ...), custom_call_target="tpu_custom_call", output_to_operand_aliasing={{0}: (5, {}), {1}: (6, {}), {2}: (7, {})} | custom-call | tf_op jit(solution)/shard_map/pallas_call | solution.py:526
  288.9 4.9 shard_map.347
  293.8 5.0 convolution_convert_fusion.1
  298.8 4.6 convolution_convert_fusion
  318.5 4.8 add_convert_fusion.1
  332.1 5.6 fusion.111
  337.7 10.6 %collective-permute-done.32 = bf16[128,2560]{1,0:T(8,128)(2,1)S(1)} collective-permute-done((bf16[128,2560]{1,0:T(8,128)(2,1)S(1)}, bf16[128,2560]{1,0:T(8,128)(2,1)S(1)}, u32[]{:S(2)}, u32[]{:S(2)}) %collective-permute-start.32) | collective-permute-done | bytes 655392 | tf_op jit(solution)/shard_map/ppermute | solution.py:22
  349.2 3.4 add_convert_fusion.5
  354.6 11.3 %collective-permute-done.33 = bf16[128,2560]{1,0:T(8,128)(2,1)S(1)} collective-permute-done((bf16[128,2560]{1,0:T(8,128)(2,1)S(1)}, bf16[128,2560]{1,0:T(8,128)(2,1)S(1)}, u32[]{:S(2)}, u32[]{:S(2)}) %collective-permute-start.33) | collective-permute-done | bytes 655392 | tf_op jit(solution)/shard_map/ppermute | solution.py:22
  369.6 6.6 %shard_map.348 = (bf16[4,128,640]{2,1,0:T(8,128)(2,1)}, f32[4,128,640]{2,1,0:T(8,128)}, f32[4,128,640]{2,1,0:T(8,128)}, f32[4,2,640]{2,1,0:T(2,128)}) custom-call(s32[28]{0:T(128)} %concatenate.53.off_ref, f32[4,128,640]{2,1,0:T(8,128)} %bitcast.154, f32[4,128,640]{2,1,0:T(8,128)} %get-tuple-element.216.by_ref, f32[4,128,640]{2,1,0:T(8,128)} %get-tuple-element.393.st_ref, ...), custom_call_target="tpu_custom_call" | custom-call | tf_op jit(solution)/shard_map/pallas_call | solution.py:569
  378.6 6.9 %collective-permute-done.38 = bf16[640,1920]{1,0:T(8,128)(2,1)} collective-permute-done((bf16[640,1920]{1,0:T(8,128)(2,1)}, bf16[640,1920]{1,0:T(8,128)(2,1)}, u32[]{:S(2)}, u32[]{:S(2)}) %collective-permute-start.38) | collective-permute-done | bytes 2457632 | tf_op jit(solution)/shard_map/ppermute | solution.py:55
  387.7 4.3 add_convert_fusion.4
  393.8 3.7 add_convert_fusion.3
  399.7 9.5 %shard_map.349 = (f32[4,128,640]{2,1,0:T(8,128)}, bf16[4,128,128]{2,1,0:T(8,128)(2,1)}, f32[2560,128]{1,0:T(8,128)}, f32[8,640]{1,0:T(8,128)}) custom-call(s32[28]{0:T(128)} %concatenate.53.off_ref, f32[4,128,640]{2,1,0:T(8,128)} %get-tuple-element.301.c_ref, f32[4,128,640]{2,1,0:T(8,128)} %get-tuple-element.302.a_ref, ...), custom_call_target="tpu_custom_call" | custom-call | tf_op jit(solution)/shard_map/pallas_call | solution.py:569
  409.3 4.1 shard_map.350
  418.8 6.4 %collective-permute-done.43 = bf16[320,1920]{1,0:T(8,128)(2,1)} collective-permute-done((bf16[320,1920]{1,0:T(8,128)(2,1)}, bf16[320,1920]{1,0:T(8,128)(2,1)}, u32[]{:S(2)}, u32[]{:S(2)}) %collective-permute-start.43) | collective-permute-done | bytes 1228832 | tf_op jit(solution)/shard_map/ppermute | solution.py:55
  426.1 4.5 fusion.113
  439.8 5.2 shard_map.351
  448.7 5.9 %convolution_add_fusion.part_ref = f32[512,2560]{1,0:T(8,128)S(1)} fusion(f32[512,2560]{1,0:T(8,128)} %fusion.113, bf16[512,640]{1,0:T(8,128)(2,1)} %bitcast.143, bf16[640,2560]{1,0:T(8,128)(2,1)} %wx_ref.7), kind=kOutput, calls=%fused_computation.4 | convolution fusion | flops 1679032320 | bytes 14417920 | tf_op jit(solution)/shard_map/dot_general | solution.py:591
  457.8 5.1 shard_map.352
  466.6 9.0 %collective-permute-done.48 = bf16[128,2560]{1,0:T(8,128)(2,1)} collective-permute-done((bf16[128,2560]{1,0:T(8,128)(2,1)}, bf16[128,2560]{1,0:T(8,128)(2,1)}, u32[]{:S(2)}, u32[]{:S(2)}) %collective-permute-start.48) | collective-permute-done | bytes 655392 | tf_op jit(solution)/shard_map/ppermute | solution.py:22
  483.7 9.0 %collective-permute-done.52 = f32[2,2560]{1,0:T(2,128)S(1)} collective-permute-done((f32[2,2560]{1,0:T(2,128)S(1)}, f32[2,2560]{1,0:T(2,128)S(1)}, u32[]{:S(2)}, u32[]{:S(2)}) %collective-permute-start.52) | collective-permute-done | bytes 20512 | tf_op jit(solution)/shard_map/ppermute | solution.py:55
  492.6 3.8 collective-permute-done.51
  501.5 3.9 add_bitcast_fusion.1
  506.2 9.0 %collective-permute-done.55 = f32[2,2560]{1,0:T(2,128)S(1)} collective-permute-done((f32[2,2560]{1,0:T(2,128)S(1)}, f32[2,2560]{1,0:T(2,128)S(1)}, u32[]{:S(2)}, u32[]{:S(2)}) %collective-permute-start.55) | collective-permute-done | bytes 20512 | tf_op jit(solution)/shard_map/ppermute | solution.py:55
  546.7 3.9 add_bitcast_fusion
  561.9 5.2 collective-permute-done.73
  (422 shorter events, 217.3 us)
Async XLA Ops:
  0.7 20.2 %collective-permute-start = (bf16[128,2560]{1,0:T(8,128)(2,1)}, bf16[128,2560]{1,0:T(8,128)(2,1)}, u32[]{:S(2)}, u32[]{:S(2)}) collective-permute-start(bf16[128,2560]{1,0:T(8,128)(2,1)} %bitcast.135), channel_id=1, source_target_pairs={{0,1},{1,2},{2,3},{3,0},{4,5},{5,6},{6,7},{7,4},{8,9},{9,10},{10,1... | collective-permute-start | bytes 1966088 | tf_op jit(solution)/shard_map/ppermute | solution.py:22
  25.0 17.4 %collective-permute-start.1 = (bf16[128,2560]{1,0:T(8,128)(2,1)}, bf16[128,2560]{1,0:T(8,128)(2,1)}, u32[]{:S(2)}, u32[]{:S(2)}) collective-permute-start(bf16[128,2560]{1,0:T(8,128)(2,1)} %collective-permute-done.x_ref), channel_id=1, source_target_pairs={{0,1},{1,2},{2,3},{3,0},{4,5},{5,6},{6,7},{7,4},{8,9},{9,10},{10,1... | collective-permute-start | bytes 1966088 | tf_op jit(solution)/shard_map/ppermute | solution.py:22
  42.5 18.7 %collective-permute-start.5 = (bf16[128,2560]{1,0:T(8,128)(2,1)}, bf16[128,2560]{1,0:T(8,128)(2,1)}, u32[]{:S(2)}, u32[]{:S(2)}) collective-permute-start(bf16[128,2560]{1,0:T(8,128)(2,1)} %collective-permute-done.1.x_ref), channel_id=1, source_target_pairs={{0,1},{1,2},{2,3},{3,0},{4,5},{5,6},{6,7},{7,4},{8,9},{9,10},{10,1... | collective-permute-start | bytes 1966088 | tf_op jit(solution)/shard_map/ppermute | solution.py:22
  49.7 28.8 %collective-permute-start.7 = (bf16[2,16,640]{2,1,0:T(8,128)(2,1)}, bf16[2,16,640]{2,1,0:T(8,128)(2,1)S(1)}, u32[]{:S(2)}, u32[]{:S(2)}) collective-permute-start(bf16[2,16,640]{2,1,0:T(8,128)(2,1)} %bitcast.127), channel_id=1, source_target_pairs={{0,1},{1,2},{2,3},{3,0},{4,5},{5,6},{6,7},{7,4},{8,9},{9,10},{10,1... | collective-permute-start | bytes 122888 | tf_op jit(solution)/shard_map/ppermute | solution.py:678
  50.0 28.5 %collective-permute-start.8 = (bf16[2,16,640]{2,1,0:T(8,128)(2,1)}, bf16[2,16,640]{2,1,0:T(8,128)(2,1)S(1)}, u32[]{:S(2)}, u32[]{:S(2)}) collective-permute-start(bf16[2,16,640]{2,1,0:T(8,128)(2,1)} %bitcast.126), channel_id=1, source_target_pairs={{0,2},{1,3},{2,0},{3,1},{4,6},{5,7},{6,4},{7,5},{8,10},{9,11},{10,... | collective-permute-start | bytes 122888 | tf_op jit(solution)/shard_map/ppermute | solution.py:678
  53.1 25.5 %collective-permute-start.9 = (bf16[2,16,640]{2,1,0:T(8,128)(2,1)}, bf16[2,16,640]{2,1,0:T(8,128)(2,1)S(1)}, u32[]{:S(2)}, u32[]{:S(2)}) collective-permute-start(bf16[2,16,640]{2,1,0:T(8,128)(2,1)} %bitcast.125), channel_id=1, source_target_pairs={{0,3},{1,0},{2,1},{3,2},{4,7},{5,4},{6,5},{7,6},{8,11},{9,8},{10,9... | collective-permute-start | bytes 122888 | tf_op jit(solution)/shard_map/ppermute | solution.py:678
  72.5 24.1 %collective-permute-start.11 = (bf16[128,2560]{1,0:T(8,128)(2,1)}, bf16[128,2560]{1,0:T(8,128)(2,1)}, u32[]{:S(2)}, u32[]{:S(2)}) collective-permute-start(bf16[128,2560]{1,0:T(8,128)(2,1)} %bitcast.138), channel_id=1, source_target_pairs={{0,1},{1,2},{2,3},{3,0},{4,5},{5,6},{6,7},{7,4},{8,9},{9,10},{10,1... | collective-permute-start | bytes 1966088 | tf_op jit(solution)/shard_map/ppermute | solution.py:22
  96.5 18.2 %collective-permute-start.16 = (bf16[128,2560]{1,0:T(8,128)(2,1)}, bf16[128,2560]{1,0:T(8,128)(2,1)}, u32[]{:S(2)}, u32[]{:S(2)}) collective-permute-start(bf16[128,2560]{1,0:T(8,128)(2,1)} %collective-permute-done.11.refs_1_.g_ref), channel_id=1, source_target_pairs={{0,1},{1,2},{2,3},{3,0},{4,5},{5,6},{6,7},{7,4},{8,9},{9,10},{10,1... | collective-permute-start | bytes 1966088 | tf_op jit(solution)/shard_map/ppermute | solution.py:22
  120.2 20.0 %collective-permute-start.20 = (bf16[128,2560]{1,0:T(8,128)(2,1)}, bf16[128,2560]{1,0:T(8,128)(2,1)}, u32[]{:S(2)}, u32[]{:S(2)}) collective-permute-start(bf16[128,2560]{1,0:T(8,128)(2,1)} %collective-permute-done.16.refs_2_.g_ref), channel_id=1, source_target_pairs={{0,1},{1,2},{2,3},{3,0},{4,5},{5,6},{6,7},{7,4},{8,9},{9,10},{10,1... | collective-permute-start | bytes 1966088 | tf_op jit(solution)/shard_map/ppermute | solution.py:22
  131.7 19.2 %collective-permute-start.19 = (bf16[128,2560]{1,0:T(8,128)(2,1)}, bf16[128,2560]{1,0:T(8,128)(2,1)}, u32[]{:S(2)}, u32[]{:S(2)}) collective-permute-start(bf16[128,2560]{1,0:T(8,128)(2,1)} %slice.795), channel_id=1, source_target_pairs={{0,1},{1,2},{2,3},{3,0},{4,5},{5,6},{6,7},{7,4},{8,9},{9,10},{10,1... | collective-permute-start | bytes 1966088 | tf_op jit(solution)/shard_map/ppermute | solution.py:22
  153.3 15.5 %collective-permute-start.21 = (bf16[128,2560]{1,0:T(8,128)(2,1)}, bf16[128,2560]{1,0:T(8,128)(2,1)}, u32[]{:S(2)}, u32[]{:S(2)}) collective-permute-start(bf16[128,2560]{1,0:T(8,128)(2,1)} %fusion.28), channel_id=1, source_target_pairs={{0,1},{1,2},{2,3},{3,0},{4,5},{5,6},{6,7},{7,4},{8,9},{9,10},{10,1... | collective-permute-start | bytes 1966088 | tf_op jit(solution)/shard_map/ppermute | solution.py:22
  171.2 14.6 %collective-permute-start.22 = (bf16[128,2560]{1,0:T(8,128)(2,1)}, bf16[128,2560]{1,0:T(8,128)(2,1)}, u32[]{:S(2)}, u32[]{:S(2)}) collective-permute-start(bf16[128,2560]{1,0:T(8,128)(2,1)} %fusion.29), channel_id=1, source_target_pairs={{0,1},{1,2},{2,3},{3,0},{4,5},{5,6},{6,7},{7,4},{8,9},{9,10},{10,1... | collective-permute-start | bytes 1966088 | tf_op jit(solution)/shard_map/ppermute | solution.py:22
  190.0 20.9 %collective-permute-start.23 = (bf16[128,2560]{1,0:T(8,128)(2,1)}, bf16[128,2560]{1,0:T(8,128)(2,1)}, u32[]{:S(2)}, u32[]{:S(2)}) collective-permute-start(bf16[128,2560]{1,0:T(8,128)(2,1)} %multiply_convert_fusion.two_ref.refs_0_), channel_id=1, source_target_pairs={{0,1},{1,2},{2,3},{3,0},{4,5},{5,6},{6,7},{7,4},{8,9},{9,10},{10,1... | collective-permute-start | bytes 1966088 | tf_op jit(solution)/shard_map/ppermute | solution.py:22
  210.9 20.7 %collective-permute-start.24 = (bf16[128,2560]{1,0:T(8,128)(2,1)}, bf16[128,2560]{1,0:T(8,128)(2,1)}, u32[]{:S(2)}, u32[]{:S(2)}) collective-permute-start(bf16[128,2560]{1,0:T(8,128)(2,1)} %collective-permute-done.23.two_ref.refs_1_), channel_id=1, source_target_pairs={{0,1},{1,2},{2,3},{3,0},{4,5},{5,6},{6,7},{7,4},{8,9},{9,10},{10,1... | collective-permute-start | bytes 1966088 | tf_op jit(solution)/shard_map/ppermute | solution.py:22
  231.6 26.2 %collective-permute-start.26 = (bf16[128,2560]{1,0:T(8,128)(2,1)}, bf16[128,2560]{1,0:T(8,128)(2,1)}, u32[]{:S(2)}, u32[]{:S(2)}) collective-permute-start(bf16[128,2560]{1,0:T(8,128)(2,1)} %get-tuple-element.255), channel_id=1, source_target_pairs={{0,1},{1,2},{2,3},{3,0},{4,5},{5,6},{6,7},{7,4},{8,9},{9,10},{10,1... | collective-permute-start | bytes 1966088 | tf_op jit(solution)/shard_map/ppermute | solution.py:22
  232.3 27.1 %collective-permute-start.25 = (bf16[128,2560]{1,0:T(8,128)(2,1)}, bf16[128,2560]{1,0:T(8,128)(2,1)}, u32[]{:S(2)}, u32[]{:S(2)}) collective-permute-start(bf16[128,2560]{1,0:T(8,128)(2,1)} %collective-permute-done.24.two_ref.refs_2_), channel_id=1, source_target_pairs={{0,1},{1,2},{2,3},{3,0},{4,5},{5,6},{6,7},{7,4},{8,9},{9,10},{10,1... | collective-permute-start | bytes 1966088 | tf_op jit(solution)/shard_map/ppermute | solution.py:22
  261.9 22.1 %collective-permute-start.27 = (bf16[128,2560]{1,0:T(8,128)(2,1)}, bf16[128,2560]{1,0:T(8,128)(2,1)}, u32[]{:S(2)}, u32[]{:S(2)}) collective-permute-start(bf16[128,2560]{1,0:T(8,128)(2,1)} %add_convert_fusion.13), channel_id=1, source_target_pairs={{0,1},{1,2},{2,3},{3,0},{4,5},{5,6},{6,7},{7,4},{8,9},{9,10},{10,1... | collective-permute-start | bytes 1966088 | tf_op jit(solution)/shard_map/ppermute | solution.py:22
  286.4 17.0 %collective-permute-start.28 = (bf16[128,2560]{1,0:T(8,128)(2,1)}, bf16[128,2560]{1,0:T(8,128)(2,1)}, u32[]{:S(2)}, u32[]{:S(2)}) collective-permute-start(bf16[128,2560]{1,0:T(8,128)(2,1)} %add_convert_fusion.12), channel_id=1, source_target_pairs={{0,1},{1,2},{2,3},{3,0},{4,5},{5,6},{6,7},{7,4},{8,9},{9,10},{10,1... | collective-permute-start | bytes 1966088 | tf_op jit(solution)/shard_map/ppermute | solution.py:22
  303.3 15.2 %collective-permute-start.30 = (bf16[1280,1920]{1,0:T(8,128)(2,1)S(1)}, bf16[1280,1920]{1,0:T(8,128)(2,1)S(1)}, u32[]{:S(2)}, u32[]{:S(2)}) collective-permute-start(bf16[1280,1920]{1,0:T(8,128)(2,1)S(1)} %convolution_convert_fusion.1), channel_id=1, source_target_pairs={{0,4},{4,0},{8,12},{12,8},{16,20},{20,16},{24,28},{28,24},{1,5},{5... | collective-permute-start | bytes 14745608 | tf_op jit(solution)/shard_map/ppermute | solution.py:55
  303.3 20.0 %collective-permute-start.31 = (bf16[1280,1920]{1,0:T(8,128)(2,1)}, bf16[1280,1920]{1,0:T(8,128)(2,1)S(1)}, u32[]{:S(2)}, u32[]{:S(2)}) collective-permute-start(bf16[1280,1920]{1,0:T(8,128)(2,1)} %convolution_convert_fusion), channel_id=1, source_target_pairs={{0,4},{4,0},{8,12},{12,8},{16,20},{20,16},{24,28},{28,24},{1,5},{5... | collective-permute-start | bytes 14745608 | tf_op jit(solution)/shard_map/ppermute | solution.py:55
  310.7 18.6 %collective-permute-start.29 = (bf16[128,2560]{1,0:T(8,128)(2,1)S(1)}, bf16[128,2560]{1,0:T(8,128)(2,1)S(1)}, u32[]{:S(2)}, u32[]{:S(2)}) collective-permute-start(bf16[128,2560]{1,0:T(8,128)(2,1)S(1)} %get-tuple-element.388), channel_id=1, source_target_pairs={{0,1},{1,2},{2,3},{3,0},{4,5},{5,6},{6,7},{7,4},{8,9},{9,10},{10,1... | collective-permute-start | bytes 1966088 | tf_op jit(solution)/shard_map/ppermute | solution.py:22
  329.3 23.3 %collective-permute-start.35 = (bf16[1280,1024]{1,0:T(8,128)(2,1)}, bf16[1280,1024]{1,0:T(8,128)(2,1)S(1)}, u32[]{:S(2)}, u32[]{:S(2)}) collective-permute-start(bf16[1280,1024]{1,0:T(8,128)(2,1)} %convolution_convert_fusion.2), channel_id=1, source_target_pairs={{0,4},{4,0},{8,12},{12,8},{16,20},{20,16},{24,28},{28,24},{1,5},{5... | collective-permute-start | bytes 7864328 | tf_op jit(solution)/shard_map/ppermute | solution.py:55
  329.3 19.9 %collective-permute-start.34 = (bf16[1280,896]{1,0:T(8,128)(2,1)}, bf16[1280,896]{1,0:T(8,128)(2,1)S(1)}, u32[]{:S(2)}, u32[]{:S(2)}) collective-permute-start(bf16[1280,896]{1,0:T(8,128)(2,1)} %convolution_convert_fusion.3), channel_id=1, source_target_pairs={{0,4},{4,0},{8,12},{12,8},{16,20},{20,16},{24,28},{28,24},{1,5},{5... | collective-permute-start | bytes 6881288 | tf_op jit(solution)/shard_map/ppermute | solution.py:55
  329.8 18.4 %collective-permute-start.32 = (bf16[128,2560]{1,0:T(8,128)(2,1)S(1)}, bf16[128,2560]{1,0:T(8,128)(2,1)S(1)}, u32[]{:S(2)}, u32[]{:S(2)}) collective-permute-start(bf16[128,2560]{1,0:T(8,128)(2,1)S(1)} %collective-permute-done.29), channel_id=1, source_target_pairs={{0,1},{1,2},{2,3},{3,0},{4,5},{5,6},{6,7},{7,4},{8,9},{9,10},{10,1... | collective-permute-start | bytes 1966088 | tf_op jit(solution)/shard_map/ppermute | solution.py:22
  329.8 55.6 %collective-permute-start.38 = (bf16[640,1920]{1,0:T(8,128)(2,1)}, bf16[640,1920]{1,0:T(8,128)(2,1)}, u32[]{:S(2)}, u32[]{:S(2)}) collective-permute-start(bf16[640,1920]{1,0:T(8,128)(2,1)} %add_convert_fusion.1), channel_id=1, source_target_pairs={{0,8},{4,12},{8,0},{12,4},{16,24},{20,28},{24,16},{28,20},{1,9},{5... | collective-permute-start | bytes 7372808 | tf_op jit(solution)/shard_map/ppermute | solution.py:55
  331.4 55.3 %collective-permute-start.39 = (bf16[640,1920]{1,0:T(8,128)(2,1)}, bf16[640,1920]{1,0:T(8,128)(2,1)}, u32[]{:S(2)}, u32[]{:S(2)}) collective-permute-start(bf16[640,1920]{1,0:T(8,128)(2,1)} %add_convert_fusion), channel_id=1, source_target_pairs={{0,16},{4,20},{8,24},{12,28},{16,0},{20,4},{24,8},{28,12},{1,17},{... | collective-permute-start | bytes 7372808 | tf_op jit(solution)/shard_map/ppermute | solution.py:55
  348.3 17.6 %collective-permute-start.33 = (bf16[128,2560]{1,0:T(8,128)(2,1)S(1)}, bf16[128,2560]{1,0:T(8,128)(2,1)S(1)}, u32[]{:S(2)}, u32[]{:S(2)}) collective-permute-start(bf16[128,2560]{1,0:T(8,128)(2,1)S(1)} %collective-permute-done.32), channel_id=1, source_target_pairs={{0,1},{1,2},{2,3},{3,0},{4,5},{5,6},{6,7},{7,4},{8,9},{9,10},{10,1... | collective-permute-start | bytes 1966088 | tf_op jit(solution)/shard_map/ppermute | solution.py:22
  365.8 20.9 %collective-permute-start.37 = (bf16[128,2560]{1,0:T(8,128)(2,1)}, bf16[128,2560]{1,0:T(8,128)(2,1)}, u32[]{:S(2)}, u32[]{:S(2)}) collective-permute-start(bf16[128,2560]{1,0:T(8,128)(2,1)} %slice.454), channel_id=1, source_target_pairs={{0,1},{1,2},{2,3},{3,0},{4,5},{5,6},{6,7},{7,4},{8,9},{9,10},{10,1... | collective-permute-start | bytes 1966088 | tf_op jit(solution)/shard_map/ppermute | solution.py:22
  397.6 27.6 %collective-permute-start.43 = (bf16[320,1920]{1,0:T(8,128)(2,1)}, bf16[320,1920]{1,0:T(8,128)(2,1)}, u32[]{:S(2)}, u32[]{:S(2)}) collective-permute-start(bf16[320,1920]{1,0:T(8,128)(2,1)} %add_convert_fusion.4), channel_id=1, source_target_pairs={{0,16},{4,20},{8,24},{12,28},{16,0},{20,4},{24,8},{28,12},{1,17},{... | collective-permute-start | bytes 3686408 | tf_op jit(solution)/shard_map/ppermute | solution.py:55
  398.0 27.6 %collective-permute-start.44 = (bf16[320,1920]{1,0:T(8,128)(2,1)}, bf16[320,1920]{1,0:T(8,128)(2,1)}, u32[]{:S(2)}, u32[]{:S(2)}) collective-permute-start(bf16[320,1920]{1,0:T(8,128)(2,1)} %add_convert_fusion.3), channel_id=1, source_target_pairs={{0,8},{4,12},{8,0},{12,4},{16,24},{20,28},{24,16},{28,20},{1,9},{5... | collective-permute-start | bytes 3686408 | tf_op jit(solution)/shard_map/ppermute | solution.py:55
  445.0 30.6 %collective-permute-start.50 = (bf16[640,640]{1,0:T(8,128)(2,1)}, bf16[640,640]{1,0:T(8,128)(2,1)}, u32[]{:S(2)}, u32[]{:S(2)}) collective-permute-start(bf16[640,640]{1,0:T(8,128)(2,1)} %add_convert_fusion.7), channel_id=1, source_target_pairs={{0,8},{4,12},{8,0},{12,4},{16,24},{20,28},{24,16},{28,20},{1,9},{5... | collective-permute-start | bytes 2457608 | tf_op jit(solution)/shard_map/ppermute | solution.py:55
  447.2 28.3 %collective-permute-start.49 = (bf16[640,768]{1,0:T(8,128)(2,1)}, bf16[640,768]{1,0:T(8,128)(2,1)}, u32[]{:S(2)}, u32[]{:S(2)}) collective-permute-start(bf16[640,768]{1,0:T(8,128)(2,1)} %pad_maximum_fusion.4), channel_id=1, source_target_pairs={{0,16},{4,20},{8,24},{12,28},{16,0},{20,4},{24,8},{28,12},{1,17},{... | collective-permute-start | bytes 2949128 | tf_op jit(solution)/shard_map/ppermute | solution.py:55
  457.8 17.8 %collective-permute-start.48 = (bf16[128,2560]{1,0:T(8,128)(2,1)}, bf16[128,2560]{1,0:T(8,128)(2,1)}, u32[]{:S(2)}, u32[]{:S(2)}) collective-permute-start(bf16[128,2560]{1,0:T(8,128)(2,1)} %slice.794), channel_id=1, source_target_pairs={{0,1},{1,2},{2,3},{3,0},{4,5},{5,6},{6,7},{7,4},{8,9},{9,10},{10,1... | collective-permute-start | bytes 1966088 | tf_op jit(solution)/shard_map/ppermute | solution.py:22
  463.0 37.1 %collective-permute-start.58 = (bf16[640,896]{1,0:T(8,128)(2,1)}, bf16[640,896]{1,0:T(8,128)(2,1)S(1)}, u32[]{:S(2)}, u32[]{:S(2)}) collective-permute-start(bf16[640,896]{1,0:T(8,128)(2,1)} %add_convert_fusion.5), channel_id=1, source_target_pairs={{0,8},{4,12},{8,0},{12,4},{16,24},{20,28},{24,16},{28,20},{1,9},{5... | collective-permute-start | bytes 3440648 | tf_op jit(solution)/shard_map/ppermute | solution.py:55
  463.7 41.7 %collective-permute-start.59 = (bf16[640,1024]{1,0:T(8,128)(2,1)}, bf16[640,1024]{1,0:T(8,128)(2,1)S(1)}, u32[]{:S(2)}, u32[]{:S(2)}) collective-permute-start(bf16[640,1024]{1,0:T(8,128)(2,1)} %add_convert_fusion.2), channel_id=1, source_target_pairs={{0,16},{4,20},{8,24},{12,28},{16,0},{20,4},{24,8},{28,12},{1,17},{... | collective-permute-start | bytes 3932168 | tf_op jit(solution)/shard_map/ppermute | solution.py:55
  477.2 19.2 %collective-permute-start.51 = (bf16[128,2560]{1,0:T(8,128)(2,1)S(1)}, bf16[128,2560]{1,0:T(8,128)(2,1)S(1)}, u32[]{:S(2)}, u32[]{:S(2)}) collective-permute-start(bf16[128,2560]{1,0:T(8,128)(2,1)S(1)} %fusion.25), channel_id=1, source_target_pairs={{0,1},{1,2},{2,3},{3,0},{4,5},{5,6},{6,7},{7,4},{8,9},{9,10},{10,1... | collective-permute-start | bytes 1966088 | tf_op jit(solution)/shard_map/ppermute | solution.py:22
  477.3 15.3 %collective-permute-start.52 = (f32[2,2560]{1,0:T(2,128)S(1)}, f32[2,2560]{1,0:T(2,128)S(1)}, u32[]{:S(2)}, u32[]{:S(2)}) collective-permute-start(f32[2,2560]{1,0:T(2,128)S(1)} %pad_maximum_fusion.19), channel_id=1, source_target_pairs={{0,1},{1,0},{2,3},{3,2},{4,5},{5,4},{6,7},{7,6},{8,9},{9,8},{10,11... | collective-permute-start | bytes 61448 | tf_op jit(solution)/shard_map/ppermute | solution.py:55
  496.6 18.7 %collective-permute-start.54 = (bf16[128,2560]{1,0:T(8,128)(2,1)S(1)}, bf16[128,2560]{1,0:T(8,128)(2,1)S(1)}, u32[]{:S(2)}, u32[]{:S(2)}) collective-permute-start(bf16[128,2560]{1,0:T(8,128)(2,1)S(1)} %fusion.26), channel_id=1, source_target_pairs={{0,1},{1,2},{2,3},{3,0},{4,5},{5,6},{6,7},{7,4},{8,9},{9,10},{10,1... | collective-permute-start | bytes 1966088 | tf_op jit(solution)/shard_map/ppermute | solution.py:22
  496.6 18.6 %collective-permute-start.55 = (f32[2,2560]{1,0:T(2,128)S(1)}, f32[2,2560]{1,0:T(2,128)S(1)}, u32[]{:S(2)}, u32[]{:S(2)}) collective-permute-start(f32[2,2560]{1,0:T(2,128)S(1)} %fusion.107), channel_id=1, source_target_pairs={{0,2},{1,3},{2,0},{3,1},{4,6},{5,7},{6,4},{7,5},{8,10},{9,11},{10,... | collective-permute-start | bytes 61448 | tf_op jit(solution)/shard_map/ppermute | solution.py:55
  497.5 17.7 %collective-permute-start.57 = (bf16[320,640]{1,0:T(8,128)(2,1)S(1)}, bf16[320,640]{1,0:T(8,128)(2,1)S(1)}, u32[]{:S(2)}, u32[]{:S(2)}) collective-permute-start(bf16[320,640]{1,0:T(8,128)(2,1)S(1)} %add_convert_fusion.14), channel_id=1, source_target_pairs={{0,16},{4,20},{8,24},{12,28},{16,0},{20,4},{24,8},{28,12},{1,17},{... | collective-permute-start | bytes 1228808 | tf_op jit(solution)/shard_map/ppermute | solution.py:55
  500.1 15.1 %collective-permute-start.56 = (bf16[320,768]{1,0:T(8,128)(2,1)S(1)}, bf16[320,768]{1,0:T(8,128)(2,1)S(1)}, u32[]{:S(2)}, u32[]{:S(2)}) collective-permute-start(bf16[320,768]{1,0:T(8,128)(2,1)S(1)} %pad_maximum_fusion.6), channel_id=1, source_target_pairs={{0,8},{4,12},{8,0},{12,4},{16,24},{20,28},{24,16},{28,20},{1,9},{5... | collective-permute-start | bytes 1474568 | tf_op jit(solution)/shard_map/ppermute | solution.py:55
  505.4 24.6 %collective-permute-start.62 = (bf16[640,640]{1,0:T(8,128)(2,1)S(1)}, bf16[640,640]{1,0:T(8,128)(2,1)S(1)}, u32[]{:S(2)}, u32[]{:S(2)}) collective-permute-start(bf16[640,640]{1,0:T(8,128)(2,1)S(1)} %add_convert_fusion.6), channel_id=1, source_target_pairs={{0,8},{4,12},{8,0},{12,4},{16,24},{20,28},{24,16},{28,20},{1,9},{5... | collective-permute-start | bytes 2457608 | tf_op jit(solution)/shard_map/ppermute | solution.py:55
  516.5 16.7 %collective-permute-start.60 = (bf16[128,2560]{1,0:T(8,128)(2,1)S(1)}, bf16[128,2560]{1,0:T(8,128)(2,1)S(1)}, u32[]{:S(2)}, u32[]{:S(2)}) collective-permute-start(bf16[128,2560]{1,0:T(8,128)(2,1)S(1)} %add_convert_fusion.11), channel_id=1, source_target_pairs={{0,1},{1,2},{2,3},{3,0},{4,5},{5,6},{6,7},{7,4},{8,9},{9,10},{10,1... | collective-permute-start | bytes 1966088 | tf_op jit(solution)/shard_map/ppermute | solution.py:22
  533.3 19.5 %collective-permute-start.70 = (f32[10,640]{1,0:T(8,128)S(1)}, f32[10,640]{1,0:T(8,128)S(1)}, u32[]{:S(2)}, u32[]{:S(2)}) collective-permute-start(f32[10,640]{1,0:T(8,128)S(1)} %fusion.106), channel_id=1, source_target_pairs={{0,8},{4,12},{8,0},{12,4},{16,24},{20,28},{24,16},{28,20},{1,9},{5... | collective-permute-start | bytes 76808 | tf_op jit(solution)/shard_map/ppermute | solution.py:55
  536.6 33.0 %collective-permute-start.68 = (bf16[320,896]{1,0:T(8,128)(2,1)S(1)}, bf16[320,896]{1,0:T(8,128)(2,1)S(1)}, u32[]{:S(2)}, u32[]{:S(2)}) collective-permute-start(bf16[320,896]{1,0:T(8,128)(2,1)S(1)} %fusion.11), channel_id=1, source_target_pairs={{0,16},{4,20},{8,24},{12,28},{16,0},{20,4},{24,8},{28,12},{1,17},{... | collective-permute-start | bytes 1720328 | tf_op jit(solution)/shard_map/ppermute | solution.py:55
  537.4 37.9 %collective-permute-start.69 = (bf16[320,1024]{1,0:T(8,128)(2,1)}, bf16[320,1024]{1,0:T(8,128)(2,1)}, u32[]{:S(2)}, u32[]{:S(2)}) collective-permute-start(bf16[320,1024]{1,0:T(8,128)(2,1)} %fusion.10), channel_id=1, source_target_pairs={{0,8},{4,12},{8,0},{12,4},{16,24},{20,28},{24,16},{28,20},{1,9},{5... | collective-permute-start | bytes 1966088 | tf_op jit(solution)/shard_map/ppermute | solution.py:55
  542.4 37.1 %collective-permute-start.66 = (bf16[128,2560]{1,0:T(8,128)(2,1)}, bf16[128,2560]{1,0:T(8,128)(2,1)}, u32[]{:S(2)}, u32[]{:S(2)}) collective-permute-start(bf16[128,2560]{1,0:T(8,128)(2,1)} %add_convert_fusion.10), channel_id=1, source_target_pairs={{0,1},{1,2},{2,3},{3,0},{4,5},{5,6},{6,7},{7,4},{8,9},{9,10},{10,1... | collective-permute-start | bytes 1966088 | tf_op jit(solution)/shard_map/ppermute | solution.py:22
  545.9 14.5 %collective-permute-start.72 = (bf16[1,4,80,128]{3,2,1,0:T(8,128)(2,1)S(1)}, bf16[1,4,80,128]{3,2,1,0:T(8,128)(2,1)S(1)}, u32[]{:S(2)}, u32[]{:S(2)}) collective-permute-start(bf16[1,4,80,128]{3,2,1,0:T(8,128)(2,1)S(1)} %dynamic-slice_bitcast_fusion.1), channel_id=1, source_target_pairs={{0,8},{4,12},{8,0},{12,4},{16,24},{20,28},{24,16},{28,20},{1,9},{5... | collective-permute-start | bytes 245768 | tf_op jit(solution)/shard_map/ppermute | solution.py:55
  (95 other events, 889.9 us)
